TPU v7x, 32 devices: a whole 2x2x4 slice. The times are simulated.
32 devices in a mesh: dp: 8 (over z, x), tensor: 4 (over y, core).
Axes of the slice: x: 2, y: 2, z: 4, core: 2. Of those that a mesh axis runs over, the one named last changes fastest.
Arguments:
- layer_input: bfloat16 [8192, 2048], P(('dp', 'tensor')), may hold values from -6 to 6
- segments: int32 [8192], P('dp'), may hold values from 0 to 8191, as said below
- positions: int32 [8192], P('dp'), may hold values from 0 to 1023, as said below
- first_gain: bfloat16 [2048], P('dp'), may hold values from 0.5 to 1.5
- first_shift: bfloat16 [2048], P('dp'), may hold values from -4 to 4
- query_weight: bfloat16 [2048, 2048], P('dp', 'tensor'), may hold values from -0.125 to 0.125
- key_weight: bfloat16 [2048, 2048], P('dp', 'tensor'), may hold values from -0.125 to 0.125
- value_weight: bfloat16 [2048, 2048], P('dp', 'tensor'), may hold values from -0.125 to 0.125
- query_bias: bfloat16 [32, 64], P('tensor', 'dp'), may hold values from -6 to 6
- key_bias: bfloat16 [32, 16], P('tensor'), may hold values from -6 to 6
- value_bias: bfloat16 [32, 64], P('tensor', 'dp'), may hold values from -6 to 6
- out_weight: bfloat16 [2048, 2048], P('tensor', 'dp'), may hold values from -0.5 to 0.5
- second_gain: bfloat16 [2048], P('dp'), may hold values from 0.5 to 1.5
- second_shift: bfloat16 [2048], P('dp'), may hold values from -4 to 4
- gate_weight: bfloat16 [2048, 5632], P('dp', 'tensor'), may hold values from -0.125 to 0.125
- up_weight: bfloat16 [2048, 5632], P('dp', 'tensor'), may hold values from -0.125 to 0.125
- down_weight: bfloat16 [5632, 2048], P('tensor', 'dp'), may hold values from -0.078125 to 0.078125
- out_grad: bfloat16 [8192, 2048], P(('dp', 'tensor')), may hold values from -6 to 6
Outputs:
- layer_output: bfloat16 [8192, 2048], P(('dp', 'tensor'))
- input_grad: float32 [8192, 2048], P(('dp', 'tensor'))
- first_gain_grad: float32 [2048], P(('dp', 'tensor'))
- first_shift_grad: float32 [2048], P(('dp', 'tensor'))
- query_weight_grad: float32 [2048, 2048], P('dp', 'tensor')
- key_weight_grad: float32 [2048, 2048], P('dp', 'tensor')
- value_weight_grad: float32 [2048, 2048], P('dp', 'tensor')
- query_bias_grad: float32 [32, 64], P('tensor', 'dp')
- key_bias_grad: float32 [32, 16], P('tensor')
- value_bias_grad: float32 [32, 64], P('tensor', 'dp')
- out_weight_grad: float32 [2048, 2048], P('tensor', 'dp')
- second_gain_grad: float32 [2048], P(('dp', 'tensor'))
- second_shift_grad: float32 [2048], P(('dp', 'tensor'))
- gate_weight_grad: float32 [2048, 5632], P('dp', 'tensor')
- up_weight_grad: float32 [2048, 5632], P('dp', 'tensor')
- down_weight_grad: float32 [5632, 2048], P('tensor', 'dp')
Inputs may be any that keep to these rules, and one draw needn't show every extreme that they name: `segments`: the tokens form runs of 1024 rows that start at multiples of 1024; the first token of each run starts a new segment. A token's segment number is the row index of the last token of its segment, so numbers never fall along the rows and no two runs share one. `positions`: each token's position counts the earlier tokens of its segment.
All inputs are finite; a program needn't handle non-finite values.
Results may differ from a plain program's by a relative error of at most 0.015.
Values may be sent and summed in bfloat16 or wider, within the bound.
A program may use at most 256 MiB of HBM per device.

v0:
```python
import math

import jax
import jax.numpy as jnp
from jax import lax
from jax.sharding import PartitionSpec as P

HD = 64
ROT = 16
SEQ = 1024


EPS = 1e-05
NEG = -1e30


def rope_angles(positions):
    half = ROT // 2
    freqs = jnp.exp(-(2.0 / ROT) * jnp.arange(half).astype(jnp.float32) * math.log(10000.0))
    return positions.astype(jnp.float32)[:, None] * freqs[None, :]


def turn(heads, cosine, sine, direction):
    half = ROT // 2
    first = heads[..., :half]
    second = heads[..., half:ROT]
    return jnp.concatenate(
        [
            first * cosine - direction * second * sine,
            second * cosine + direction * first * sine,
            heads[..., ROT:],
        ],
        axis=-1,
    )


def norm_forward(rows, gain, shift):
    center = rows - jnp.mean(rows, axis=-1, keepdims=True)
    rstd = lax.rsqrt(jnp.mean(center * center, axis=-1, keepdims=True) + EPS)
    normal = center * rstd
    return (normal, rstd, normal * gain + shift)


def norm_backward(grad_out, normal, rstd, gain):
    scaled = grad_out * gain
    return rstd * (
        scaled
        - jnp.mean(scaled, axis=-1, keepdims=True)
        - normal * jnp.mean(scaled * normal, axis=-1, keepdims=True)
    )


def allowed_pairs(segments, start, base, block):
    q_index = start + jnp.arange(block, dtype=jnp.int32)
    k_index = base + jnp.arange(SEQ, dtype=jnp.int32)
    q_segs = lax.dynamic_slice_in_dim(segments, start, block, 0)
    return (k_index[None, :] <= q_index[:, None]) & (segments[None, :] == q_segs[:, None])


def block_scores(q_rot, k_rot, segments, number, block):
    start = number * block
    base = start // SEQ * SEQ
    q_part = lax.dynamic_slice_in_dim(q_rot, start, block, 0)
    raw = jnp.einsum("qhd,khd->hqk", q_part, k_rot, preferred_element_type=jnp.float32)
    allowed = allowed_pairs(segments, start, base, block)
    scores = jnp.where(allowed[None], raw * HD ** (-0.5), NEG)
    return (scores, start, base, q_part, k_rot)


def attend_forward(q_rot, k_rot, v_heads, segments):
    block = min(512, SEQ)
    count = q_rot.shape[0] // block

    def one_block(number):
        scores, start, base, q_part, k_part = block_scores(q_rot, k_rot, segments, number, block)
        top = jnp.max(scores, axis=-1, keepdims=True)
        expo = jnp.exp(scores - top)
        total = jnp.sum(expo, axis=-1, keepdims=True)
        probs = (expo / total).astype(jnp.bfloat16)
        mixed = jnp.einsum("hqk,khd->qhd", probs, v_heads, preferred_element_type=jnp.float32)
        return (mixed, (top + jnp.log(total))[..., 0])

    mixed, log_sums = lax.map(one_block, jnp.arange(count, dtype=jnp.int32))
    return (mixed.reshape(q_rot.shape), log_sums)


def attend_backward(q_rot, k_rot, v_heads, segments, log_sums, grad_mixed):
    block = min(512, SEQ)
    count = q_rot.shape[0] // block
    start_acc = (jnp.zeros(k_rot.shape, jnp.float32), jnp.zeros(v_heads.shape, jnp.float32))

    def one_block(carry, item):
        key_acc, value_acc = carry
        number, log_part = item
        scores, start, base, q_part, k_part = block_scores(q_rot, k_rot, segments, number, block)
        grad_part = lax.dynamic_slice_in_dim(grad_mixed, start, block, 0)
        probs = jnp.exp(scores - log_part[..., None])
        grad_probs = jnp.einsum(
            "qhd,khd->hqk", grad_part, v_heads, preferred_element_type=jnp.float32
        )
        inner = jnp.sum(probs * grad_probs, axis=-1, keepdims=True)
        grad_scores = (probs * (grad_probs - inner) * HD ** (-0.5)).astype(jnp.bfloat16)
        q_grad = jnp.einsum("hqk,khd->qhd", grad_scores, k_part, preferred_element_type=jnp.float32)
        k_grad = jnp.einsum("hqk,qhd->khd", grad_scores, q_part, preferred_element_type=jnp.float32)
        v_grad = jnp.einsum(
            "hqk,qhd->khd",
            probs.astype(jnp.bfloat16),
            grad_part,
            preferred_element_type=jnp.float32,
        )
        key_acc = key_acc + k_grad
        value_acc = value_acc + v_grad
        return ((key_acc, value_acc), q_grad)

    (key_acc, value_acc), q_blocks = lax.scan(
        one_block, start_acc, (jnp.arange(count, dtype=jnp.int32), log_sums)
    )
    return (q_blocks.reshape(q_rot.shape), key_acc, value_acc)


def local(
    layer_input,
    segments,
    positions,
    first_gain,
    first_shift,
    query_weight,
    key_weight,
    value_weight,
    query_bias,
    key_bias,
    value_bias,
    out_weight,
    second_gain,
    second_shift,
    gate_weight,
    up_weight,
    down_weight,
    out_grad,
):
    f32 = jnp.float32
    bf16 = jnp.bfloat16
    query_full, key_full, value_full, out_full, bias_query, bias_value, gain_one, shift_one = (
        lax.all_gather(query_weight, "dp", axis=0, tiled=True),
        lax.all_gather(key_weight, "dp", axis=0, tiled=True),
        lax.all_gather(value_weight, "dp", axis=0, tiled=True),
        lax.all_gather(out_weight, "dp", axis=1, tiled=True),
        lax.all_gather(query_bias, "dp", axis=1, tiled=True),
        lax.all_gather(value_bias, "dp", axis=1, tiled=True),
        lax.all_gather(first_gain, "dp", axis=0, tiled=True),
        lax.all_gather(first_shift, "dp", axis=0, tiled=True),
    )
    gate_full, up_full, down_full, gain_two, shift_two = (
        lax.all_gather(gate_weight, "dp", axis=0, tiled=True),
        lax.all_gather(up_weight, "dp", axis=0, tiled=True),
        lax.all_gather(down_weight, "dp", axis=1, tiled=True),
        lax.all_gather(second_gain, "dp", axis=0, tiled=True),
        lax.all_gather(second_shift, "dp", axis=0, tiled=True),
    )
    rows = layer_input.astype(f32)
    gain_one_f = gain_one.astype(f32)
    hat_one, rstd_one, normed_one = norm_forward(rows, gain_one_f, shift_one.astype(f32))
    norm_one_full = lax.all_gather(normed_one.astype(bf16), "tensor", axis=0, tiled=True)
    total_rows = norm_one_full.shape[0]
    local_heads = query_full.shape[1] // HD
    bias_key_full = jnp.pad(key_bias.astype(f32), ((0, 0), (0, HD - ROT))).reshape(-1)
    q_lin = jnp.dot(norm_one_full, query_full, preferred_element_type=f32) + bias_query.astype(
        f32
    ).reshape(-1)
    k_lin = jnp.dot(norm_one_full, key_full, preferred_element_type=f32) + bias_key_full
    v_lin = jnp.dot(norm_one_full, value_full, preferred_element_type=f32) + bias_value.astype(
        f32
    ).reshape(-1)
    angles = rope_angles(positions)
    cosine = jnp.cos(angles)[:, None, :]
    sine = jnp.sin(angles)[:, None, :]
    q_rot = turn(q_lin.reshape(total_rows, local_heads, HD), cosine, sine, 1.0).astype(bf16)
    k_rot = turn(k_lin.reshape(total_rows, local_heads, HD), cosine, sine, 1.0).astype(bf16)
    v_heads = v_lin.reshape(total_rows, local_heads, HD).astype(bf16)
    mixed, log_sums = attend_forward(q_rot, k_rot, v_heads, segments)
    mixed_low = mixed.reshape(total_rows, -1).astype(bf16)
    attended = rows + lax.psum_scatter(
        jnp.dot(mixed_low, out_full, preferred_element_type=f32),
        "tensor",
        scatter_dimension=0,
        tiled=True,
    )
    gain_two_f = gain_two.astype(f32)
    hat_two, rstd_two, normed_two = norm_forward(attended, gain_two_f, shift_two.astype(f32))
    norm_two_full = lax.all_gather(normed_two.astype(bf16), "tensor", axis=0, tiled=True)
    gate_lin = jnp.dot(norm_two_full, gate_full, preferred_element_type=f32)
    up_lin = jnp.dot(norm_two_full, up_full, preferred_element_type=f32)
    sigma = jax.nn.sigmoid(gate_lin)
    activated = gate_lin * sigma
    hidden_low = (activated * up_lin).astype(bf16)
    layer_output = (
        attended
        + lax.psum_scatter(
            jnp.dot(hidden_low, down_full, preferred_element_type=f32).astype(jnp.bfloat16),
            "tensor",
            scatter_dimension=0,
            tiled=True,
        ).astype(jnp.float32)
    ).astype(bf16)
    fresh = (
        lax.all_gather(query_weight, "dp", axis=0, tiled=True),
        lax.all_gather(key_weight, "dp", axis=0, tiled=True),
        lax.all_gather(value_weight, "dp", axis=0, tiled=True),
        lax.all_gather(out_weight, "dp", axis=1, tiled=True),
        lax.all_gather(gate_weight, "dp", axis=0, tiled=True),
        lax.all_gather(up_weight, "dp", axis=0, tiled=True),
        lax.all_gather(down_weight, "dp", axis=1, tiled=True),
        lax.all_gather(second_gain, "dp", axis=0, tiled=True),
    )
    query_back, key_back, value_back, out_back, gate_back, up_back, down_back, gain_back = fresh
    grad_full = lax.all_gather(out_grad, "tensor", axis=0, tiled=True)
    grad_hidden = jnp.einsum("sd,fd->sf", grad_full, down_back, preferred_element_type=f32)
    down_grad = jnp.einsum("sf,sd->fd", hidden_low, grad_full, preferred_element_type=f32)
    grad_gate = (grad_hidden * up_lin * sigma * (1.0 + gate_lin * (1.0 - sigma))).astype(bf16)
    grad_up = (grad_hidden * activated).astype(bf16)
    gate_grad = jnp.einsum("sd,sf->df", norm_two_full, grad_gate, preferred_element_type=f32)
    up_grad = jnp.einsum("sd,sf->df", norm_two_full, grad_up, preferred_element_type=f32)
    grad_norm_two = lax.psum_scatter(
        jnp.einsum("sf,df->sd", grad_gate, gate_back, preferred_element_type=f32)
        + jnp.einsum("sf,df->sd", grad_up, up_back, preferred_element_type=f32),
        "tensor",
        scatter_dimension=0,
        tiled=True,
    )
    gain_two_grad = jnp.sum(grad_norm_two * hat_two, axis=0)
    shift_two_grad = jnp.sum(grad_norm_two, axis=0)
    grad_attended = out_grad.astype(f32) + norm_backward(
        grad_norm_two, hat_two, rstd_two, gain_back.astype(f32)
    )
    residual_full = lax.all_gather(grad_attended.astype(bf16), "tensor", axis=0, tiled=True)
    grad_mixed = jnp.einsum(
        "sd,kd->sk", residual_full, out_back, preferred_element_type=f32
    ).astype(bf16)
    out_weight_grad = jnp.einsum("sk,sd->kd", mixed_low, residual_full, preferred_element_type=f32)
    grad_qrot, grad_krot, grad_vheads = attend_backward(
        q_rot, k_rot, v_heads, segments, log_sums, grad_mixed.reshape(total_rows, local_heads, HD)
    )
    grad_query = turn(grad_qrot, cosine, sine, -1.0).reshape(total_rows, -1)
    grad_key = turn(grad_krot, cosine, sine, -1.0).reshape(total_rows, -1)
    grad_value = grad_vheads.reshape(total_rows, -1)
    query_bias_grad = jnp.sum(grad_query, axis=0).reshape(local_heads, HD)
    key_bias_grad = jnp.sum(grad_key, axis=0).reshape(local_heads, HD)[:, :ROT]
    value_bias_grad = jnp.sum(grad_value, axis=0).reshape(local_heads, HD)
    query_low = grad_query.astype(bf16)
    key_low = grad_key.astype(bf16)
    value_low = grad_value.astype(bf16)
    query_weight_grad = jnp.einsum(
        "sd,sk->dk", norm_one_full, query_low, preferred_element_type=f32
    )
    key_weight_grad = jnp.einsum("sd,sk->dk", norm_one_full, key_low, preferred_element_type=f32)
    value_weight_grad = jnp.einsum(
        "sd,sk->dk", norm_one_full, value_low, preferred_element_type=f32
    )
    total = jnp.einsum("sk,dk->sd", query_low, query_back, preferred_element_type=f32)
    total = total + jnp.einsum("sk,dk->sd", key_low, key_back, preferred_element_type=f32)
    grad_norm_one = lax.psum_scatter(
        total + jnp.einsum("sk,dk->sd", value_low, value_back, preferred_element_type=f32),
        "tensor",
        scatter_dimension=0,
        tiled=True,
    )
    gain_one_grad = jnp.sum(grad_norm_one * hat_one, axis=0)
    shift_one_grad = jnp.sum(grad_norm_one, axis=0)
    input_grad = grad_attended + norm_backward(grad_norm_one, hat_one, rstd_one, gain_one_f)
    gate_sum, up_sum, down_sum = (
        lax.psum_scatter(gate_grad, "dp", scatter_dimension=0, tiled=True),
        lax.psum_scatter(up_grad, "dp", scatter_dimension=0, tiled=True),
        lax.psum_scatter(down_grad, "dp", scatter_dimension=1, tiled=True),
    )
    query_sum, key_sum, value_sum, out_sum, bquery_sum, bvalue_sum = (
        lax.psum_scatter(query_weight_grad, "dp", scatter_dimension=0, tiled=True),
        lax.psum_scatter(key_weight_grad, "dp", scatter_dimension=0, tiled=True),
        lax.psum_scatter(value_weight_grad, "dp", scatter_dimension=0, tiled=True),
        lax.psum_scatter(out_weight_grad, "dp", scatter_dimension=1, tiled=True),
        lax.psum_scatter(query_bias_grad, "dp", scatter_dimension=1, tiled=True),
        lax.psum_scatter(value_bias_grad, "dp", scatter_dimension=1, tiled=True),
    )
    bkey_sum = lax.psum(key_bias_grad, "dp")
    gain_one_sum, shift_one_sum, gain_two_sum, shift_two_sum = (
        lax.psum_scatter(gain_one_grad, ("dp", "tensor"), scatter_dimension=0, tiled=True),
        lax.psum_scatter(shift_one_grad, ("dp", "tensor"), scatter_dimension=0, tiled=True),
        lax.psum_scatter(gain_two_grad, ("dp", "tensor"), scatter_dimension=0, tiled=True),
        lax.psum_scatter(shift_two_grad, ("dp", "tensor"), scatter_dimension=0, tiled=True),
    )
    return (
        layer_output,
        input_grad,
        gain_one_sum,
        shift_one_sum,
        query_sum,
        key_sum,
        value_sum,
        bquery_sum,
        bkey_sum,
        bvalue_sum,
        out_sum,
        gain_two_sum,
        shift_two_sum,
        gate_sum,
        up_sum,
        down_sum,
    )


def solution(mesh):
    return jax.shard_map(
        local,
        mesh=mesh,
        in_specs=(
            P(("dp", "tensor"), None),
            P("dp"),
            P("dp"),
            P("dp"),
            P("dp"),
            P("dp", "tensor"),
            P("dp", "tensor"),
            P("dp", "tensor"),
            P("tensor", "dp"),
            P("tensor", None),
            P("tensor", "dp"),
            P("tensor", "dp"),
            P("dp"),
            P("dp"),
            P("dp", "tensor"),
            P("dp", "tensor"),
            P("tensor", "dp"),
            P(("dp", "tensor"), None),
        ),
        out_specs=(
            P(("dp", "tensor"), None),
            P(("dp", "tensor"), None),
            P(("dp", "tensor")),
            P(("dp", "tensor")),
            P("dp", "tensor"),
            P("dp", "tensor"),
            P("dp", "tensor"),
            P("tensor", "dp"),
            P("tensor", None),
            P("tensor", "dp"),
            P("tensor", "dp"),
            P(("dp", "tensor")),
            P(("dp", "tensor")),
            P("dp", "tensor"),
            P("dp", "tensor"),
            P("tensor", "dp"),
        ),
        check_vma=False,
    )
```

profile of v0, /device:TPU:0, one launch (start us, length us, event | category | flops | bytes accessed | tf_op | source)
XLA Modules:
  0.0 2123.2 jit_solution(928444203976927270)
XLA Ops:
  9.3 22.2 %all-gather.1 = bf16[8,1,256]{2,1,0:T(2,128)(2,1)S(1)} all-gather(bf16[1,1,256]{2,1,0:T(2,128)(2,1)S(1)} %reshape.335), channel_id=1, replica_groups=mesh['dp'=8,'tensor'=4] {'dp'}, dimensions={0}, use_global_device_ids=true | all-gather | bytes 4608 | tf_op jit(solution)/shard_map/all_gather | solution.py:151
  31.5 16.4 all-gather
  55.5 26.0 %all_gather.66 = bf16[8,64]{0,1:T(8,128)(2,1)S(1)} all-gather(bf16[8,8]{0,1:T(8,128)(2,1)S(1)} %copy.48), channel_id=1, replica_groups=mesh['dp'=8,'tensor'=4] {'dp'}, dimensions={1}, use_global_device_ids=true | all-gather | bytes 1152 | tf_op jit(solution)/shard_map/all_gather | solution.py:149
  81.6 26.0 %all_gather.63 = bf16[8,64]{0,1:T(8,128)(2,1)S(1)} all-gather(bf16[8,8]{0,1:T(8,128)(2,1)S(1)} %copy.46), channel_id=1, replica_groups=mesh['dp'=8,'tensor'=4] {'dp'}, dimensions={1}, use_global_device_ids=true | all-gather | bytes 1152 | tf_op jit(solution)/shard_map/all_gather | solution.py:148
  115.3 33.6 %all-gather.18.cloned.1.call-done = bf16[2048,512]{1,0:T(8,128)(2,1)} async-done(((bf16[256,512]{1,0:T(8,128)(2,1)}), bf16[2048,512]{1,0:T(8,128)(2,1)}) %all-gather.18.cloned.1.call-update) | async-done | bytes 2097168 | tf_op jit(solution)/shard_map/all_gather | solution.py:144
  157.0 41.7 %all-gather.22.cloned.1.call-done = bf16[2048,512]{1,0:T(8,128)(2,1)} async-done(((bf16[256,512]{1,0:T(8,128)(2,1)}), bf16[2048,512]{1,0:T(8,128)(2,1)}) %all-gather.22.cloned.1.call-update) | async-done | bytes 2097168 | tf_op jit(solution)/shard_map/all_gather | solution.py:146
  204.9 34.3 %while.31 = (s32[]{:T(128)}, bf16[2,512,8,64]{1,3,2,0:T(8,128)(2,1)S(1)}, f32[2,8,512]{2,1,0:T(8,128)S(1)}, s32[2]{0:T(128)S(1)}, s32[1024]{0:T(1024)S(1)}, /*in...) while((s32[]{:T(128)}, ...), condition=%wide.region_5.6_spmd, body=%wide.region_2.5_spmd.sunk | while | flops 1125643776 | bytes 56252800 | solution.py:83
  240.6 9.7 all-gather.24.cloned.1.call-done
  250.2 7.2 fusion.66
  258.4 17.7 all-gather.3
  276.1 16.9 all-gather.2
  292.9 34.6 %reduce-scatter.14.cloned.1.call-done = f32[256,2048]{1,0:T(8,128)} async-done(((f32[1024,2048]{1,0:T(8,128)}), f32[256,2048]{1,0:T(8,128)}) %reduce-scatter.14.cloned.1.call-update) | async-done | bytes 2097168 | tf_op jit(solution)/shard_map/reduce_scatter | solution.py:182
  333.4 89.3 %all-gather.30.cloned.1.call-done = bf16[2048,1408]{1,0:T(8,128)(2,1)} async-done(((bf16[256,1408]{1,0:T(8,128)(2,1)}), bf16[2048,1408]{1,0:T(8,128)(2,1)}) %all-gather.30.cloned.1.call-update) | async-done | bytes 5767184 | tf_op jit(solution)/shard_map/all_gather | solution.py:155
  422.7 34.9 %all-gather.26.cloned.1.call-done = bf16[1024,2048]{1,0:T(8,128)(2,1)} async-done(((bf16[256,2048]{1,0:T(8,128)(2,1)}), bf16[1024,2048]{1,0:T(8,128)(2,1)}) %all-gather.26.cloned.1.call-update) | async-done | bytes 4194320 | tf_op jit(solution)/shard_map/all_gather | solution.py:190
  457.6 11.9 fusion.68
  469.5 83.2 %all-gather.28.cloned.1.call-done = bf16[2048,1408]{1,0:T(8,128)(2,1)} async-done(((bf16[256,1408]{1,0:T(8,128)(2,1)}), bf16[2048,1408]{1,0:T(8,128)(2,1)}) %all-gather.28.cloned.1.call-update) | async-done | bytes 5767184 | tf_op jit(solution)/shard_map/all_gather | solution.py:154
  552.7 11.7 fusion.67
  564.4 22.5 %all-gather.34.cloned.1.call-done = bf16[1024,2048]{1,0:T(8,128)(2,1)} async-done(((bf16[256,2048]{1,0:T(8,128)(2,1)}), bf16[1024,2048]{1,0:T(8,128)(2,1)}) %all-gather.34.cloned.1.call-update) | async-done | bytes 4194320 | tf_op jit(solution)/shard_map/all_gather | solution.py:216
  586.9 95.9 %all-gather.32.cloned.1.call-done = bf16[1408,2048]{1,0:T(8,128)(2,1)} async-done(((bf16[1408,256]{1,0:T(8,128)(2,1)}), bf16[1408,2048]{1,0:T(8,128)(2,1)}) %all-gather.32.cloned.1.call-update) | async-done | bytes 5767184 | tf_op jit(solution)/shard_map/all_gather | solution.py:156
  682.8 16.6 multiply_convert_fusion.1
  699.4 8.7 fusion.69
  708.1 11.1 convolution_add_fusion
  719.2 10.9 convolution_convert_fusion
  730.2 59.0 %reduce-scatter.18.cloned.1.call-done = f32[256,2048]{1,0:T(8,128)} async-done(((f32[1024,2048]{1,0:T(8,128)}), f32[256,2048]{1,0:T(8,128)}) %reduce-scatter.18.cloned.1.call-update) | async-done | bytes 2097168 | tf_op jit(solution)/shard_map/reduce_scatter | solution.py:223
  792.4 44.0 %reduce-scatter.16.cloned.1.call-done = bf16[256,2048]{1,0:T(8,128)(2,1)} async-done(((bf16[1024,2048]{1,0:T(8,128)(2,1)}), bf16[256,2048]{1,0:T(8,128)(2,1)}) %reduce-scatter.16.cloned.1.call-update) | async-done | bytes 1048592 | tf_op jit(solution)/shard_map/reduce_scatter | solution.py:198
  841.4 34.6 %all-gather.36.cloned.1.call-done = bf16[1024,2048]{1,0:T(8,128)(2,1)} async-done(((bf16[256,2048]{1,0:T(8,128)(2,1)}), bf16[1024,2048]{1,0:T(8,128)(2,1)}) %all-gather.36.cloned.1.call-update) | async-done | bytes 4194320 | tf_op jit(solution)/shard_map/all_gather | solution.py:235
  882.2 183.5 %while.32 = (s32[]{:T(128)}, f32[1024,8,64]{0,2,1:T(8,128)}, f32[1024,8,64]{0,2,1:T(8,128)S(1)}, f32[2,512,8,64]{1,0,3,2:T(2,128)}, s32[2]{0:T(128)S(1)}, /*inde...) while((s32[]{:T(128)}, f32[1024,8,64]{0,2,1:T(8,128)}, ...), condition=%wide.region_15.16_spmd.clone, body=%wide.region_13.15_spmd.clone.sunk | while | flops 2746756608 | bytes 238098896 | solution.py:115
  896.1 9.5 fusion.158
  905.6 22.9 %fusion.159 = f32[1,512,8,64]{1,3,2,0:T(8,128)} fusion(bf16[1024,8,64]{0,2,1:T(8,128)(2,1)} %get-tuple-element.590, f32[8,512,1024]{2,1,0:T(8,128)} %copy-done, f32[8,512,1024]{2,1,0:T(8,128)} %fusion.158), kind=kOutput, calls=%fused_computation.31.clone.1 | convolution fusion | flops 557847552 | bytes 35651584 | tf_op jit(solution)/shard_map/while/body/eval_jaxpr/hqk,khd->qhd/dot_general | solution.py:103
  928.5 23.5 %bitcast_add_fusion.4 = f32[1024,8,64]{0,2,1:T(8,128)} fusion(f32[1024,8,64]{0,2,1:T(8,128)} %get-tuple-element.566, f32[8,512,1024]{2,1,0:T(8,128)} %copy-done, f32[8,512,1024]{2,1,0:T(8,128)} %fusion.158, pred[]{:T(512)S(6)} %compare.14, bf16[1024,8,64]{0,2,1:T(8,128)(2,1)} %get-tuple-element.588, s32[]{:T(128)S(6)} %select_n.75), kind=kOutput, calls=%fused_computation.29.clone.1 | convolution fusion | flops 558896128 | bytes 71827464 | tf_op jit(solution)/shard_map/while/body/eval_jaxpr/hqk,qhd->khd/dot_general | solution.py:104
  954.2 19.6 dynamic_update_slice.28
  987.3 9.5 fusion.158
  996.8 22.9 %fusion.159 = f32[1,512,8,64]{1,3,2,0:T(8,128)} fusion(bf16[1024,8,64]{0,2,1:T(8,128)(2,1)} %get-tuple-element.590, f32[8,512,1024]{2,1,0:T(8,128)} %copy-done, f32[8,512,1024]{2,1,0:T(8,128)} %fusion.158), kind=kOutput, calls=%fused_computation.31.clone.1 | convolution fusion | flops 557847552 | bytes 35651584 | tf_op jit(solution)/shard_map/while/body/eval_jaxpr/hqk,khd->qhd/dot_general | solution.py:103
  1019.7 24.0 %bitcast_add_fusion.4 = f32[1024,8,64]{0,2,1:T(8,128)} fusion(f32[1024,8,64]{0,2,1:T(8,128)} %get-tuple-element.566, f32[8,512,1024]{2,1,0:T(8,128)} %copy-done, f32[8,512,1024]{2,1,0:T(8,128)} %fusion.158, pred[]{:T(512)S(6)} %compare.14, bf16[1024,8,64]{0,2,1:T(8,128)(2,1)} %get-tuple-element.588, s32[]{:T(128)S(6)} %select_n.75), kind=kOutput, calls=%fused_computation.29.clone.1 | convolution fusion | flops 558896128 | bytes 71827464 | tf_op jit(solution)/shard_map/while/body/eval_jaxpr/hqk,qhd->khd/dot_general | solution.py:104
  1046.0 19.6 dynamic_update_slice.28
  1086.2 12.3 fusion.78
  1098.5 12.9 fusion.77
  1111.5 11.9 fusion.76
  1123.5 7.1 fusion.75
  1154.6 38.4 %all-reduce.8 = (f32[8,64]{1,0:T(8,128)S(1)}, f32[8,16]{1,0:T(8,128)}, f32[8,64]{1,0:T(8,128)S(1)}) all-reduce(f32[8,64]{1,0:T(8,128)S(1)} %fusion.61, f32[8,16]{1,0:T(8,128)S(1)} %bitcast.138, f32[8,64]{1,0:T(8,128)S(1)} %get-tuple-element.370), channel_id=11, replica_groups=mesh['dp'=8,'tensor'=4] {'dp'}, use_global_device_ids=true, to_apply=%region_27.28.clone | all-reduce | flops 1152 | bytes 9216
  1197.1 41.1 %all-reduce.7 = (f32[2048]{0:T(1024)S(1)}, f32[2048]{0:T(1024)S(1)}, f32[2048]{0:T(1024)S(1)}, f32[2048]{0:T(1024)S(1)}) all-reduce(f32[2048]{0:T(1024)S(1)} %get-tuple-element.302, f32[2048]{0:T(1024)S(1)} %get-tuple-element.307, f32[2048]{0:T(1024)S(1)} %copy-done.24, ...), channel_id=6, replica_groups=mesh['dp'=8,'tensor'=4] {'dp','tensor'}, use_global_device_ids=true, to_apply=%region_20.21.clone | all-reduce | flops 8192 | bytes 65536
  1244.3 111.9 %reduce-scatter.34.cloned.1.call-done = f32[1408,256]{1,0:T(8,128)} async-done(((f32[1408,2048]{1,0:T(8,128)}), f32[1408,256]{1,0:T(8,128)}) %reduce-scatter.34.cloned.1.call-update) | async-done | bytes 1441808 | tf_op jit(solution)/shard_map/reduce_scatter | solution.py:273
  1356.3 195.9 %reduce-scatter.32.cloned.1.call-done = f32[256,1408]{1,0:T(8,128)} async-done(((f32[2048,1408]{1,0:T(8,128)}), f32[256,1408]{1,0:T(8,128)}) %reduce-scatter.32.cloned.1.call-update) | async-done | bytes 1441808 | tf_op jit(solution)/shard_map/reduce_scatter | solution.py:272
  1552.1 195.8 %reduce-scatter.30.cloned.1.call-done = f32[256,1408]{1,0:T(8,128)} async-done(((f32[2048,1408]{1,0:T(8,128)}), f32[256,1408]{1,0:T(8,128)}) %reduce-scatter.30.cloned.1.call-update) | async-done | bytes 1441808 | tf_op jit(solution)/shard_map/reduce_scatter | solution.py:271
  1747.9 91.6 %reduce-scatter.28.cloned.1.call-done = f32[512,256]{1,0:T(8,128)} async-done(((f32[512,2048]{1,0:T(8,128)}), f32[512,256]{1,0:T(8,128)}) %reduce-scatter.28.cloned.1.call-update) | async-done | bytes 524304 | tf_op jit(solution)/shard_map/reduce_scatter | solution.py:279
  1839.6 92.2 %reduce-scatter.26.cloned.1.call-done = f32[256,512]{1,0:T(8,128)} async-done(((f32[2048,512]{1,0:T(8,128)}), f32[256,512]{1,0:T(8,128)}) %reduce-scatter.26.cloned.1.call-update) | async-done | bytes 524304 | tf_op jit(solution)/shard_map/reduce_scatter | solution.py:278
  1931.8 91.9 %reduce-scatter.24.cloned.1.call-done = f32[256,512]{1,0:T(8,128)} async-done(((f32[2048,512]{1,0:T(8,128)}), f32[256,512]{1,0:T(8,128)}) %reduce-scatter.24.cloned.1.call-update) | async-done | bytes 524304 | tf_op jit(solution)/shard_map/reduce_scatter | solution.py:277
  2023.6 92.3 %reduce-scatter.22.cloned.1.call-done = f32[256,512]{1,0:T(8,128)} async-done(((f32[2048,512]{1,0:T(8,128)}), f32[256,512]{1,0:T(8,128)}) %reduce-scatter.22.cloned.1.call-update) | async-done | bytes 524304 | tf_op jit(solution)/shard_map/reduce_scatter | solution.py:276
  (243 shorter events, 170.3 us)
Async XLA Ops:
  7.2 44.6 %copy-start.1 = (bf16[256,2048]{1,0:T(8,128)(2,1)S(1)}, bf16[256,2048]{1,0:T(8,128)(2,1)}, u32[]{:S(2)}) copy-start(bf16[256,2048]{1,0:T(8,128)(2,1)} %param.22) | copy-start | bytes 3145732
  7.2 101.4 %all-gather.20.cloned.1.call-start = ((), (), s32[]{:S(2)}) async-start(), calls=%async_computation.13 | async-start | bytes 2359296 | tf_op jit(solution)/shard_map/all_gather | solution.py:145
  7.9 100.7 %all-gather.16.cloned.1.call-start = ((), (), s32[]{:S(2)}) async-start(), calls=%async_computation.11 | async-start | bytes 5242880 | tf_op jit(solution)/shard_map/all_gather | solution.py:163
  48.0 3.2 copy-start.22
  48.0 7.2 copy-start.32
  48.0 7.3 copy-start.33
  48.0 7.4 copy-start.30
  48.0 7.4 copy-start.31
  53.2 95.7 %all-gather.18.cloned.1.call-start = ((), (), s32[]{:S(2)}) async-start(), calls=%async_computation.12 | async-start | bytes 2359296 | tf_op jit(solution)/shard_map/all_gather | solution.py:144
  53.9 144.8 %all-gather.22.cloned.1.call-start = ((), (), s32[]{:S(2)}) async-start(), calls=%async_computation.14 | async-start | bytes 2359296 | tf_op jit(solution)/shard_map/all_gather | solution.py:146
  54.5 195.7 %all-gather.24.cloned.1.call-start = ((), (), s32[]{:S(2)}) async-start(), calls=%async_computation.15 | async-start | bytes 2359296 | tf_op jit(solution)/shard_map/all_gather | solution.py:147
  55.1 272.5 %reduce-scatter.14.cloned.1.call-start = ((), (), s32[]{:S(2)}) async-start(), calls=%async_computation.16 | async-start | bytes 10485760 | tf_op jit(solution)/shard_map/reduce_scatter | solution.py:182
  108.6 45.7 %copy-start.19 = (f32[1024,8]{0,1:T(8,128)}, f32[1024,8]{0,1:T(8,128)S(1)}, u32[]{:S(2)}) copy-start(f32[1024,8]{0,1:T(8,128)S(1)} %get-tuple-element.379) | copy-start | bytes 98308
  157.0 47.9 %copy-start.17 = (s32[1024]{0:T(1024)S(1)}, s32[1024]{0:T(1024)}, u32[]{:S(2)}) copy-start(s32[1024]{0:T(1024)} %param.23) | copy-start | bytes 12292
  240.5 16.9 copy-start.16
  257.5 70.1 %copy-start.2 = (bf16[256,2048]{1,0:T(8,128)(2,1)S(1)}, bf16[256,2048]{1,0:T(8,128)(2,1)}, u32[]{:S(2)}) copy-start(bf16[256,2048]{1,0:T(8,128)(2,1)} %param.22) | copy-start | bytes 3145732
  257.5 165.2 %all-gather.30.cloned.1.call-start = ((), (), s32[]{:S(2)}) async-start(), calls=%async_computation.19 | async-start | bytes 6488064 | tf_op jit(solution)/shard_map/all_gather | solution.py:155
  258.3 199.3 %all-gather.26.cloned.1.call-start = ((), (), s32[]{:S(2)}) async-start(), calls=%async_computation.17 | async-start | bytes 5242880 | tf_op jit(solution)/shard_map/all_gather | solution.py:190
  331.3 221.4 %all-gather.28.cloned.1.call-start = ((), (), s32[]{:S(2)}) async-start(), calls=%async_computation.18 | async-start | bytes 6488064 | tf_op jit(solution)/shard_map/all_gather | solution.py:154
  332.0 254.9 %all-gather.34.cloned.1.call-start = ((), (), s32[]{:S(2)}) async-start(), calls=%async_computation.22 | async-start | bytes 5242880 | tf_op jit(solution)/shard_map/all_gather | solution.py:216
  332.6 350.1 %all-gather.32.cloned.1.call-start = ((), (), s32[]{:S(2)}) async-start(), calls=%async_computation.20 | async-start | bytes 6488064 | tf_op jit(solution)/shard_map/all_gather | solution.py:156
  333.3 455.9 %reduce-scatter.18.cloned.1.call-start = ((), (), s32[]{:S(2)}) async-start(), calls=%async_computation.23 | async-start | bytes 10485760 | tf_op jit(solution)/shard_map/reduce_scatter | solution.py:223
  682.8 16.6 copy-start.34
  699.4 8.7 copy-start.40
  719.2 117.2 %reduce-scatter.16.cloned.1.call-start = ((), (), s32[]{:S(2)}) async-start(), calls=%async_computation.21 | async-start | bytes 5242880 | tf_op jit(solution)/shard_map/reduce_scatter | solution.py:198
  730.2 106.2 %copy-start.8 = (bf16[256,2048]{1,0:T(8,128)(2,1)S(1)}, bf16[256,2048]{1,0:T(8,128)(2,1)}, u32[]{:S(2)}) copy-start(bf16[256,2048]{1,0:T(8,128)(2,1)} %param.39) | copy-start | bytes 3145732
  730.2 145.8 %all-gather.36.cloned.1.call-start = ((), (), s32[]{:S(2)}) async-start(), calls=%async_computation.24 | async-start | bytes 5242880 | tf_op jit(solution)/shard_map/all_gather | solution.py:235
  841.3 353.0 %reduce-scatter.20.cloned.1.call-start = ((), (), s32[]{:S(2)}) async-start(), calls=%async_computation.25 | async-start | bytes 10485760 | tf_op jit(solution)/shard_map/reduce_scatter | solution.py:261
  890.4 5.7 copy-start
  981.6 5.7 copy-start
  1071.4 3.0 copy-start.4
  1075.5 2.4 copy-start.36
  1086.1 270.1 %reduce-scatter.34.cloned.1.call-start = ((), (), s32[]{:S(2)}) async-start(), calls=%async_computation.32 | async-start | bytes 12976128 | tf_op jit(solution)/shard_map/reduce_scatter | solution.py:273
  1098.5 453.6 %reduce-scatter.32.cloned.1.call-start = ((), (), s32[]{:S(2)}) async-start(), calls=%async_computation.31 | async-start | bytes 12976128 | tf_op jit(solution)/shard_map/reduce_scatter | solution.py:272
  1111.5 636.4 %reduce-scatter.30.cloned.1.call-start = ((), (), s32[]{:S(2)}) async-start(), calls=%async_computation.30 | async-start | bytes 12976128 | tf_op jit(solution)/shard_map/reduce_scatter | solution.py:271
  1123.5 716.1 %reduce-scatter.28.cloned.1.call-start = ((), (), s32[]{:S(2)}) async-start(), calls=%async_computation.29 | async-start | bytes 4718592 | tf_op jit(solution)/shard_map/reduce_scatter | solution.py:279
  1130.6 801.1 %reduce-scatter.26.cloned.1.call-start = ((), (), s32[]{:S(2)}) async-start(), calls=%async_computation.28 | async-start | bytes 4718592 | tf_op jit(solution)/shard_map/reduce_scatter | solution.py:278
  1137.4 886.3 %reduce-scatter.24.cloned.1.call-start = ((), (), s32[]{:S(2)}) async-start(), calls=%async_computation.27 | async-start | bytes 4718592 | tf_op jit(solution)/shard_map/reduce_scatter | solution.py:277
  1144.3 971.7 %reduce-scatter.22.cloned.1.call-start = ((), (), s32[]{:S(2)}) async-start(), calls=%async_computation.26 | async-start | bytes 4718592 | tf_op jit(solution)/shard_map/reduce_scatter | solution.py:276
  1150.9 3.5 copy-start.5
  1150.9 3.5 copy-start.10
  1150.9 43.4 %copy-start.3 = (bf16[256,2048]{1,0:T(8,128)(2,1)S(1)}, bf16[256,2048]{1,0:T(8,128)(2,1)}, u32[]{:S(2)}) copy-start(bf16[256,2048]{1,0:T(8,128)(2,1)} %param.22) | copy-start | bytes 3145732
  1151.0 43.4 %copy-start.23 = (f32[8,1,256]{2,1,0:T(1,128)S(1)}, f32[8,1,256]{2,1,0:T(1,128)}, u32[]{:S(2)}) copy-start(f32[8,1,256]{2,1,0:T(1,128)} %copy-done.22) | copy-start | bytes 24580
  1151.0 43.4 %copy-start.27 = (f32[256]{0:T(256)S(1)}, f32[256]{0:T(256)}, u32[]{:S(2)}) copy-start(f32[256]{0:T(256)} %copy-done.26) | copy-start | bytes 3076
  1151.0 43.4 %copy-start.29 = (f32[256]{0:T(256)S(1)}, f32[256]{0:T(256)}, u32[]{:S(2)}) copy-start(f32[256]{0:T(256)} %copy-done.28) | copy-start | bytes 3076
  1154.4 42.6 %copy-start.24 = (f32[2048]{0:T(1024)S(1)}, f32[2048]{0:T(1024)}, u32[]{:S(2)}) copy-start(f32[2048]{0:T(1024)} %get-tuple-element.300) | copy-start | bytes 24580
  1154.4 42.6 %copy-start.25 = (f32[2048]{0:T(1024)S(1)}, f32[2048]{0:T(1024)}, u32[]{:S(2)}) copy-start(f32[2048]{0:T(1024)} %get-tuple-element.306) | copy-start | bytes 24580
  1194.4 46.2 %copy-start.7 = (f32[256,2048]{1,0:T(8,128)S(1)}, f32[256,2048]{1,0:T(8,128)}, u32[]{:S(2)}) copy-start(f32[256,2048]{1,0:T(8,128)} %reduce-scatter.20.cloned.1.call-done) | copy-start | bytes 6291460
  (16 other events, 22.9 us)
Sparse Core Ops, SparseCore 0:
  10.2 52.0 all-gather.19
  64.4 33.0 all-gather.15
  99.6 49.2 all-gather.17
  150.9 47.7 all-gather.21
  200.6 49.6 all-gather.23
  257.6 69.8 reduce-scatter.13
  330.0 92.6 all-gather.29
  424.9 32.6 all-gather.25
  460.0 92.6 all-gather.27
  554.2 32.6 all-gather.33
  589.1 93.5 all-gather.31
  719.3 69.9 reduce-scatter.17
  791.8 44.4 reduce-scatter.15
  841.5 34.4 all-gather.35
  1086.3 71.6 reduce-scatter.19
  1162.0 194.1 reduce-scatter.33
  1360.3 191.8 reduce-scatter.31
  1556.1 191.7 reduce-scatter.29
  1752.1 87.3 reduce-scatter.27
  1844.1 87.6 reduce-scatter.25
  1936.0 87.6 reduce-scatter.23
  2028.3 87.6 reduce-scatter.21
where the time goes:
time: 2130 us; the launch traced here: 2120 us
  waiting for transfers between devices  1460 us (69%)
  matrix products  328 us (15%)
  blocking collectives  205 us (10%)
  local copies, waits for them, and re-layouts  69 us (3%)
  other arithmetic  40.7 us (2%)
    reduce_scatter x1, waiting for transfers between devices, local(): lax.psum_scatter(up_grad, 'dp', scatter_dimension=0, tiled=True)  196 us
    reduce_scatter x1, waiting for transfers between devices, local(): lax.psum_scatter(gate_grad, 'dp', scatter_dimension=0, tiled=True)  196 us
    reduce_scatter x1, waiting for transfers between devices, local(): lax.psum_scatter(down_grad, 'dp', scatter_dimension=1, tiled=True)  112 us
    all_gather x1, waiting for transfers between devices, local(): lax.all_gather(down_weight, 'dp', axis=1, tiled=True)  95.9 us
    reduce_scatter x1, waiting for transfers between devices, local(): lax.psum_scatter(query_weight_grad, 'dp', scatter_dimension=0, tiled=True)  92.3 us
    reduce_scatter x1, waiting for transfers between devices, local(): lax.psum_scatter(value_weight_grad, 'dp', scatter_dimension=0, tiled=True)  92.2 us
    reduce_scatter x1, waiting for transfers between devices, local(): lax.psum_scatter(key_weight_grad, 'dp', scatter_dimension=0, tiled=True)  91.9 us
    reduce_scatter x1, waiting for transfers between devices, local(): lax.psum_scatter(out_weight_grad, 'dp', scatter_dimension=1, tiled=True)  91.6 us
  transfers between devices with their start and end apart: 22, of which 19 were waited for; matrix products, arithmetic and copies ran while one was open for 8% of the time, Pallas kernels for 0%

commit v1 on v0

v1 whole, which is shorter than its diff:
```python
import math

import jax
import jax.numpy as jnp
from jax import lax
from jax.experimental import pallas as pl
from jax.experimental.pallas import tpu as pltpu
from jax.sharding import PartitionSpec as P

HD = 64
ROT = 16
SEQ = 1024
HALF = ROT // 2
SCALE = HD ** (-0.5)

EPS = 1e-05
NEG = -1e30
QB = 256
f32 = jnp.float32
bf16 = jnp.bfloat16


def barrier(value, after):
    return lax.optimization_barrier((value, after))[0]


class Ring:
    def __init__(self):
        self.n = lax.axis_size("dp")
        self.ring = self.n % 2 == 0 and self.n <= 8
        order = list(range(0, self.n, 2)) + list(range(self.n - 1, 0, -2))
        self.up = [(order[i], order[(i + 1) % self.n]) for i in range(self.n)]
        self.down = [(b, a) for a, b in self.up]
        me = lax.axis_index("dp")
        self.me = me
        self.pos = jnp.where(me % 2 == 0, me // 2, self.n - 1 - (me - 1) // 2)

    def owner(self, offset):
        p = (self.pos + offset + 2 * self.n) % self.n
        return jnp.where(p < self.n // 2, 2 * p, 2 * (self.n - 1 - p) + 1)

    def gather(self, shard, pieces=1, after=None):
        n = self.n
        rows, cols = shard.shape
        if not self.ring:
            return lax.all_gather(shard, "dp", axis=0, tiled=True), [shard] * n
        if after is not None:
            shard = barrier(shard, after)
        full = jnp.zeros((n, rows, cols), shard.dtype)
        full = lax.dynamic_update_slice(full, shard[None], (self.me, 0, 0))
        size = rows // (2 * pieces)
        lanes = []
        for k in range(2 * pieces):
            lanes.append([k % 2, k * size, shard[k * size : (k + 1) * size]])
        marks = []
        for step in range(1, n):
            for lane in lanes:
                way, base, block = lane
                block = lax.ppermute(block, "dp", self.down if way else self.up)
                lane[2] = block
                whose = self.owner(step if way else -step)
                full = lax.dynamic_update_slice(full, block[None], (whose, base, 0))
            marks.append(lanes[-1][2])
        return full.reshape(n * rows, cols), marks

    def scatter(self, partial, pieces=1, after=None):
        n = self.n
        if not self.ring:
            return lax.psum_scatter(partial.astype(bf16), "dp", scatter_dimension=0, tiled=True).astype(f32)
        cols = partial.shape[1]
        rows = partial.shape[0] // n
        partial = partial.reshape(n, rows, cols)
        size = rows // (2 * pieces)
        done = []
        for k in range(2 * pieces):
            way = k % 2

            def block(step):
                whose = self.owner(1 + step if way else -1 - step)
                return lax.dynamic_slice(partial, (whose, k * size, 0), (1, size, cols))[0].astype(f32)

            moving = block(0)
            for step in range(1, n):
                got = lax.ppermute(moving.astype(bf16), "dp", self.down if way else self.up)
                moving = got.astype(f32) + block(step)
            done.append(moving)
        return jnp.concatenate(done, axis=0)


CORE = [(0, 1), (1, 0), (2, 3), (3, 2)]
CHIP = [(0, 2), (2, 0), (1, 3), (3, 1)]


def tensor_gather(rows, after=None):
    if lax.axis_size("tensor") != 4:
        return lax.all_gather(rows, "tensor", axis=0, tiled=True)
    if after is not None:
        rows = barrier(rows, after)
    t = lax.axis_index("tensor")
    far = lax.ppermute(rows, "tensor", CHIP)
    near = lax.ppermute(rows, "tensor", CORE)
    last = lax.ppermute(far, "tensor", CORE)
    full = jnp.zeros((4,) + rows.shape, rows.dtype)
    for flip, block in ((0, rows), (1, near), (2, far), (3, last)):
        full = lax.dynamic_update_slice(full, block[None], (t ^ flip, 0, 0))
    return full.reshape(4 * rows.shape[0], rows.shape[1])


def tensor_scatter(partial):
    if lax.axis_size("tensor") != 4:
        return lax.psum_scatter(partial.astype(bf16), "tensor", scatter_dimension=0, tiled=True).astype(f32)
    t = lax.axis_index("tensor")
    rows = partial.shape[0] // 4
    blocks = partial.reshape(4, rows, partial.shape[1])

    def block(flip):
        return lax.dynamic_slice(blocks, (t ^ flip, 0, 0), (1,) + blocks.shape[1:])[0]

    other = lax.ppermute(block(3).astype(bf16), "tensor", CORE)
    own = lax.ppermute(block(1).astype(bf16), "tensor", CORE)
    far = lax.ppermute((block(2) + other.astype(f32)).astype(bf16), "tensor", CHIP)
    return block(0) + own.astype(f32) + far.astype(f32)


def sum_all(vector, axes):
    for axis in axes:
        n = lax.axis_size(axis)
        if n & (n - 1):
            vector = lax.psum(vector, axis)
            continue
        step = 1
        while step < n:
            vector = vector + lax.ppermute(vector, axis, [(i, i ^ step) for i in range(n)])
            step *= 2
    return vector


def rotate(rows, cosine, sine, direction):
    first, second = rows[:HALF], rows[HALF:ROT]
    return jnp.concatenate(
        [first * cosine - direction * second * sine, second * cosine + direction * first * sine, rows[ROT:]], axis=0
    )


def dot(a, b, dims):
    return lax.dot_general(a, b, ((dims[0], dims[1]), ((), ())), preferred_element_type=f32)


def forward_kernel(q_ref, k_ref, v_ref, cos_ref, sin_ref, bias_ref, mixed_ref, q_out, k_out, v_out, log_ref):
    seq = q_ref.shape[1]
    cosine, sine = cos_ref[...], sin_ref[...]
    v_all = v_ref[...].astype(bf16)
    v_out[...] = v_all
    parts = []
    for head in range(q_ref.shape[0] // HD):
        rows = slice(head * HD, (head + 1) * HD)
        q = rotate(q_ref[rows, :], cosine, sine, 1.0).astype(bf16)
        k = rotate(k_ref[rows, :], cosine, sine, 1.0).astype(bf16)
        q_out[rows, :] = q
        k_out[rows, :] = k
        keys = k.T
        values = v_all[rows, :]
        q = q * jnp.asarray(SCALE, bf16)
        cols = []
        for start in range(0, seq, QB):
            end = start + QB
            scores = dot(keys[:end], q[:, start:end], ((1,), (0,))) + bias_ref[:end, start:end]
            top = jnp.max(scores, axis=0, keepdims=True)
            expo = jnp.exp(scores - top)
            total = jnp.sum(expo, axis=0, keepdims=True)
            probs = (expo * (1.0 / total)).astype(bf16)
            cols.append(dot(values[:, :end], probs, ((1,), (0,))).astype(bf16))
            log_ref[0, head : head + 1, start:end] = top + jnp.log(total)
        parts.append(jnp.concatenate(cols, axis=1))
    mixed_ref[...] = jnp.concatenate(parts, axis=0).T


def attend_forward(lin, cosine, sine, bias):
    width, seq = lin.shape[0] // 3, lin.shape[1]
    pair = 2 * HD
    count = width // pair
    outs = []
    block = lambda base: pl.BlockSpec((pair, seq), lambda i: (base * count + i, 0))
    whole = lambda shape: pl.BlockSpec(shape, lambda i: (0, 0))
    return pl.pallas_call(
        forward_kernel,
        grid=(count,),
        in_specs=[block(0), block(1), block(2), whole(cosine.shape), whole(sine.shape), whole(bias.shape)],
        out_specs=[
            pl.BlockSpec((seq, pair), lambda i: (0, i)),
            pl.BlockSpec((pair, seq), lambda i: (i, 0)),
            pl.BlockSpec((pair, seq), lambda i: (i, 0)),
            pl.BlockSpec((pair, seq), lambda i: (i, 0)),
            pl.BlockSpec((1, 2, seq), lambda i: (i, 0, 0)),
        ],
        out_shape=[
            jax.ShapeDtypeStruct((seq, width), bf16),
            jax.ShapeDtypeStruct((width, seq), bf16),
            jax.ShapeDtypeStruct((width, seq), bf16),
            jax.ShapeDtypeStruct((width, seq), bf16),
            jax.ShapeDtypeStruct((count, 2, seq), f32),
        ],
        compiler_params=pltpu.CompilerParams(vmem_limit_bytes=48 << 20),
        cost_estimate=pl.CostEstimate(
            flops=4 * width * seq * seq, bytes_accessed=30 << 20, transcendentals=width // HD * seq * seq
        ),
        name="attend_forward",
    )(lin, lin, lin, cosine, sine, bias)


def backward_kernel(q_ref, k_ref, v_ref, d_ref, log_ref, cos_ref, sin_ref, bias_ref, dq_out, dk_out, dv_out, sums_ref, dk_acc, dv_acc):
    seq = q_ref.shape[1]
    cosine, sine = cos_ref[...], sin_ref[...]
    for head in range(q_ref.shape[0] // HD):
        rows = slice(head * HD, (head + 1) * HD)
        q, k, v, d = q_ref[rows, :], k_ref[rows, :], v_ref[rows, :], d_ref[rows, :]
        keys, values = k.T, v.T
        q_small = q * jnp.asarray(SCALE, bf16)
        dk_acc[...] = jnp.zeros_like(dk_acc)
        dv_acc[...] = jnp.zeros_like(dv_acc)
        cols = []
        for start in range(0, seq, QB):
            end = start + QB
            here = slice(start, end)
            scores = dot(keys[:end], q_small[:, here], ((1,), (0,))) + bias_ref[:end, here]
            probs = jnp.exp(scores - log_ref[0, head : head + 1, here])
            grad = dot(values[:end], d[:, here], ((1,), (0,)))
            both = probs * grad
            inner = jnp.sum(both, axis=0, keepdims=True)
            grad = ((both - probs * inner) * SCALE).astype(bf16)
            probs = probs.astype(bf16)
            cols.append(dot(k[:, :end], grad, ((1,), (0,))))
            dk_acc[:, :end] += dot(q[:, here], grad, ((1,), (1,)))
            dv_acc[:, :end] += dot(d[:, here], probs, ((1,), (1,)))
        dq = rotate(jnp.concatenate(cols, axis=1), cosine, sine, -1.0)
        dk = rotate(dk_acc[...], cosine, sine, -1.0)
        dv = dv_acc[...]
        for part, (out, value) in enumerate(((dq_out, dq), (dk_out, dk), (dv_out, dv))):
            out[rows, :] = value.astype(bf16)
            sums_ref[0, rows, part : part + 1] = jnp.sum(value, axis=1, keepdims=True)


def attend_backward(q, k, v, d, logs, cosine, sine, bias):
    width, seq = q.shape
    pair = 2 * HD
    count = width // pair
    block = pl.BlockSpec((pair, seq), lambda i: (i, 0))
    whole = lambda shape: pl.BlockSpec(shape, lambda i: (0, 0))
    return pl.pallas_call(
        backward_kernel,
        grid=(count,),
        in_specs=[block] * 4
        + [pl.BlockSpec((1, 2, seq), lambda i: (i, 0, 0)), whole(cosine.shape), whole(sine.shape), whole(bias.shape)],
        out_specs=[block] * 3 + [pl.BlockSpec((1, pair, 128), lambda i: (i, 0, 0))],
        out_shape=[jax.ShapeDtypeStruct((width, seq), bf16)] * 3 + [jax.ShapeDtypeStruct((count, pair, 128), f32)],
        scratch_shapes=[pltpu.VMEM((HD, seq), f32), pltpu.VMEM((HD, seq), f32)],
        compiler_params=pltpu.CompilerParams(vmem_limit_bytes=48 << 20),
        cost_estimate=pl.CostEstimate(
            flops=10 * width * seq * seq, bytes_accessed=30 << 20, transcendentals=width // HD * seq * seq
        ),
        name="attend_backward",
    )(q, k, v, d, logs, cosine, sine, bias)


def norm_forward(rows):
    center = rows - jnp.mean(rows, axis=-1, keepdims=True)
    rstd = lax.rsqrt(jnp.mean(center * center, axis=-1, keepdims=True) + EPS)
    return center * rstd, rstd


def norm_backward(grad_out, normal, rstd, gain):
    scaled = grad_out * gain
    return rstd * (
        scaled
        - jnp.mean(scaled, axis=-1, keepdims=True)
        - normal * jnp.mean(scaled * normal, axis=-1, keepdims=True)
    )


def local(
    layer_input,
    segments,
    positions,
    first_gain,
    first_shift,
    query_weight,
    key_weight,
    value_weight,
    query_bias,
    key_bias,
    value_bias,
    out_weight,
    second_gain,
    second_shift,
    gate_weight,
    up_weight,
    down_weight,
    out_grad,
):
    ring = Ring()
    n = ring.n
    width = query_weight.shape[1]
    heads = width // HD
    model = layer_input.shape[1]

    x_full = tensor_gather(layer_input)
    g_full = tensor_gather(out_grad, after=x_full)

    small = jnp.concatenate(
        [first_gain, first_shift, second_gain, second_shift, query_bias.reshape(-1), value_bias.reshape(-1)]
    )
    small = lax.all_gather(small.reshape(1, -1), "dp", axis=0, tiled=True)
    part = model // n
    gain_one, shift_one, gain_two, shift_two = (
        small[:, i * part : (i + 1) * part].reshape(model).astype(f32) for i in range(4)
    )
    per = HD // n
    biases = small[:, 4 * part :].reshape(n, 2, heads, per).transpose(1, 2, 0, 3).reshape(2, width).astype(f32)
    bias_key = jnp.pad(key_bias.astype(f32), ((0, 0), (0, HD - ROT))).reshape(-1)
    bias_lin = jnp.concatenate([biases[0], bias_key, biases[1]])

    qkv, marks = ring.gather(jnp.concatenate([query_weight, key_weight, value_weight], axis=1), pieces=2)
    out_t, _ = ring.gather(out_weight.T, after=marks[-2])
    gate, marks = ring.gather(gate_weight, after=marks[-2])
    up, marks = ring.gather(up_weight, pieces=2, after=marks[-2])
    down_t, _ = ring.gather(down_weight.T, pieces=2, after=marks[-2])

    hat_full, _ = norm_forward(x_full.astype(f32))
    normed = (hat_full * gain_one + shift_one).astype(bf16)

    lin = dot(qkv, normed, ((0,), (1,))) + bias_lin[:, None]
    freqs = jnp.exp(-(2.0 / ROT) * jnp.arange(HALF).astype(f32) * math.log(10000.0))
    angles = freqs[:, None] * positions.astype(f32)[None, :]
    cosine, sine = jnp.cos(angles), jnp.sin(angles)
    index = jnp.arange(segments.shape[0], dtype=jnp.int32)
    allowed = (index[:, None] <= index[None, :]) & (segments[:, None] == segments[None, :])
    bias = jnp.where(allowed, 0.0, NEG).astype(f32)
    mixed, q_rot, k_rot, v_heads, logs = attend_forward(lin, cosine, sine, bias)
    rows = layer_input.astype(f32)
    attended = rows + tensor_scatter(dot(mixed, out_t, ((1,), (1,))))

    hat_two, rstd_two = norm_forward(attended)
    second = tensor_gather((hat_two * gain_two + shift_two).astype(bf16))
    gate_lin = dot(second, gate, ((1,), (0,)))
    up_lin = dot(second, up, ((1,), (0,)))
    sigma = jax.nn.sigmoid(gate_lin)
    activated = gate_lin * sigma
    hidden = (activated * up_lin).astype(bf16)
    layer_output = (attended + tensor_scatter(dot(hidden, down_t, ((1,), (1,))))).astype(bf16)

    down_grad = dot(g_full, hidden, ((0,), (0,)))
    grad_hidden = dot(g_full, down_t, ((1,), (0,)))
    grad_gate = (grad_hidden * up_lin * sigma * (1.0 + gate_lin * (1.0 - sigma))).astype(bf16)
    grad_up = (grad_hidden * activated).astype(bf16)
    grad_second = tensor_scatter(dot(grad_gate, gate, ((1,), (1,))) + dot(grad_up, up, ((1,), (1,))))
    gate_grad = dot(second, grad_gate, ((0,), (0,)))
    up_grad = dot(second, grad_up, ((0,), (0,)))
    down_sum = ring.scatter(down_grad).T
    gate_sum = ring.scatter(gate_grad)
    up_sum = ring.scatter(up_grad)
    grad_attended = out_grad.astype(f32) + norm_backward(grad_second, hat_two, rstd_two, gain_two)
    residual = tensor_gather(grad_attended.astype(bf16))

    grad_mixed = dot(out_t, residual, ((0,), (1,))).astype(bf16)
    out_grad_t = dot(residual, mixed, ((0,), (0,)))
    out_sum = ring.scatter(out_grad_t).T
    dq, dk, dv, sums = attend_backward(q_rot, k_rot, v_heads, grad_mixed, logs, cosine, sine, bias)
    grad_lin = jnp.concatenate([dq, dk, dv], axis=0)
    qkv_grad = dot(normed, grad_lin, ((0,), (1,)))
    qkv_sum = ring.scatter(qkv_grad, pieces=2)
    grad_first = tensor_scatter(dot(grad_lin, qkv, ((0,), (1,))))
    hat_one, rstd_one = norm_forward(rows)
    input_grad = grad_attended + norm_backward(grad_first, hat_one, rstd_one, gain_one)

    vectors = jnp.stack(
        [
            jnp.sum(grad_first * hat_one, axis=0),
            jnp.sum(grad_first, axis=0),
            jnp.sum(grad_second * hat_two, axis=0),
            jnp.sum(grad_second, axis=0),
        ]
    )
    vectors = sum_all(vectors, ["tensor"])
    sums = sums.reshape(width, 128)[:, :3]
    packed = sum_all(jnp.concatenate([vectors.reshape(-1), sums.reshape(-1)]), ["dp"])
    each = model // (n * lax.axis_size("tensor"))
    at = ring.me * lax.axis_size("tensor") + lax.axis_index("tensor")
    vectors = lax.dynamic_slice(packed[: 4 * model].reshape(4, -1, each), (0, at, 0), (4, 1, each))[:, 0]
    sums = packed[4 * model :].reshape(heads, n, per, 3)
    mine = lax.dynamic_slice(sums, (0, ring.me, 0, 0), (heads, 1, per, 3))[:, 0]
    key_sum = sums[..., 1].reshape(heads, HD)[:, :ROT]

    return (
        layer_output,
        input_grad,
        vectors[0],
        vectors[1],
        qkv_sum[:, :width],
        qkv_sum[:, width : 2 * width],
        qkv_sum[:, 2 * width :],
        mine[..., 0],
        key_sum,
        mine[..., 2],
        out_sum,
        vectors[2],
        vectors[3],
        gate_sum,
        up_sum,
        down_sum,
    )


def solution(mesh):
    both = ("dp", "tensor")
    return jax.shard_map(
        local,
        mesh=mesh,
        in_specs=(
            P(both, None),
            P("dp"),
            P("dp"),
            P("dp"),
            P("dp"),
            P("dp", "tensor"),
            P("dp", "tensor"),
            P("dp", "tensor"),
            P("tensor", "dp"),
            P("tensor", None),
            P("tensor", "dp"),
            P("tensor", "dp"),
            P("dp"),
            P("dp"),
            P("dp", "tensor"),
            P("dp", "tensor"),
            P("tensor", "dp"),
            P(both, None),
        ),
        out_specs=(
            P(both, None),
            P(both, None),
            P(both),
            P(both),
            P("dp", "tensor"),
            P("dp", "tensor"),
            P("dp", "tensor"),
            P("tensor", "dp"),
            P("tensor", None),
            P("tensor", "dp"),
            P("tensor", "dp"),
            P(both),
            P(both),
            P("dp", "tensor"),
            P("dp", "tensor"),
            P("tensor", "dp"),
        ),
        check_vma=False,
    )
```

time: 2130 us -> 1030 us (0.48)
  waiting for transfers between devices: 1460 us -> 349 us
  starting transfers between devices: 1.14 us -> 231 us
  matrix products: 328 us -> 137 us
  blocking collectives: 205 us -> 30.9 us
  local copies, waits for them, and re-layouts: 69 us -> 147 us
  Pallas kernels: 0 us -> 45 us
  other arithmetic: 40.7 us -> 78 us
    reduce_scatter x11 -> x0, waiting for transfers between devices: 1010 us -> none  [the longest x1 196 us: local(): lax.psum_scatter(up_grad, 'dp', scatter_dimension=0, tiled=True)]
    all_gather x11 -> x0, waiting for transfers between devices: 445 us -> none  [the longest x1 95.9 us: local(): lax.all_gather(down_weight, 'dp', axis=1, tiled=True)]
    ppermute x0 -> x225, waiting for transfers between devices: none -> 349 us  [the longest x112 201 us: gather(): block = lax.ppermute(block, 'dp', self.down if way else self.up)]
    ppermute x0 -> x225, starting transfers between devices: none -> 231 us  [the longest x112 126 us: gather(): block = lax.ppermute(block, 'dp', self.down if way else self.up)]
    dot_general x35 -> x15, matrix products: 328 us -> 137 us  [dot(): lax.dot_general(a, b, ((dims[0], dims[1]), ((), ())), preferred_element_t...]
    all_gather x6 -> x1, blocking collectives: 125 us -> 30.9 us  [local(): small = lax.all_gather(small.reshape(1, -1), 'dp', axis=0, tiled=True)]
    unnamed x2 -> x0, blocking collectives: 79.5 us -> none
    pallas_call x0 -> x2, Pallas kernels: none -> 45 us  [the longest x1 23 us: attend_backward(): pl.pallas_call(backward_kernel, grid=(count,), in_specs=[block] * 4 + [pl...]
  transfers between devices with their start and end apart: 22 -> 225, of which waited for: 19 -> 127; matrix products, arithmetic and copies ran while one was open for 8% -> 29% of each run, Pallas kernels for 0% -> 4%
where the time goes in v1:
time: 1030 us; the launch traced here: 1020 us
  waiting for transfers between devices  349 us (34%)
  starting transfers between devices  231 us (22%)
  local copies, waits for them, and re-layouts  147 us (14%)
  matrix products  137 us (13%)
  other arithmetic  78 us (8%)
  Pallas kernels  45 us (4%)
  blocking collectives  30.9 us (3%)
    ppermute x112, waiting for transfers between devices, gather(): block = lax.ppermute(block, 'dp', self.down if way else self.up)  201 us
    dot_general x15, matrix products, dot(): lax.dot_general(a, b, ((dims[0], dims[1]), ((), ())), preferred_element_t...  137 us
    ppermute x112, starting transfers between devices, gather(): block = lax.ppermute(block, 'dp', self.down if way else self.up)  126 us
    ppermute x84, waiting for transfers between devices, scatter(): got = lax.ppermute(moving.astype(bf16), 'dp', self.down if way else self.up)  119 us
    ppermute x84, starting transfers between devices, scatter(): got = lax.ppermute(moving.astype(bf16), 'dp', self.down if way else self.up)  84 us
    dynamic_update_slice x113, local copies, waits for them, and re-layouts, gather(): full = lax.dynamic_update_slice(full, block[None], (whose, base, 0))  46.4 us
    all_gather x1, blocking collectives, local(): small = lax.all_gather(small.reshape(1, -1), 'dp', axis=0, tiled=True)  30.9 us
    dot_general x5, local copies, waits for them, and re-layouts, dot(): lax.dot_general(a, b, ((dims[0], dims[1]), ((), ())), preferred_element_t...  30.4 us
  transfers between devices with their start and end apart: 225, of which 127 were waited for; matrix products, arithmetic and copies ran while one was open for 29% of the time, Pallas kernels for 4%

profile of v1, /device:TPU:0, one launch (start us, length us, event | category | flops | bytes accessed | tf_op | source)
XLA Modules:
  0.0 1020.7 jit_solution(17442954554923563113)
XLA Ops:
  13.8 30.9 %all-gather.1 = bf16[8,1,1152]{2,1,0:T(2,128)(2,1)S(1)} all-gather(bf16[1,1,1152]{2,1,0:T(2,128)(2,1)S(1)} %reshape.308), channel_id=2, replica_groups=mesh['dp'=8,'tensor'=4] {'dp'}, dimensions={0}, use_global_device_ids=true | all-gather | bytes 20736 | tf_op jit(solution)/shard_map/all_gather | solution.py:312
  71.9 5.0 collective-permute-done.2
  81.4 6.9 collective-permute-done.5
  90.1 4.8 collective-permute-done.6
  99.7 6.7 collective-permute-done.9
  108.2 6.0 collective-permute-done.10
  118.7 5.4 collective-permute-done.13
  134.4 5.2 collective-permute-done.17
  167.6 5.6 collective-permute-done.31
  202.1 4.8 collective-permute-done.33
  208.5 4.7 collective-permute-done.34
  261.7 6.4 copy.121
  277.3 6.4 copy.117
  283.7 12.1 %convolution_add_fusion.q_ref.k_ref.v_ref = f32[1536,1024]{1,0:T(8,128)} fusion(bf16[2048,1536]{1,0:T(8,128)(2,1)} %bitcast.29, bf16[1024,2048]{1,0:T(8,128)(2,1)} %bitcast.810, f32[1536]{0:T(1024)S(1)} %pad_maximum_fusion.4), kind=kOutput, calls=%fused_computation.14 | convolution fusion | flops 6444023808 | bytes 16783360 | tf_op jit(solution)/shard_map/dot_general | solution.py:146
  295.9 22.0 %attend_forward.1 = (bf16[1024,512]{1,0:T(8,128)(2,1)S(1)}, bf16[512,1024]{1,0:T(8,128)(2,1)S(1)}, bf16[512,1024]{1,0:T(8,128)(2,1)S(1)}, bf16[512,1024]{1,0:T(8,128)(2,1)S(1)}, f32[4,2,1024]{2,1,0:T(2,128)S(1)}) custom-call(f32[1536,1024]{1,0:T(8,128)} %convolution_add_fusion.q_ref.k_ref.v_ref, f32[1536,1024]{1,0:T(8,128)} %convolution_add_fusion.q_ref.k_ref.v_ref, ...), custom_call_target="tpu_custom_call" | custom-call | flops 2147483648 | bytes 31457280 | tf_op jit(solution)/shard_map/attend_forward/pallas_call | solution.py:185
  337.0 5.0 collective-permute-done.57
  346.3 5.3 collective-permute-done.59
  357.1 4.8 collective-permute-done.62
  375.9 5.5 collective-permute-done.69
  387.6 4.8 collective-permute-done.71
  430.1 7.7 collective-permute-done.88
  463.3 5.5 collective-permute-done.92
  527.3 11.7 %fusion.153 = f32[1024,1408]{1,0:T(8,128)} fusion(bf16[1024,2048]{1,0:T(8,128)(2,1)} %bitcast.152, bf16[2048,1408]{1,0:T(8,128)(2,1)S(1)} %bitcast.804), kind=kOutput, calls=%fused_computation.463 | convolution fusion | flops 5905580032 | bytes 15728640 | tf_op jit(solution)/shard_map/dot_general | solution.py:146
  539.1 8.4 fusion.151
  547.6 14.3 %multiply_convert_fusion.1 = (bf16[1024,1408]{1,0:T(8,128)(2,1)}, bf16[1024,1408]{1,0:T(8,128)(2,1)}, bf16[1024,1408]{1,0:T(8,128)(2,1)}) fusion(f32[1024,1408]{1,0:T(8,128)} %fusion.153, f32[1024,1408]{1,0:T(8,128)} %fusion.151, bf16[1024,2048]{1,0:T(8,128)(2,1)S(1)} %bitcast.792, bf16[2048,1408]{1,0:T(8,128)(2,1)S(1)} %bitcast.798), kind=kOutput, calls=%fused_computation.10 | convolution fusion | flops 5927206912 | bytes 30146560 | tf_op jit(solution)/shard_map/dot_general | solution.py:146
  561.9 8.6 fusion.12
  577.7 6.4 copy.120
  584.1 11.7 %fusion.154 = f32[1024,2048]{1,0:T(8,128)} fusion(bf16[1024,1408]{1,0:T(8,128)(2,1)} %get-tuple-element.206, bf16[2048,1408]{1,0:T(8,128)(2,1)} %bitcast.803), kind=kOutput, calls=%fused_computation.464 | convolution fusion | flops 5905580032 | bytes 17039360 | tf_op jit(solution)/shard_map/dot_general | solution.py:146
  595.8 6.7 fusion.14
  605.6 10.4 %fusion.16 = f32[8,256,1408]{2,1,0:T(8,128)S(1)} fusion(bf16[8,256,1024]{2,1,0:T(8,128)(2,1)} %bitcast.813, bf16[1024,1408]{1,0:T(8,128)(2,1)} %get-tuple-element.205), kind=kOutput, calls=%fused_computation.29 | convolution fusion | flops 5905580032 | bytes 18612224 | tf_op jit(solution)/shard_map/dot_general | solution.py:146
  619.4 12.1 %convolution_add_fusion.1 = f32[1024,2048]{1,0:T(8,128)} fusion(f32[1024,2048]{1,0:T(8,128)} %fusion.154, bf16[1024,1408]{1,0:T(8,128)(2,1)} %get-tuple-element.205, bf16[2048,1408]{1,0:T(8,128)(2,1)S(1)} %bitcast.801), kind=kOutput, calls=%fused_computation.19 | convolution fusion | flops 5907677184 | bytes 25427968 | tf_op jit(solution)/shard_map/dot_general | solution.py:146
  631.6 9.7 fusion.152
  651.7 6.0 collective-permute-done.212
  661.6 5.7 collective-permute-done.198
  670.8 5.1 collective-permute-done.184
  680.9 6.4 collective-permute-done.213
  704.9 5.5 collective-permute-done.214
  728.1 5.5 collective-permute-done.215
  749.4 5.4 collective-permute-done.194
  761.7 19.9 %collective-permute-done.129 = bf16[256,2048]{1,0:T(8,128)(2,1)S(1)} collective-permute-done((bf16[256,2048]{1,0:T(8,128)(2,1)S(1)}, bf16[256,2048]{1,0:T(8,128)(2,1)S(1)}, u32[]{:S(2)}, u32[]{:S(2)}) %collective-permute-start.129) | collective-permute-done | bytes 1048608 | tf_op jit(solution)/shard_map/ppermute | solution.py:121
  784.4 6.0 multiply_reduce_fusion
  834.1 6.4 copy.125
  840.5 4.7 fusion.47
  847.3 5.6 convolution_convert_fusion.d_ref
  852.9 23.0 %attend_backward.1 = (bf16[512,1024]{1,0:T(8,128)(2,1)S(1)}, bf16[512,1024]{1,0:T(8,128)(2,1)S(1)}, bf16[512,1024]{1,0:T(8,128)(2,1)S(1)}, f32[4,128,128]{2,1,0:T(8,128)S(1)}) custom-call(bf16[512,1024]{1,0:T(8,128)(2,1)S(1)} %get-tuple-element.36.q_ref, bf16[512,1024]{1,0:T(8,128)(2,1)S(1)} %get-tuple-element.37.k_ref, bf16[512,1024]{1,0:T(8,128)(2,1)} %copy-done.4, ...), custom_call_target="tpu_custom_call" | custom-call | flops 5368709120 | bytes 31457280 | tf_op jit(solution)/shard_map/attend_backward/pallas_call | solution.py:249
  879.3 7.0 fusion.10
  893.6 4.8 copy.124
  898.4 9.9 fusion.155
  (831 shorter events, 619.7 us)
Async XLA Ops:
  0.6 147.0 %collective-permute-start.28 = (bf16[256,2048]{1,0:T(8,128)(2,1)}, bf16[256,2048]{1,0:T(8,128)(2,1)}, u32[]{:S(2)}, u32[]{:S(2)}) collective-permute-start(bf16[256,2048]{1,0:T(8,128)(2,1)} %param.18), channel_id=1, source_target_pairs={{0,1},{1,0},{2,3},{3,2},{4,5},{5,4},{6,7},{7,6},{8,9},{9,8},{10,11... | collective-permute-start | bytes 3145736 | tf_op jit(solution)/shard_map/ppermute | solution.py:101
  1.2 153.2 %collective-permute-start.29 = (bf16[256,2048]{1,0:T(8,128)(2,1)}, bf16[256,2048]{1,0:T(8,128)(2,1)}, u32[]{:S(2)}, u32[]{:S(2)}) collective-permute-start(bf16[256,2048]{1,0:T(8,128)(2,1)} %param.18), channel_id=1, source_target_pairs={{0,2},{2,0},{1,3},{3,1},{4,6},{6,4},{5,7},{7,5},{8,10},{10,8},{9,1... | collective-permute-start | bytes 3145736 | tf_op jit(solution)/shard_map/ppermute | solution.py:100
  7.5 64.4 %collective-permute-start.3 = (bf16[64,1536]{1,0:T(8,128)(2,1)S(1)}, bf16[64,1536]{1,0:T(8,128)(2,1)}, u32[]{:S(2)}, u32[]{:S(2)}) collective-permute-start(bf16[64,1536]{1,0:T(8,128)(2,1)S(1)} %get-tuple-element.237), channel_id=1, source_target_pairs={{8,0},{16,8},{24,16},{28,24},{20,28},{12,20},{4,12},{0,4},{9,1},{1... | collective-permute-start | bytes 589832 | tf_op jit(solution)/shard_map/ppermute | solution.py:59
  9.0 56.5 %collective-permute-start = (bf16[64,1536]{1,0:T(8,128)(2,1)}, bf16[64,1536]{1,0:T(8,128)(2,1)}, u32[]{:S(2)}, u32[]{:S(2)}) collective-permute-start(bf16[64,1536]{1,0:T(8,128)(2,1)} %get-tuple-element.240), channel_id=1, source_target_pairs={{0,8},{8,16},{16,24},{24,28},{28,20},{20,12},{12,4},{4,0},{1,9},{9... | collective-permute-start | bytes 589832 | tf_op jit(solution)/shard_map/ppermute | solution.py:59
  9.5 141.6 %collective-permute-start.124 = (bf16[256,2048]{1,0:T(8,128)(2,1)}, bf16[256,2048]{1,0:T(8,128)(2,1)}, u32[]{:S(2)}, u32[]{:S(2)}) collective-permute-start(bf16[256,2048]{1,0:T(8,128)(2,1)} %param.35), channel_id=1, source_target_pairs={{0,1},{1,0},{2,3},{3,2},{4,5},{5,4},{6,7},{7,6},{8,9},{9,8},{10,11... | collective-permute-start | bytes 3145736 | tf_op jit(solution)/shard_map/ppermute | solution.py:101
  157.8 94.2 %collective-permute-start.30 = (bf16[256,2048]{1,0:T(8,128)(2,1)}, bf16[256,2048]{1,0:T(8,128)(2,1)S(1)}, u32[]{:S(2)}, u32[]{:S(2)}) collective-permute-start(bf16[256,2048]{1,0:T(8,128)(2,1)} %collective-permute-done.29), channel_id=1, source_target_pairs={{0,1},{1,0},{2,3},{3,2},{4,5},{5,4},{6,7},{7,6},{8,9},{9,8},{10,11... | collective-permute-start | bytes 3145736 | tf_op jit(solution)/shard_map/ppermute | solution.py:102
  158.9 101.7 %collective-permute-start.126 = (bf16[256,2048]{1,0:T(8,128)(2,1)S(1)}, bf16[256,2048]{1,0:T(8,128)(2,1)S(1)}, u32[]{:S(2)}, u32[]{:S(2)}) collective-permute-start(bf16[256,2048]{1,0:T(8,128)(2,1)S(1)} %collective-permute-done.125), channel_id=1, source_target_pairs={{0,1},{1,0},{2,3},{3,2},{4,5},{5,4},{6,7},{7,6},{8,9},{9,8},{10,11... | collective-permute-start | bytes 3145736 | tf_op jit(solution)/shard_map/ppermute | solution.py:102
  159.9 54.5 %collective-permute-start.51 = (bf16[128,1408]{1,0:T(8,128)(2,1)S(1)}, bf16[128,1408]{1,0:T(8,128)(2,1)S(1)}, u32[]{:S(2)}, u32[]{:S(2)}) collective-permute-start(bf16[128,1408]{1,0:T(8,128)(2,1)S(1)} %get-tuple-element.245), channel_id=1, source_target_pairs={{0,8},{8,16},{16,24},{24,28},{28,20},{20,12},{12,4},{4,0},{1,9},{9... | collective-permute-start | bytes 1081352 | tf_op jit(solution)/shard_map/ppermute | solution.py:59
  161.3 54.7 %collective-permute-start.52 = (bf16[128,1408]{1,0:T(8,128)(2,1)S(1)}, bf16[128,1408]{1,0:T(8,128)(2,1)S(1)}, u32[]{:S(2)}, u32[]{:S(2)}) collective-permute-start(bf16[128,1408]{1,0:T(8,128)(2,1)S(1)} %get-tuple-element.246), channel_id=1, source_target_pairs={{8,0},{16,8},{24,16},{28,24},{20,28},{12,20},{4,12},{0,4},{9,1},{1... | collective-permute-start | bytes 1081352 | tf_op jit(solution)/shard_map/ppermute | solution.py:59
  215.9 28.4 %collective-permute-start.53 = (bf16[128,1408]{1,0:T(8,128)(2,1)S(1)}, bf16[128,1408]{1,0:T(8,128)(2,1)}, u32[]{:S(2)}, u32[]{:S(2)}) collective-permute-start(bf16[128,1408]{1,0:T(8,128)(2,1)S(1)} %collective-permute-done.51), channel_id=1, source_target_pairs={{0,8},{8,16},{16,24},{24,28},{28,20},{20,12},{12,4},{4,0},{1,9},{9... | collective-permute-start | bytes 1081352 | tf_op jit(solution)/shard_map/ppermute | solution.py:59
  218.2 27.9 %collective-permute-start.54 = (bf16[128,1408]{1,0:T(8,128)(2,1)S(1)}, bf16[128,1408]{1,0:T(8,128)(2,1)}, u32[]{:S(2)}, u32[]{:S(2)}) collective-permute-start(bf16[128,1408]{1,0:T(8,128)(2,1)S(1)} %collective-permute-done.52), channel_id=1, source_target_pairs={{8,0},{16,8},{24,16},{28,24},{20,28},{12,20},{4,12},{0,4},{9,1},{1... | collective-permute-start | bytes 1081352 | tf_op jit(solution)/shard_map/ppermute | solution.py:59
  246.1 85.3 %collective-permute-start.55 = (bf16[128,1408]{1,0:T(8,128)(2,1)}, bf16[128,1408]{1,0:T(8,128)(2,1)}, u32[]{:S(2)}, u32[]{:S(2)}) collective-permute-start(bf16[128,1408]{1,0:T(8,128)(2,1)} %collective-permute-done.53), channel_id=1, source_target_pairs={{0,8},{8,16},{16,24},{24,28},{28,20},{20,12},{12,4},{4,0},{1,9},{9... | collective-permute-start | bytes 1081352 | tf_op jit(solution)/shard_map/ppermute | solution.py:59
  248.5 85.5 %collective-permute-start.56 = (bf16[128,1408]{1,0:T(8,128)(2,1)}, bf16[128,1408]{1,0:T(8,128)(2,1)}, u32[]{:S(2)}, u32[]{:S(2)}) collective-permute-start(bf16[128,1408]{1,0:T(8,128)(2,1)} %collective-permute-done.54), channel_id=1, source_target_pairs={{8,0},{16,8},{24,16},{28,24},{20,28},{12,20},{4,12},{0,4},{9,1},{1... | collective-permute-start | bytes 1081352 | tf_op jit(solution)/shard_map/ppermute | solution.py:59
  250.4 68.4 %collective-permute-start.43 = (bf16[128,512]{0,1:T(8,128)(2,1)S(1)}, bf16[128,512]{0,1:T(8,128)(2,1)}, u32[]{:S(2)}, u32[]{:S(2)}) collective-permute-start(bf16[128,512]{0,1:T(8,128)(2,1)S(1)} %collective-permute-done.41), channel_id=1, source_target_pairs={{0,8},{8,16},{16,24},{24,28},{28,20},{20,12},{12,4},{4,0},{1,9},{9... | collective-permute-start | bytes 393224 | tf_op jit(solution)/shard_map/ppermute | solution.py:59
  251.9 72.9 %collective-permute-start.44 = (bf16[128,512]{0,1:T(8,128)(2,1)S(1)}, bf16[128,512]{0,1:T(8,128)(2,1)}, u32[]{:S(2)}, u32[]{:S(2)}) collective-permute-start(bf16[128,512]{0,1:T(8,128)(2,1)S(1)} %collective-permute-done.42), channel_id=1, source_target_pairs={{8,0},{16,8},{24,16},{28,24},{20,28},{12,20},{4,12},{0,4},{9,1},{1... | collective-permute-start | bytes 393224 | tf_op jit(solution)/shard_map/ppermute | solution.py:59
  330.8 25.5 %collective-permute-start.46 = (bf16[256,2048]{1,0:T(8,128)(2,1)S(1)}, bf16[256,2048]{1,0:T(8,128)(2,1)S(1)}, u32[]{:S(2)}, u32[]{:S(2)}) collective-permute-start(bf16[256,2048]{1,0:T(8,128)(2,1)S(1)} %get-tuple-element.215), channel_id=1, source_target_pairs={{0,1},{1,0},{2,3},{3,2},{4,5},{5,4},{6,7},{7,6},{8,9},{9,8},{10,11... | collective-permute-start | bytes 3145736 | tf_op jit(solution)/shard_map/ppermute | solution.py:119
  330.9 90.7 %collective-permute-start.45 = (bf16[256,2048]{1,0:T(8,128)(2,1)S(1)}, bf16[256,2048]{1,0:T(8,128)(2,1)S(1)}, u32[]{:S(2)}, u32[]{:S(2)}) collective-permute-start(bf16[256,2048]{1,0:T(8,128)(2,1)S(1)} %get-tuple-element.214), channel_id=1, source_target_pairs={{0,1},{1,0},{2,3},{3,2},{4,5},{5,4},{6,7},{7,6},{8,9},{9,8},{10,11... | collective-permute-start | bytes 3145736 | tf_op jit(solution)/shard_map/ppermute | solution.py:120
  356.6 66.4 %collective-permute-start.47 = (bf16[256,2048]{1,0:T(8,128)(2,1)S(1)}, bf16[256,2048]{1,0:T(8,128)(2,1)S(1)}, u32[]{:S(2)}, u32[]{:S(2)}) collective-permute-start(bf16[256,2048]{1,0:T(8,128)(2,1)S(1)} %fusion.37), channel_id=1, source_target_pairs={{0,2},{2,0},{1,3},{3,1},{4,6},{6,4},{5,7},{7,5},{8,10},{10,8},{9,1... | collective-permute-start | bytes 3145736 | tf_op jit(solution)/shard_map/ppermute | solution.py:121
  369.9 30.6 %collective-permute-start.63 = (bf16[128,1408]{1,0:T(8,128)(2,1)S(1)}, bf16[128,1408]{1,0:T(8,128)(2,1)S(1)}, u32[]{:S(2)}, u32[]{:S(2)}) collective-permute-start(bf16[128,1408]{1,0:T(8,128)(2,1)S(1)} %collective-permute-done.61), channel_id=1, source_target_pairs={{0,8},{8,16},{16,24},{24,28},{28,20},{20,12},{12,4},{4,0},{1,9},{9... | collective-permute-start | bytes 1081352 | tf_op jit(solution)/shard_map/ppermute | solution.py:59
  372.0 28.6 %collective-permute-start.64 = (bf16[128,1408]{1,0:T(8,128)(2,1)S(1)}, bf16[128,1408]{1,0:T(8,128)(2,1)S(1)}, u32[]{:S(2)}, u32[]{:S(2)}) collective-permute-start(bf16[128,1408]{1,0:T(8,128)(2,1)S(1)} %collective-permute-done.62), channel_id=1, source_target_pairs={{8,0},{16,8},{24,16},{28,24},{20,28},{12,20},{4,12},{0,4},{9,1},{1... | collective-permute-start | bytes 1081352 | tf_op jit(solution)/shard_map/ppermute | solution.py:59
  425.3 81.0 %collective-permute-start.48 = (bf16[256,2048]{1,0:T(8,128)(2,1)S(1)}, bf16[256,2048]{1,0:T(8,128)(2,1)S(1)}, u32[]{:S(2)}, u32[]{:S(2)}) collective-permute-start(bf16[256,2048]{1,0:T(8,128)(2,1)S(1)} %get-tuple-element.122), channel_id=1, source_target_pairs={{0,1},{1,0},{2,3},{3,2},{4,5},{5,4},{6,7},{7,6},{8,9},{9,8},{10,11... | collective-permute-start | bytes 3145736 | tf_op jit(solution)/shard_map/ppermute | solution.py:101
  426.0 80.4 %collective-permute-start.49 = (bf16[256,2048]{1,0:T(8,128)(2,1)S(1)}, bf16[256,2048]{1,0:T(8,128)(2,1)S(1)}, u32[]{:S(2)}, u32[]{:S(2)}) collective-permute-start(bf16[256,2048]{1,0:T(8,128)(2,1)S(1)} %get-tuple-element.122), channel_id=1, source_target_pairs={{0,2},{2,0},{1,3},{3,1},{4,6},{6,4},{5,7},{7,5},{8,10},{10,8},{9,1... | collective-permute-start | bytes 3145736 | tf_op jit(solution)/shard_map/ppermute | solution.py:100
  440.1 30.8 %collective-permute-start.93 = (bf16[64,1408]{1,0:T(8,128)(2,1)S(1)}, bf16[64,1408]{1,0:T(8,128)(2,1)S(1)}, u32[]{:S(2)}, u32[]{:S(2)}) collective-permute-start(bf16[64,1408]{1,0:T(8,128)(2,1)S(1)} %get-tuple-element.244), channel_id=1, source_target_pairs={{0,8},{8,16},{16,24},{24,28},{28,20},{20,12},{12,4},{4,0},{1,9},{9... | collective-permute-start | bytes 540680 | tf_op jit(solution)/shard_map/ppermute | solution.py:59
  441.3 29.7 %collective-permute-start.94 = (bf16[64,1408]{1,0:T(8,128)(2,1)S(1)}, bf16[64,1408]{1,0:T(8,128)(2,1)S(1)}, u32[]{:S(2)}, u32[]{:S(2)}) collective-permute-start(bf16[64,1408]{1,0:T(8,128)(2,1)S(1)} %get-tuple-element.243), channel_id=1, source_target_pairs={{8,0},{16,8},{24,16},{28,24},{20,28},{12,20},{4,12},{0,4},{9,1},{1... | collective-permute-start | bytes 540680 | tf_op jit(solution)/shard_map/ppermute | solution.py:59
  506.4 32.6 %collective-permute-start.50 = (bf16[256,2048]{1,0:T(8,128)(2,1)S(1)}, bf16[256,2048]{1,0:T(8,128)(2,1)S(1)}, u32[]{:S(2)}, u32[]{:S(2)}) collective-permute-start(bf16[256,2048]{1,0:T(8,128)(2,1)S(1)} %collective-permute-done.49), channel_id=1, source_target_pairs={{0,1},{1,0},{2,3},{3,2},{4,5},{5,4},{6,7},{7,6},{8,9},{9,8},{10,11... | collective-permute-start | bytes 3145736 | tf_op jit(solution)/shard_map/ppermute | solution.py:102
  575.7 66.3 %collective-permute-start.211 = (bf16[128,1408]{1,0:T(8,128)(2,1)}, bf16[128,1408]{1,0:T(8,128)(2,1)S(1)}, u32[]{:S(2)}, u32[]{:S(2)}) collective-permute-start(bf16[128,1408]{1,0:T(8,128)(2,1)} %get-tuple-element.171), channel_id=1, source_target_pairs={{0,8},{8,16},{16,24},{24,28},{28,20},{20,12},{12,4},{4,0},{1,9},{9... | collective-permute-start | bytes 1081352 | tf_op jit(solution)/shard_map/ppermute | solution.py:84
  577.7 64.4 %collective-permute-start.218 = (bf16[128,1408]{1,0:T(8,128)(2,1)}, bf16[128,1408]{1,0:T(8,128)(2,1)}, u32[]{:S(2)}, u32[]{:S(2)}) collective-permute-start(bf16[128,1408]{1,0:T(8,128)(2,1)} %get-tuple-element.172), channel_id=1, source_target_pairs={{8,0},{16,8},{24,16},{28,24},{20,28},{12,20},{4,12},{0,4},{9,1},{1... | collective-permute-start | bytes 1081352 | tf_op jit(solution)/shard_map/ppermute | solution.py:84
  603.6 41.5 %collective-permute-start.197 = (bf16[128,1408]{1,0:T(8,128)(2,1)}, bf16[128,1408]{1,0:T(8,128)(2,1)S(1)}, u32[]{:S(2)}, u32[]{:S(2)}) collective-permute-start(bf16[128,1408]{1,0:T(8,128)(2,1)} %get-tuple-element.187), channel_id=1, source_target_pairs={{0,8},{8,16},{16,24},{24,28},{28,20},{20,12},{12,4},{4,0},{1,9},{9... | collective-permute-start | bytes 1081352 | tf_op jit(solution)/shard_map/ppermute | solution.py:84
  605.6 39.6 %collective-permute-start.204 = (bf16[128,1408]{1,0:T(8,128)(2,1)}, bf16[128,1408]{1,0:T(8,128)(2,1)}, u32[]{:S(2)}, u32[]{:S(2)}) collective-permute-start(bf16[128,1408]{1,0:T(8,128)(2,1)} %get-tuple-element.188), channel_id=1, source_target_pairs={{8,0},{16,8},{24,16},{28,24},{20,28},{12,20},{4,12},{0,4},{9,1},{1... | collective-permute-start | bytes 1081352 | tf_op jit(solution)/shard_map/ppermute | solution.py:84
  616.8 30.4 %collective-permute-start.183 = (bf16[128,1408]{1,0:T(8,128)(2,1)}, bf16[128,1408]{1,0:T(8,128)(2,1)S(1)}, u32[]{:S(2)}, u32[]{:S(2)}) collective-permute-start(bf16[128,1408]{1,0:T(8,128)(2,1)} %get-tuple-element.203), channel_id=1, source_target_pairs={{0,8},{8,16},{16,24},{24,28},{28,20},{20,12},{12,4},{4,0},{1,9},{9... | collective-permute-start | bytes 1081352 | tf_op jit(solution)/shard_map/ppermute | solution.py:84
  642.1 36.0 %collective-permute-start.122 = (bf16[256,2048]{1,0:T(8,128)(2,1)S(1)}, bf16[256,2048]{1,0:T(8,128)(2,1)S(1)}, u32[]{:S(2)}, u32[]{:S(2)}) collective-permute-start(bf16[256,2048]{1,0:T(8,128)(2,1)S(1)} %get-tuple-element.213), channel_id=1, source_target_pairs={{0,1},{1,0},{2,3},{3,2},{4,5},{5,4},{6,7},{7,6},{8,9},{9,8},{10,11... | collective-permute-start | bytes 3145736 | tf_op jit(solution)/shard_map/ppermute | solution.py:119
  645.1 113.1 %collective-permute-start.121 = (bf16[256,2048]{1,0:T(8,128)(2,1)S(1)}, bf16[256,2048]{1,0:T(8,128)(2,1)S(1)}, u32[]{:S(2)}, u32[]{:S(2)}) collective-permute-start(bf16[256,2048]{1,0:T(8,128)(2,1)S(1)} %get-tuple-element.212), channel_id=1, source_target_pairs={{0,1},{1,0},{2,3},{3,2},{4,5},{5,4},{6,7},{7,6},{8,9},{9,8},{10,11... | collective-permute-start | bytes 3145736 | tf_op jit(solution)/shard_map/ppermute | solution.py:120
  645.2 34.9 %collective-permute-start.128 = (bf16[256,2048]{1,0:T(8,128)(2,1)S(1)}, bf16[256,2048]{1,0:T(8,128)(2,1)S(1)}, u32[]{:S(2)}, u32[]{:S(2)}) collective-permute-start(bf16[256,2048]{1,0:T(8,128)(2,1)S(1)} %get-tuple-element.211), channel_id=1, source_target_pairs={{0,1},{1,0},{2,3},{3,2},{4,5},{5,4},{6,7},{7,6},{8,9},{9,8},{10,11... | collective-permute-start | bytes 3145736 | tf_op jit(solution)/shard_map/ppermute | solution.py:119
  733.6 24.7 %collective-permute-start.127 = (bf16[256,2048]{1,0:T(8,128)(2,1)S(1)}, bf16[256,2048]{1,0:T(8,128)(2,1)S(1)}, u32[]{:S(2)}, u32[]{:S(2)}) collective-permute-start(bf16[256,2048]{1,0:T(8,128)(2,1)S(1)} %get-tuple-element.210), channel_id=1, source_target_pairs={{0,1},{1,0},{2,3},{3,2},{4,5},{5,4},{6,7},{7,6},{8,9},{9,8},{10,11... | collective-permute-start | bytes 3145736 | tf_op jit(solution)/shard_map/ppermute | solution.py:120
  735.2 26.1 %collective-permute-start.123 = (bf16[256,2048]{1,0:T(8,128)(2,1)S(1)}, bf16[256,2048]{1,0:T(8,128)(2,1)S(1)}, u32[]{:S(2)}, u32[]{:S(2)}) collective-permute-start(bf16[256,2048]{1,0:T(8,128)(2,1)S(1)} %fusion.33), channel_id=1, source_target_pairs={{0,2},{2,0},{1,3},{3,1},{4,6},{6,4},{5,7},{7,5},{8,10},{10,8},{9,1... | collective-permute-start | bytes 3145736 | tf_op jit(solution)/shard_map/ppermute | solution.py:121
  737.7 44.0 %collective-permute-start.129 = (bf16[256,2048]{1,0:T(8,128)(2,1)S(1)}, bf16[256,2048]{1,0:T(8,128)(2,1)S(1)}, u32[]{:S(2)}, u32[]{:S(2)}) collective-permute-start(bf16[256,2048]{1,0:T(8,128)(2,1)S(1)} %fusion.31), channel_id=1, source_target_pairs={{0,2},{2,0},{1,3},{3,1},{4,6},{6,4},{5,7},{7,5},{8,10},{10,8},{9,1... | collective-permute-start | bytes 3145736 | tf_op jit(solution)/shard_map/ppermute | solution.py:121
  754.7 41.0 %collective-permute-start.216 = (bf16[128,1408]{1,0:T(8,128)(2,1)}, bf16[128,1408]{1,0:T(8,128)(2,1)}, u32[]{:S(2)}, u32[]{:S(2)}) collective-permute-start(bf16[128,1408]{1,0:T(8,128)(2,1)} %get-tuple-element.161), channel_id=1, source_target_pairs={{0,8},{8,16},{16,24},{24,28},{28,20},{20,12},{12,4},{4,0},{1,9},{9... | collective-permute-start | bytes 1081352 | tf_op jit(solution)/shard_map/ppermute | solution.py:84
  758.2 37.9 %collective-permute-start.223 = (bf16[128,1408]{1,0:T(8,128)(2,1)}, bf16[128,1408]{1,0:T(8,128)(2,1)}, u32[]{:S(2)}, u32[]{:S(2)}) collective-permute-start(bf16[128,1408]{1,0:T(8,128)(2,1)} %get-tuple-element.162), channel_id=1, source_target_pairs={{8,0},{16,8},{24,16},{28,24},{20,28},{12,20},{4,12},{0,4},{9,1},{1... | collective-permute-start | bytes 1081352 | tf_op jit(solution)/shard_map/ppermute | solution.py:84
  758.3 39.5 %collective-permute-start.202 = (bf16[128,1408]{1,0:T(8,128)(2,1)}, bf16[128,1408]{1,0:T(8,128)(2,1)}, u32[]{:S(2)}, u32[]{:S(2)}) collective-permute-start(bf16[128,1408]{1,0:T(8,128)(2,1)} %get-tuple-element.177), channel_id=1, source_target_pairs={{0,8},{8,16},{16,24},{24,28},{28,20},{20,12},{12,4},{4,0},{1,9},{9... | collective-permute-start | bytes 1081352 | tf_op jit(solution)/shard_map/ppermute | solution.py:84
  761.3 38.1 %collective-permute-start.209 = (bf16[128,1408]{1,0:T(8,128)(2,1)}, bf16[128,1408]{1,0:T(8,128)(2,1)}, u32[]{:S(2)}, u32[]{:S(2)}) collective-permute-start(bf16[128,1408]{1,0:T(8,128)(2,1)} %get-tuple-element.178), channel_id=1, source_target_pairs={{8,0},{16,8},{24,16},{28,24},{20,28},{12,20},{4,12},{0,4},{9,1},{1... | collective-permute-start | bytes 1081352 | tf_op jit(solution)/shard_map/ppermute | solution.py:84
  796.1 34.7 %collective-permute-start.130 = (bf16[256,2048]{1,0:T(8,128)(2,1)S(1)}, bf16[256,2048]{1,0:T(8,128)(2,1)S(1)}, u32[]{:S(2)}, u32[]{:S(2)}) collective-permute-start(bf16[256,2048]{1,0:T(8,128)(2,1)S(1)} %get-tuple-element.118), channel_id=1, source_target_pairs={{0,1},{1,0},{2,3},{3,2},{4,5},{5,4},{6,7},{7,6},{8,9},{9,8},{10,11... | collective-permute-start | bytes 3145736 | tf_op jit(solution)/shard_map/ppermute | solution.py:101
  797.8 31.8 %collective-permute-start.131 = (bf16[256,2048]{1,0:T(8,128)(2,1)S(1)}, bf16[256,2048]{1,0:T(8,128)(2,1)S(1)}, u32[]{:S(2)}, u32[]{:S(2)}) collective-permute-start(bf16[256,2048]{1,0:T(8,128)(2,1)S(1)} %get-tuple-element.118), channel_id=1, source_target_pairs={{0,2},{2,0},{1,3},{3,1},{4,6},{6,4},{5,7},{7,5},{8,10},{10,8},{9,1... | collective-permute-start | bytes 3145736 | tf_op jit(solution)/shard_map/ppermute | solution.py:100
  845.3 63.1 %collective-permute-start.169 = (bf16[128,512]{1,0:T(8,128)(2,1)S(1)}, bf16[128,512]{1,0:T(8,128)(2,1)S(1)}, u32[]{:S(2)}, u32[]{:S(2)}) collective-permute-start(bf16[128,512]{1,0:T(8,128)(2,1)S(1)} %get-tuple-element.230), channel_id=1, source_target_pairs={{0,8},{8,16},{16,24},{24,28},{28,20},{20,12},{12,4},{4,0},{1,9},{9... | collective-permute-start | bytes 393224 | tf_op jit(solution)/shard_map/ppermute | solution.py:84
  845.9 62.5 %collective-permute-start.176 = (bf16[128,512]{1,0:T(8,128)(2,1)S(1)}, bf16[128,512]{1,0:T(8,128)(2,1)S(1)}, u32[]{:S(2)}, u32[]{:S(2)}) collective-permute-start(bf16[128,512]{1,0:T(8,128)(2,1)S(1)} %get-tuple-element.231), channel_id=1, source_target_pairs={{8,0},{16,8},{24,16},{28,24},{20,28},{12,20},{4,12},{0,4},{9,1},{1... | collective-permute-start | bytes 393224 | tf_op jit(solution)/shard_map/ppermute | solution.py:84
  890.9 24.4 %collective-permute-start.141 = (bf16[64,1536]{1,0:T(8,128)(2,1)S(1)}, bf16[64,1536]{1,0:T(8,128)(2,1)S(1)}, u32[]{:S(2)}, u32[]{:S(2)}) collective-permute-start(bf16[64,1536]{1,0:T(8,128)(2,1)S(1)} %get-tuple-element.153), channel_id=1, source_target_pairs={{0,8},{8,16},{16,24},{24,28},{28,20},{20,12},{12,4},{4,0},{1,9},{9... | collective-permute-start | bytes 589832 | tf_op jit(solution)/shard_map/ppermute | solution.py:84
  893.0 24.5 %collective-permute-start.155 = (bf16[64,1536]{1,0:T(8,128)(2,1)S(1)}, bf16[64,1536]{1,0:T(8,128)(2,1)S(1)}, u32[]{:S(2)}, u32[]{:S(2)}) collective-permute-start(bf16[64,1536]{1,0:T(8,128)(2,1)S(1)} %get-tuple-element.155), channel_id=1, source_target_pairs={{0,8},{8,16},{16,24},{24,28},{28,20},{20,12},{12,4},{4,0},{1,9},{9... | collective-permute-start | bytes 589832 | tf_op jit(solution)/shard_map/ppermute | solution.py:84
  915.3 54.0 %collective-permute-start.134 = (bf16[256,2048]{1,0:T(8,128)(2,1)S(1)}, bf16[256,2048]{1,0:T(8,128)(2,1)S(1)}, u32[]{:S(2)}, u32[]{:S(2)}) collective-permute-start(bf16[256,2048]{1,0:T(8,128)(2,1)S(1)} %get-tuple-element.209), channel_id=1, source_target_pairs={{0,1},{1,0},{2,3},{3,2},{4,5},{5,4},{6,7},{7,6},{8,9},{9,8},{10,11... | collective-permute-start | bytes 3145736 | tf_op jit(solution)/shard_map/ppermute | solution.py:119
  962.5 32.2 %collective-permute-start.133 = (bf16[256,2048]{1,0:T(8,128)(2,1)S(1)}, bf16[256,2048]{1,0:T(8,128)(2,1)}, u32[]{:S(2)}, u32[]{:S(2)}) collective-permute-start(bf16[256,2048]{1,0:T(8,128)(2,1)S(1)} %get-tuple-element.208), channel_id=1, source_target_pairs={{0,1},{1,0},{2,3},{3,2},{4,5},{5,4},{6,7},{7,6},{8,9},{9,8},{10,11... | collective-permute-start | bytes 3145736 | tf_op jit(solution)/shard_map/ppermute | solution.py:120
  (241 other events, 3694.8 us)

commit v2 on v1

--- a/solution.py
+++ b/solution.py
@@ -262,6 +262,293 @@
     )(q, k, v, d, logs, cosine, sine, bias)
 
 
+MESH = pl.DeviceIdType.MESH
+HBM = pl.BlockSpec(memory_space=pl.ANY)
+VMEM = pl.BlockSpec(memory_space=pltpu.VMEM)
+DMA = pltpu.SemaphoreType.DMA
+
+
+class Place:
+    def __init__(self, n):
+        self.n = n
+        self.me = lax.axis_index("dp")
+        self.t = lax.axis_index("tensor")
+        odd = lax.rem(self.me, 2)
+        half = lax.div(self.me, 2)
+        self.pos = jnp.where(odd == 0, half, n - 1 - half)
+        self.up = self.owner(1)
+        self.down = self.owner(-1)
+        self.core = self.t + 1 - 2 * lax.rem(self.t, 2)
+        self.chip = lax.rem(self.t + 2, 4)
+        self.cross = lax.rem(self.core + 2, 4)
+
+    def owner(self, offset):
+        p = lax.rem(self.pos + (offset + 2 * self.n), self.n)
+        return jnp.where(p < self.n // 2, 2 * p, 2 * (self.n - 1 - p) + 1)
+
+    def barrier(self, dp, tensor):
+        sem = pltpu.get_barrier_semaphore()
+        for there in dp:
+            pl.semaphore_signal(sem, inc=1, device_id={"dp": there}, device_id_type=MESH)
+        for there in tensor:
+            pl.semaphore_signal(sem, inc=1, device_id={"tensor": there}, device_id_type=MESH)
+        pl.semaphore_wait(sem, len(dp) + len(tensor))
+
+
+class Lane:
+    def __init__(self, place, full, base, size, way, send, recv):
+        self.place, self.full, self.base, self.size, self.way = place, full, base, size, way
+        self.send, self.recv = send, recv
+
+    def whose(self, step):
+        return self.place.owner(step if self.way else -step)
+
+    def copy(self, step, whose):
+        piece = self.full.at[whose, pl.ds(self.base, self.size)]
+        return pltpu.make_async_remote_copy(
+            src_ref=piece,
+            dst_ref=piece,
+            send_sem=self.send.at[step - 1],
+            recv_sem=self.recv.at[step - 1],
+            device_id={"dp": self.place.down if self.way else self.place.up},
+            device_id_type=MESH,
+        )
+
+    def start(self, step):
+        self.copy(step, self.whose(step - 1)).start()
+
+    def arrive(self, step):
+        self.copy(step, self.whose(step)).wait_recv()
+
+    def finish(self):
+        for step in range(1, self.place.n):
+            self.copy(step, self.whose(step - 1)).wait_send()
+
+
+class Exchange:
+    def __init__(self, send, recv):
+        self.send, self.recv = send, recv
+
+    def copy(self, number, src, dst, there):
+        return pltpu.make_async_remote_copy(
+            src_ref=src,
+            dst_ref=dst,
+            send_sem=self.send.at[number],
+            recv_sem=self.recv.at[number],
+            device_id={"tensor": there},
+            device_id_type=MESH,
+        )
+
+
+def row_norm(value, gain, shift):
+    center = value - jnp.mean(value, axis=1, keepdims=True)
+    rstd = lax.rsqrt(jnp.mean(center * center, axis=1, keepdims=True) + EPS)
+    return center * rstd * gain + shift
+
+
+def lane_vector(full, first, count):
+    pieces = [full[d, r : r + 1, :].astype(f32) for d in range(full.shape[0]) for r in range(first, first + count)]
+    return jnp.concatenate(pieces, axis=1)
+
+
+def enter_kernel(
+    n,
+    x_ref, g_ref, wq, wk, wv, wo, small_ref,
+    normed_out, g_out, qkv_out, out_out, lin, small_full,
+    x_full, normed, left, right, outs,
+    small_send, small_recv, send, recv, x_send, x_recv, local, stored,
+):
+    place = Place(n)
+    rows = x_ref.shape[0]
+    size = wq.shape[0]
+    width = wq.shape[1]
+    half = width // 2
+    me, t = place.me, place.t
+    loads = [
+        pltpu.make_async_copy(wq, left.at[me, :, pl.ds(0, width)], local.at[0]),
+        pltpu.make_async_copy(wk.at[:, pl.ds(0, half)], left.at[me, :, pl.ds(width, half)], local.at[1]),
+        pltpu.make_async_copy(wk.at[:, pl.ds(half, half)], right.at[me, :, pl.ds(0, half)], local.at[2]),
+        pltpu.make_async_copy(wv, right.at[me, :, pl.ds(half, width)], local.at[3]),
+        pltpu.make_async_copy(x_ref, x_full.at[t], local.at[4]),
+        pltpu.make_async_copy(g_ref, g_out.at[t], local.at[5]),
+    ]
+    for load in loads:
+        load.start()
+    outs[me] = wo[...].T
+    small_full[me] = small_ref[...]
+    place.barrier([place.owner(k) for k in range(1, n)], [place.core, place.chip])
+
+    smalls = []
+    for k in range(1, n):
+        smalls.append(
+            pltpu.make_async_remote_copy(
+                src_ref=small_ref,
+                dst_ref=small_full.at[me],
+                send_sem=small_send.at[k - 1],
+                recv_sem=small_recv.at[k - 1],
+                device_id={"dp": place.owner(k)},
+                device_id_type=MESH,
+            )
+        )
+        smalls[-1].start()
+
+    swap = Exchange(x_send, x_recv)
+    to_chip = swap.copy(0, x_ref, x_full.at[t], place.chip)
+    to_core = swap.copy(1, x_ref, x_full.at[t], place.core)
+    relay = swap.copy(2, x_full.at[place.chip], x_full.at[place.chip], place.core)
+    g_chip = swap.copy(3, g_ref, g_out.at[t], place.chip)
+    g_core = swap.copy(4, g_ref, g_out.at[t], place.core)
+    g_relay = swap.copy(5, g_out.at[place.chip], g_out.at[place.chip], place.core)
+    to_chip.start()
+    to_core.start()
+    for load in loads[:4]:
+        load.wait()
+    lanes = []
+    for number, (full, base, count, way) in enumerate(
+        (
+            (left, 0, size // 2, 0),
+            (right, 0, size // 2, 1),
+            (left, size // 2, size // 2, 0),
+            (right, size // 2, size // 2, 1),
+            (outs, 0, size // 2, 0),
+            (outs, size // 2, size // 2, 1),
+        )
+    ):
+        lanes.append(Lane(place, full, base, count, way, send.at[number], recv.at[number]))
+
+    def store(step):
+        whose, other = place.owner(-step), place.owner(step)
+        if step == n:
+            return []
+        return [
+            pltpu.make_async_copy(left.at[whose], qkv_out.at[whose, :, pl.ds(0, width + half)], stored.at[0, step]),
+            pltpu.make_async_copy(right.at[other], qkv_out.at[other, :, pl.ds(width + half, width + half)], stored.at[1, step]),
+            pltpu.make_async_copy(outs.at[whose, pl.ds(0, size // 2)], out_out.at[whose, pl.ds(0, size // 2)], stored.at[2, step]),
+            pltpu.make_async_copy(
+                outs.at[other, pl.ds(size // 2, size // 2)], out_out.at[other, pl.ds(size // 2, size // 2)], stored.at[3, step]
+            ),
+        ]
+
+    writes = []
+
+    def tick(step):
+        for lane in lanes:
+            if step > 1:
+                lane.arrive(step - 1)
+            if step < n:
+                lane.start(step)
+        for write in store(step - 1):
+            write.start()
+            writes.append(write)
+
+    gain = shift = None
+
+    def norm(block):
+        @pl.loop(0, rows // 16)
+        def _(i):
+            here = pl.ds(pl.multiple_of(i * 16, 16), 16)
+            there = pl.ds(pl.multiple_of(block * rows + i * 16, 16), 16)
+            normed[there, :] = row_norm(x_full[block, here, :].astype(f32), gain, shift).astype(bf16)
+
+    def project(step):
+        for full, whose, base in ((left, place.owner(-step), 0), (right, place.owner(step), width + half)):
+            xs = normed[:, pl.ds(pl.multiple_of(whose * size, size), size)]
+            for j in range(0, width + half, 256):
+                part = dot(full[whose, :, j : j + 256].T, xs, ((1,), (1,)))
+                where = slice(base + j, base + j + 256)
+                if step == 0:
+                    lin[where, :] = part
+                else:
+                    lin[where, :] += part
+
+    tick(1)
+    loads[4].wait()
+    for small in smalls:
+        small.wait_recv()
+    count = small_ref.shape[1]
+    gain = lane_vector(small_full, 0, size // count)
+    shift = lane_vector(small_full, size // count, size // count)
+    norm(t)
+    to_core.wait_recv()
+    norm(place.core)
+    tick(2)
+    tick(3)
+    to_chip.wait_recv()
+    relay.start()
+    g_chip.start()
+    g_core.start()
+    norm(place.chip)
+    tick(4)
+    relay.wait_recv()
+    norm(place.cross)
+    normed_store = pltpu.make_async_copy(normed, normed_out, local.at[6])
+    normed_store.start()
+    project(0)
+    done = 1
+    for step in range(5, n):
+        tick(step)
+        while done < min(step - 1, 2 * (step - 4) + 1):
+            project(done)
+            done += 1
+    g_chip.wait_recv()
+    g_relay.start()
+    while done < n - 1:
+        project(done)
+        done += 1
+    tick(n)
+    project(n - 1)
+    for copy in (to_chip, to_core, relay, g_chip, g_core, g_relay):
+        copy.wait_send()
+    g_core.wait_recv()
+    g_relay.wait_recv()
+    for small in smalls:
+        small.wait_send()
+    for lane in lanes:
+        lane.finish()
+    loads[5].wait()
+    for write in writes:
+        write.wait()
+    normed_store.wait()
+
+
+def enter(x, g, wq, wk, wv, wo, small, n):
+    rows, model = x.shape
+    size, width = wq.shape
+    big = 3 * width // 2
+    kernel = lambda *refs: enter_kernel(n, *refs)
+    return pl.pallas_call(
+        kernel,
+        in_specs=[HBM] * 5 + [VMEM, VMEM],
+        out_specs=[HBM, HBM, HBM, HBM, VMEM, VMEM],
+        out_shape=[
+            jax.ShapeDtypeStruct((4 * rows, model), bf16),
+            jax.ShapeDtypeStruct((4, rows, model), bf16),
+            jax.ShapeDtypeStruct((n, size, 3 * width), bf16),
+            jax.ShapeDtypeStruct((n, size, width), bf16),
+            jax.ShapeDtypeStruct((3 * width, 4 * rows), f32),
+            jax.ShapeDtypeStruct((n,) + small.shape, bf16),
+        ],
+        scratch_shapes=[
+            pltpu.VMEM((4, rows, model), bf16),
+            pltpu.VMEM((4 * rows, model), bf16),
+            pltpu.VMEM((n, size, big), bf16),
+            pltpu.VMEM((n, size, big), bf16),
+            pltpu.VMEM((n, size, width), bf16),
+            DMA((n - 1,)),
+            DMA((n - 1,)),
+            DMA((6, n - 1)),
+            DMA((6, n - 1)),
+            DMA((6,)),
+            DMA((6,)),
+            DMA((7,)),
+            DMA((4, n)),
+        ],
+        compiler_params=pltpu.CompilerParams(collective_id=1, has_side_effects=True, vmem_limit_bytes=56 << 20),
+        cost_estimate=pl.CostEstimate(flops=6 * width * rows * 4 * model, bytes_accessed=40 << 20, transcendentals=0),
+        name="enter",
+    )(x, g, wq, wk, wv, wo, small)
+
+
 def norm_forward(rows):
     center = rows - jnp.mean(rows, axis=-1, keepdims=True)
     rstd = lax.rsqrt(jnp.mean(center * center, axis=-1, keepdims=True) + EPS)
@@ -303,32 +590,48 @@
     heads = width // HD
     model = layer_input.shape[1]
 
-    x_full = tensor_gather(layer_input)
-    g_full = tensor_gather(out_grad, after=x_full)
-
-    small = jnp.concatenate(
-        [first_gain, first_shift, second_gain, second_shift, query_bias.reshape(-1), value_bias.reshape(-1)]
-    )
-    small = lax.all_gather(small.reshape(1, -1), "dp", axis=0, tiled=True)
+    bias_key = jnp.pad(key_bias.astype(f32), ((0, 0), (0, HD - ROT))).reshape(-1)
     part = model // n
+    per = HD // n
+    if ring.ring:
+        lanes = 128
+        small = jnp.concatenate(
+            [first_gain, first_shift, second_gain, second_shift, query_bias.reshape(-1), value_bias.reshape(-1)]
+        )
+        small = jnp.pad(small.reshape(-1, lanes), ((0, 16 - small.shape[0] // lanes), (0, 0)))
+        normed, g_full, qkv, out_t, lin, small = enter(
+            layer_input, out_grad, query_weight, key_weight, value_weight, out_weight, small, n
+        )
+        g_full = g_full.reshape(-1, model)
+        qkv = qkv.reshape(model, -1)
+        out_t = out_t.reshape(model, -1)
+        small = small.reshape(n, -1)[:, : 4 * part + 2 * heads * per]
+        gate, marks = ring.gather(gate_weight, after=lin)
+        up, marks = ring.gather(up_weight, pieces=2, after=marks[-2])
+        down_t, _ = ring.gather(down_weight.T, pieces=2, after=marks[-2])
+    else:
+        x_full = tensor_gather(layer_input)
+        g_full = tensor_gather(out_grad, after=x_full)
+        small = jnp.concatenate(
+            [first_gain, first_shift, second_gain, second_shift, query_bias.reshape(-1), value_bias.reshape(-1)]
+        )
+        small = lax.all_gather(small.reshape(1, -1), "dp", axis=0, tiled=True)
+        qkv, _ = ring.gather(jnp.concatenate([query_weight, key_weight, value_weight], axis=1))
+        out_t, _ = ring.gather(out_weight.T)
+        gate, _ = ring.gather(gate_weight)
+        up, _ = ring.gather(up_weight)
+        down_t, _ = ring.gather(down_weight.T)
     gain_one, shift_one, gain_two, shift_two = (
         small[:, i * part : (i + 1) * part].reshape(model).astype(f32) for i in range(4)
     )
-    per = HD // n
     biases = small[:, 4 * part :].reshape(n, 2, heads, per).transpose(1, 2, 0, 3).reshape(2, width).astype(f32)
-    bias_key = jnp.pad(key_bias.astype(f32), ((0, 0), (0, HD - ROT))).reshape(-1)
     bias_lin = jnp.concatenate([biases[0], bias_key, biases[1]])
-
-    qkv, marks = ring.gather(jnp.concatenate([query_weight, key_weight, value_weight], axis=1), pieces=2)
-    out_t, _ = ring.gather(out_weight.T, after=marks[-2])
-    gate, marks = ring.gather(gate_weight, after=marks[-2])
-    up, marks = ring.gather(up_weight, pieces=2, after=marks[-2])
-    down_t, _ = ring.gather(down_weight.T, pieces=2, after=marks[-2])
-
-    hat_full, _ = norm_forward(x_full.astype(f32))
-    normed = (hat_full * gain_one + shift_one).astype(bf16)
-
-    lin = dot(qkv, normed, ((0,), (1,))) + bias_lin[:, None]
+    if not ring.ring:
+        hat_full, _ = norm_forward(x_full.astype(f32))
+        normed = (hat_full * gain_one + shift_one).astype(bf16)
+        lin = dot(qkv, normed, ((0,), (1,)))
+    lin = lin + bias_lin[:, None]
+
     freqs = jnp.exp(-(2.0 / ROT) * jnp.arange(HALF).astype(f32) * math.log(10000.0))
     angles = freqs[:, None] * positions.astype(f32)[None, :]
     cosine, sine = jnp.cos(angles), jnp.sin(angles)

time: 1030 us -> 850 us (0.83)
  waiting for transfers between devices: 349 us -> 221 us
  Pallas kernels: 45 us -> 137 us
  local copies, waits for them, and re-layouts: 147 us -> 96.2 us
  starting transfers between devices: 231 us -> 188 us
  blocking collectives: 30.9 us -> 0 us
  matrix products: 137 us -> 124 us
    ppermute x112 -> x70, waiting for transfers between devices: 201 us -> 77.8 us  [gather(): block = lax.ppermute(block, 'dp', self.down if way else self.up)]
    pallas_call x0 -> x1, Pallas kernels: none -> 92.5 us  [enter(): pl.pallas_call(kernel, in_specs=[HBM] * 5 + [VMEM, VMEM], out_specs=[HBM,...]
    ppermute x112 -> x70, starting transfers between devices: 126 us -> 81.2 us  [gather(): block = lax.ppermute(block, 'dp', self.down if way else self.up)]
    all_gather x1 -> x0, blocking collectives: 30.9 us -> none  [local(): small = lax.all_gather(small.reshape(1, -1), 'dp', axis=0, tiled=True)]
    dynamic_update_slice x113 -> x70, local copies, waits for them, and re-layouts: 46.4 us -> 19.2 us  [gather(): full = lax.dynamic_update_slice(full, block[None], (whose, base, 0))]
    dot_general x15 -> x14, matrix products: 137 us -> 124 us  [dot(): lax.dot_general(a, b, ((dims[0], dims[1]), ((), ())), preferred_element_t...]
    dynamic_update_slice x14 -> x6, local copies, waits for them, and re-layouts: 15.9 us -> 3.63 us  [tensor_gather(): full = lax.dynamic_update_slice(full, block[None], (t ^ flip, 0, 0))]
    dot_general x5 -> x4, local copies, waits for them, and re-layouts: 30.4 us -> 24.4 us  [dot(): lax.dot_general(a, b, ((dims[0], dims[1]), ((), ())), preferred_element_t...]
  transfers between devices with their start and end apart: 225 -> 177, of which waited for: 127 -> 96; matrix products, arithmetic and copies ran while one was open for 29% -> 26% of each run, Pallas kernels for 4% -> 5%
where the time goes in v2:
time: 850 us; the launch traced here: 837 us
  waiting for transfers between devices  221 us (26%)
  starting transfers between devices  188 us (22%)
  Pallas kernels  137 us (16%)
  matrix products  124 us (15%)
  local copies, waits for them, and re-layouts  96.2 us (11%)
  other arithmetic  68.4 us (8%)
    dot_general x14, matrix products, dot(): lax.dot_general(a, b, ((dims[0], dims[1]), ((), ())), preferred_element_t...  124 us
    ppermute x84, waiting for transfers between devices, scatter(): got = lax.ppermute(moving.astype(bf16), 'dp', self.down if way else self.up)  112 us
    pallas_call x1, Pallas kernels, enter(): pl.pallas_call(kernel, in_specs=[HBM] * 5 + [VMEM, VMEM], out_specs=[HBM,...  92.5 us
    ppermute x84, starting transfers between devices, scatter(): got = lax.ppermute(moving.astype(bf16), 'dp', self.down if way else self.up)  92.1 us
    ppermute x70, starting transfers between devices, gather(): block = lax.ppermute(block, 'dp', self.down if way else self.up)  81.2 us
    ppermute x70, waiting for transfers between devices, gather(): block = lax.ppermute(block, 'dp', self.down if way else self.up)  77.8 us
    convert_element_type x30, other arithmetic, scatter(): got = lax.ppermute(moving.astype(bf16), 'dp', self.down if way else self.up)  26 us
    dot_general x4, local copies, waits for them, and re-layouts, dot(): lax.dot_general(a, b, ((dims[0], dims[1]), ((), ())), preferred_element_t...  24.4 us
  transfers between devices with their start and end apart: 177, of which 96 were waited for; matrix products, arithmetic and copies ran while one was open for 26% of the time, Pallas kernels for 5%

profile of v2, /device:TPU:0, one launch (start us, length us, event | category | flops | bytes accessed | tf_op | source)
XLA Modules:
  0.0 836.9 jit_solution(17485475483932332351)
XLA Ops:
  5.5 92.5 %enter.1 = (bf16[1024,2048]{1,0:T(8,128)(2,1)}, bf16[4,256,2048]{2,1,0:T(8,128)(2,1)}, bf16[8,256,1536]{2,1,0:T(8,128)(2,1)}, bf16[8,256,512]{2,1,0:T(8,128)(2,1...) custom-call(bf16[256,2048]{1,0:T(8,128)(2,1)} %refs_0_.1, bf16[256,2048]{1,0:T(8,128)(2,1)} %refs_1_.1, ...), custom_call_target="tpu_custom_call" | custom-call | flops 6442450944 | bytes 41943040 | tf_op jit(solution)/shard_map/enter/pallas_call | solution.py:519
  102.4 6.0 broadcast_add_fusion.q_ref.k_ref.v_ref
  111.2 22.1 %attend_forward.1 = (bf16[1024,512]{1,0:T(8,128)(2,1)S(1)}, bf16[512,1024]{1,0:T(8,128)(2,1)S(1)}, bf16[512,1024]{1,0:T(8,128)(2,1)S(1)}, bf16[512,1024]{1,0:T(8,128)(2,1)S(1)}, f32[4,2,1024]{2,1,0:T(2,128)S(1)}) custom-call(f32[1536,1024]{1,0:T(8,128)} %broadcast_add_fusion.q_ref.k_ref.v_ref, f32[1536,1024]{1,0:T(8,128)} %broadcast_add_fusion.q_ref.k_ref.v_ref, ...), custom_call_target="tpu_custom_call" | custom-call | flops 2147483648 | bytes 31457280 | tf_op jit(solution)/shard_map/attend_forward/pallas_call | solution.py:185
  135.3 5.7 fusion.137
  141.0 3.9 fusion.30
  147.1 6.5 copy.100
  163.6 6.0 collective-permute-done.8
  182.6 5.0 collective-permute-done.12
  191.2 5.0 collective-permute-done.14
  221.6 5.3 collective-permute-done.18
  266.8 5.0 collective-permute-done.43
  276.9 5.3 collective-permute-done.44
  283.3 4.4 collective-permute-done.45
  289.5 5.6 collective-permute-done.46
  336.0 8.5 %fusion.138 = f32[1024,1408]{1,0:T(8,128)} fusion(bf16[1024,2048]{1,0:T(8,128)(2,1)S(1)} %bitcast.669, bf16[2048,1408]{1,0:T(8,128)(2,1)S(1)} %bitcast.684), kind=kOutput, calls=%fused_computation.386 | convolution fusion | flops 5905580032 | bytes 15728640 | tf_op jit(solution)/shard_map/dot_general | solution.py:146
  344.4 6.4 copy.99
  362.1 11.9 %fusion.140 = f32[1024,1408]{1,0:T(8,128)} fusion(bf16[1024,2048]{1,0:T(8,128)(2,1)} %bitcast.699, bf16[2048,1408]{1,0:T(8,128)(2,1)} %bitcast.688), kind=kOutput, calls=%fused_computation.388 | convolution fusion | flops 5905580032 | bytes 15728640 | tf_op jit(solution)/shard_map/dot_general | solution.py:146
  374.0 15.1 %multiply_convert_fusion.1 = (bf16[1024,1408]{1,0:T(8,128)(2,1)}, bf16[1024,1408]{1,0:T(8,128)(2,1)}, bf16[1024,1408]{1,0:T(8,128)(2,1)S(1)}) fusion(f32[1024,1408]{1,0:T(8,128)} %fusion.140, f32[1024,1408]{1,0:T(8,128)} %fusion.138, bf16[1024,2048]{1,0:T(8,128)(2,1)S(1)} %bitcast.671, bf16[2048,1408]{1,0:T(8,128)(2,1)} %bitcast.29), kind=kOutput, calls=%fused_computation.1 | convolution fusion | flops 5927206912 | bytes 30146560 | tf_op jit(solution)/shard_map/dot_general | solution.py:146
  389.1 6.8 fusion.3
  395.9 4.3 copy-done.15
  403.2 8.9 %fusion.141 = f32[1024,2048]{1,0:T(8,128)} fusion(bf16[1024,1408]{1,0:T(8,128)(2,1)S(1)} %copy-done.56, bf16[2048,1408]{1,0:T(8,128)(2,1)S(1)} %bitcast.687), kind=kOutput, calls=%fused_computation.389 | convolution fusion | flops 5905580032 | bytes 17039360 | tf_op jit(solution)/shard_map/dot_general | solution.py:146
  412.1 6.8 fusion.5
  421.5 10.0 %fusion.7 = f32[8,256,1408]{2,1,0:T(8,128)S(1)} fusion(bf16[8,256,1024]{2,1,0:T(8,128)(2,1)S(1)} %bitcast.702, bf16[1024,1408]{1,0:T(8,128)(2,1)} %get-tuple-element.197), kind=kOutput, calls=%fused_computation.17 | convolution fusion | flops 5905580032 | bytes 18612224 | tf_op jit(solution)/shard_map/dot_general | solution.py:146
  433.2 12.9 %convolution_add_fusion = f32[1024,2048]{1,0:T(8,128)} fusion(f32[1024,2048]{1,0:T(8,128)} %fusion.141, bf16[1024,1408]{1,0:T(8,128)(2,1)} %get-tuple-element.197, bf16[2048,1408]{1,0:T(8,128)(2,1)} %bitcast.29), kind=kOutput, calls=%fused_computation.8 | convolution fusion | flops 5907677184 | bytes 25427968 | tf_op jit(solution)/shard_map/dot_general | solution.py:146
  446.1 10.5 %fusion.139 = f32[4,256,2048]{2,1,0:T(8,128)} fusion(bf16[4,256,1408]{2,1,0:T(8,128)(2,1)} %bitcast.732, bf16[2048,1408,1]{1,0,2:T(8,128)(2,1)S(1)} %bitcast.691), kind=kOutput, calls=%fused_computation.387 | convolution fusion | flops 5905580032 | bytes 17039360 | tf_op jit(solution)/shard_map/dot_general | solution.py:146
  467.7 7.1 collective-permute-done.164
  478.3 6.4 collective-permute-done.150
  488.3 5.5 collective-permute-done.136
  498.9 6.2 collective-permute-done.165
  508.8 4.1 collective-permute-done.151
  516.6 4.0 collective-permute-done.137
  523.0 5.4 collective-permute-done.166
  532.0 4.0 collective-permute-done.152
  539.8 4.0 collective-permute-done.138
  546.2 5.3 collective-permute-done.167
  560.9 3.8 collective-permute-done.139
  567.8 4.5 collective-permute-done.146
  579.8 19.8 %collective-permute-done.81 = bf16[256,2048]{1,0:T(8,128)(2,1)S(1)} collective-permute-done((bf16[256,2048]{1,0:T(8,128)(2,1)S(1)}, bf16[256,2048]{1,0:T(8,128)(2,1)S(1)}, u32[]{:S(2)}, u32[]{:S(2)}) %collective-permute-start.81) | collective-permute-done | bytes 1048608 | tf_op jit(solution)/shard_map/ppermute | solution.py:121
  601.9 5.1 multiply_reduce_fusion
  649.5 6.4 copy.104
  655.9 4.7 fusion.38
  663.0 5.6 convolution_convert_fusion.d_ref
  668.5 22.6 %attend_backward.1 = (bf16[512,1024]{1,0:T(8,128)(2,1)S(1)}, bf16[512,1024]{1,0:T(8,128)(2,1)S(1)}, bf16[512,1024]{1,0:T(8,128)(2,1)S(1)}, f32[4,128,128]{2,1,0:T(8,128)S(1)}) custom-call(bf16[512,1024]{1,0:T(8,128)(2,1)S(1)} %get-tuple-element.42.q_ref, bf16[512,1024]{1,0:T(8,128)(2,1)S(1)} %get-tuple-element.43.k_ref, bf16[512,1024]{1,0:T(8,128)(2,1)} %copy-done.4, ...), custom_call_target="tpu_custom_call" | custom-call | flops 5368709120 | bytes 31457280 | tf_op jit(solution)/shard_map/attend_backward/pallas_call | solution.py:249
  694.5 6.9 fusion.143
  701.4 4.4 copy-done.13
  708.9 5.1 copy.103
  714.0 9.9 %fusion.142 = f32[4,256,2048]{2,1,0:T(8,128)S(1)} fusion(bf16[4,256,1536]{2,1,0:T(8,128)(2,1)} %bitcast.704, bf16[2048,1536,1]{1,0,2:T(8,128)(2,1)} %bitcast.731), kind=kOutput, calls=%fused_computation.390 | convolution fusion | flops 6442450944 | bytes 17825792 | tf_op jit(solution)/shard_map/dot_general | solution.py:146
  732.4 3.7 collective-permute-done.93
  (669 shorter events, 399.8 us)
Async XLA Ops:
  99.0 60.0 %collective-permute-start.6 = (bf16[128,1408]{1,0:T(8,128)(2,1)}, bf16[128,1408]{1,0:T(8,128)(2,1)}, u32[]{:S(2)}, u32[]{:S(2)}) collective-permute-start(bf16[128,1408]{1,0:T(8,128)(2,1)} %get-tuple-element.233), channel_id=1, source_target_pairs={{0,8},{8,16},{16,24},{24,28},{28,20},{20,12},{12,4},{4,0},{1,9},{9... | collective-permute-start | bytes 1081352 | tf_op jit(solution)/shard_map/ppermute | solution.py:59
  100.4 60.1 %collective-permute-start.7 = (bf16[128,1408]{1,0:T(8,128)(2,1)}, bf16[128,1408]{1,0:T(8,128)(2,1)S(1)}, u32[]{:S(2)}, u32[]{:S(2)}) collective-permute-start(bf16[128,1408]{1,0:T(8,128)(2,1)} %get-tuple-element.234), channel_id=1, source_target_pairs={{8,0},{16,8},{24,16},{28,24},{20,28},{12,20},{4,12},{0,4},{9,1},{1... | collective-permute-start | bytes 1081352 | tf_op jit(solution)/shard_map/ppermute | solution.py:59
  144.9 28.3 %collective-permute-start.1 = (bf16[256,2048]{1,0:T(8,128)(2,1)}, bf16[256,2048]{1,0:T(8,128)(2,1)}, u32[]{:S(2)}, u32[]{:S(2)}) collective-permute-start(bf16[256,2048]{1,0:T(8,128)(2,1)} %get-tuple-element.207), channel_id=1, source_target_pairs={{0,1},{1,0},{2,3},{3,2},{4,5},{5,4},{6,7},{7,6},{8,9},{9,8},{10,11... | collective-permute-start | bytes 3145736 | tf_op jit(solution)/shard_map/ppermute | solution.py:119
  144.9 55.3 %collective-permute-start = (bf16[256,2048]{1,0:T(8,128)(2,1)}, bf16[256,2048]{1,0:T(8,128)(2,1)}, u32[]{:S(2)}, u32[]{:S(2)}) collective-permute-start(bf16[256,2048]{1,0:T(8,128)(2,1)} %get-tuple-element.206), channel_id=1, source_target_pairs={{0,1},{1,0},{2,3},{3,2},{4,5},{5,4},{6,7},{7,6},{8,9},{9,8},{10,11... | collective-permute-start | bytes 3145736 | tf_op jit(solution)/shard_map/ppermute | solution.py:120
  175.4 24.7 %collective-permute-start.2 = (bf16[256,2048]{1,0:T(8,128)(2,1)S(1)}, bf16[256,2048]{1,0:T(8,128)(2,1)S(1)}, u32[]{:S(2)}, u32[]{:S(2)}) collective-permute-start(bf16[256,2048]{1,0:T(8,128)(2,1)S(1)} %fusion.28), channel_id=1, source_target_pairs={{0,2},{2,0},{1,3},{3,1},{4,6},{6,4},{5,7},{7,5},{8,10},{10,8},{9,1... | collective-permute-start | bytes 3145736 | tf_op jit(solution)/shard_map/ppermute | solution.py:121
  204.4 61.8 %collective-permute-start.3 = (bf16[256,2048]{1,0:T(8,128)(2,1)S(1)}, bf16[256,2048]{1,0:T(8,128)(2,1)S(1)}, u32[]{:S(2)}, u32[]{:S(2)}) collective-permute-start(bf16[256,2048]{1,0:T(8,128)(2,1)S(1)} %get-tuple-element.114), channel_id=1, source_target_pairs={{0,1},{1,0},{2,3},{3,2},{4,5},{5,4},{6,7},{7,6},{8,9},{9,8},{10,11... | collective-permute-start | bytes 3145736 | tf_op jit(solution)/shard_map/ppermute | solution.py:101
  204.5 62.1 %collective-permute-start.4 = (bf16[256,2048]{1,0:T(8,128)(2,1)S(1)}, bf16[256,2048]{1,0:T(8,128)(2,1)S(1)}, u32[]{:S(2)}, u32[]{:S(2)}) collective-permute-start(bf16[256,2048]{1,0:T(8,128)(2,1)S(1)} %get-tuple-element.114), channel_id=1, source_target_pairs={{0,2},{2,0},{1,3},{3,1},{4,6},{6,4},{5,7},{7,5},{8,10},{10,8},{9,1... | collective-permute-start | bytes 3145736 | tf_op jit(solution)/shard_map/ppermute | solution.py:100
  266.6 69.2 %collective-permute-start.5 = (bf16[256,2048]{1,0:T(8,128)(2,1)S(1)}, bf16[256,2048]{1,0:T(8,128)(2,1)S(1)}, u32[]{:S(2)}, u32[]{:S(2)}) collective-permute-start(bf16[256,2048]{1,0:T(8,128)(2,1)S(1)} %collective-permute-done.4), channel_id=1, source_target_pairs={{0,1},{1,0},{2,3},{3,2},{4,5},{5,4},{6,7},{7,6},{8,9},{9,8},{10,11... | collective-permute-start | bytes 3145736 | tf_op jit(solution)/shard_map/ppermute | solution.py:102
  272.4 23.7 %collective-permute-start.48 = (bf16[64,1408]{1,0:T(8,128)(2,1)S(1)}, bf16[64,1408]{1,0:T(8,128)(2,1)S(1)}, u32[]{:S(2)}, u32[]{:S(2)}) collective-permute-start(bf16[64,1408]{1,0:T(8,128)(2,1)S(1)} %get-tuple-element.232), channel_id=1, source_target_pairs={{0,8},{8,16},{16,24},{24,28},{28,20},{20,12},{12,4},{4,0},{1,9},{9... | collective-permute-start | bytes 540680 | tf_op jit(solution)/shard_map/ppermute | solution.py:59
  273.7 23.4 %collective-permute-start.49 = (bf16[64,1408]{1,0:T(8,128)(2,1)S(1)}, bf16[64,1408]{1,0:T(8,128)(2,1)S(1)}, u32[]{:S(2)}, u32[]{:S(2)}) collective-permute-start(bf16[64,1408]{1,0:T(8,128)(2,1)S(1)} %get-tuple-element.231), channel_id=1, source_target_pairs={{8,0},{16,8},{24,16},{28,24},{20,28},{12,20},{4,12},{0,4},{9,1},{1... | collective-permute-start | bytes 540680 | tf_op jit(solution)/shard_map/ppermute | solution.py:59
  274.5 23.8 %collective-permute-start.50 = (bf16[64,1408]{1,0:T(8,128)(2,1)S(1)}, bf16[64,1408]{1,0:T(8,128)(2,1)S(1)}, u32[]{:S(2)}, u32[]{:S(2)}) collective-permute-start(bf16[64,1408]{1,0:T(8,128)(2,1)S(1)} %get-tuple-element.230), channel_id=1, source_target_pairs={{0,8},{8,16},{16,24},{24,28},{28,20},{20,12},{12,4},{4,0},{1,9},{9... | collective-permute-start | bytes 540680 | tf_op jit(solution)/shard_map/ppermute | solution.py:59
  330.3 20.6 %collective-permute-start.68 = (bf16[64,1408]{1,0:T(8,128)(2,1)S(1)}, bf16[64,1408]{1,0:T(8,128)(2,1)S(1)}, u32[]{:S(2)}, u32[]{:S(2)}) collective-permute-start(bf16[64,1408]{1,0:T(8,128)(2,1)S(1)} %collective-permute-done.64), channel_id=1, source_target_pairs={{0,8},{8,16},{16,24},{24,28},{28,20},{20,12},{12,4},{4,0},{1,9},{9... | collective-permute-start | bytes 540680 | tf_op jit(solution)/shard_map/ppermute | solution.py:59
  331.1 21.0 %collective-permute-start.69 = (bf16[64,1408]{1,0:T(8,128)(2,1)S(1)}, bf16[64,1408]{1,0:T(8,128)(2,1)S(1)}, u32[]{:S(2)}, u32[]{:S(2)}) collective-permute-start(bf16[64,1408]{1,0:T(8,128)(2,1)S(1)} %collective-permute-done.65), channel_id=1, source_target_pairs={{8,0},{16,8},{24,16},{28,24},{20,28},{12,20},{4,12},{0,4},{9,1},{1... | collective-permute-start | bytes 540680 | tf_op jit(solution)/shard_map/ppermute | solution.py:59
  332.5 21.8 %collective-permute-start.70 = (bf16[64,1408]{1,0:T(8,128)(2,1)S(1)}, bf16[64,1408]{1,0:T(8,128)(2,1)S(1)}, u32[]{:S(2)}, u32[]{:S(2)}) collective-permute-start(bf16[64,1408]{1,0:T(8,128)(2,1)S(1)} %collective-permute-done.66), channel_id=1, source_target_pairs={{0,8},{8,16},{16,24},{24,28},{28,20},{20,12},{12,4},{4,0},{1,9},{9... | collective-permute-start | bytes 540680 | tf_op jit(solution)/shard_map/ppermute | solution.py:59
  334.3 21.2 %collective-permute-start.71 = (bf16[64,1408]{1,0:T(8,128)(2,1)S(1)}, bf16[64,1408]{1,0:T(8,128)(2,1)}, u32[]{:S(2)}, u32[]{:S(2)}) collective-permute-start(bf16[64,1408]{1,0:T(8,128)(2,1)S(1)} %collective-permute-done.67), channel_id=1, source_target_pairs={{8,0},{16,8},{24,16},{28,24},{20,28},{12,20},{4,12},{0,4},{9,1},{1... | collective-permute-start | bytes 540680 | tf_op jit(solution)/shard_map/ppermute | solution.py:59
  401.0 58.4 %collective-permute-start.163 = (bf16[128,1408]{1,0:T(8,128)(2,1)}, bf16[128,1408]{1,0:T(8,128)(2,1)S(1)}, u32[]{:S(2)}, u32[]{:S(2)}) collective-permute-start(bf16[128,1408]{1,0:T(8,128)(2,1)} %get-tuple-element.163), channel_id=1, source_target_pairs={{0,8},{8,16},{16,24},{24,28},{28,20},{20,12},{12,4},{4,0},{1,9},{9... | collective-permute-start | bytes 1081352 | tf_op jit(solution)/shard_map/ppermute | solution.py:84
  402.5 57.6 %collective-permute-start.170 = (bf16[128,1408]{1,0:T(8,128)(2,1)S(1)}, bf16[128,1408]{1,0:T(8,128)(2,1)S(1)}, u32[]{:S(2)}, u32[]{:S(2)}) collective-permute-start(bf16[128,1408]{1,0:T(8,128)(2,1)S(1)} %get-tuple-element.164), channel_id=1, source_target_pairs={{8,0},{16,8},{24,16},{28,24},{20,28},{12,20},{4,12},{0,4},{9,1},{1... | collective-permute-start | bytes 1081352 | tf_op jit(solution)/shard_map/ppermute | solution.py:84
  419.1 42.8 %collective-permute-start.149 = (bf16[128,1408]{1,0:T(8,128)(2,1)S(1)}, bf16[128,1408]{1,0:T(8,128)(2,1)S(1)}, u32[]{:S(2)}, u32[]{:S(2)}) collective-permute-start(bf16[128,1408]{1,0:T(8,128)(2,1)S(1)} %get-tuple-element.179), channel_id=1, source_target_pairs={{0,8},{8,16},{16,24},{24,28},{28,20},{20,12},{12,4},{4,0},{1,9},{9... | collective-permute-start | bytes 1081352 | tf_op jit(solution)/shard_map/ppermute | solution.py:84
  420.6 41.7 %collective-permute-start.156 = (bf16[128,1408]{1,0:T(8,128)(2,1)S(1)}, bf16[128,1408]{1,0:T(8,128)(2,1)S(1)}, u32[]{:S(2)}, u32[]{:S(2)}) collective-permute-start(bf16[128,1408]{1,0:T(8,128)(2,1)S(1)} %get-tuple-element.180), channel_id=1, source_target_pairs={{8,0},{16,8},{24,16},{28,24},{20,28},{12,20},{4,12},{0,4},{9,1},{1... | collective-permute-start | bytes 1081352 | tf_op jit(solution)/shard_map/ppermute | solution.py:84
  431.6 32.3 %collective-permute-start.135 = (bf16[128,1408]{1,0:T(8,128)(2,1)S(1)}, bf16[128,1408]{1,0:T(8,128)(2,1)S(1)}, u32[]{:S(2)}, u32[]{:S(2)}) collective-permute-start(bf16[128,1408]{1,0:T(8,128)(2,1)S(1)} %get-tuple-element.195), channel_id=1, source_target_pairs={{0,8},{8,16},{16,24},{24,28},{28,20},{20,12},{12,4},{4,0},{1,9},{9... | collective-permute-start | bytes 1081352 | tf_op jit(solution)/shard_map/ppermute | solution.py:84
  460.1 36.0 %collective-permute-start.77 = (bf16[256,2048]{1,0:T(8,128)(2,1)S(1)}, bf16[256,2048]{1,0:T(8,128)(2,1)S(1)}, u32[]{:S(2)}, u32[]{:S(2)}) collective-permute-start(bf16[256,2048]{1,0:T(8,128)(2,1)S(1)} %get-tuple-element.205), channel_id=1, source_target_pairs={{0,1},{1,0},{2,3},{3,2},{4,5},{5,4},{6,7},{7,6},{8,9},{9,8},{10,11... | collective-permute-start | bytes 3145736 | tf_op jit(solution)/shard_map/ppermute | solution.py:119
  461.8 112.6 %collective-permute-start.76 = (bf16[256,2048]{1,0:T(8,128)(2,1)S(1)}, bf16[256,2048]{1,0:T(8,128)(2,1)S(1)}, u32[]{:S(2)}, u32[]{:S(2)}) collective-permute-start(bf16[256,2048]{1,0:T(8,128)(2,1)S(1)} %get-tuple-element.204), channel_id=1, source_target_pairs={{0,1},{1,0},{2,3},{3,2},{4,5},{5,4},{6,7},{7,6},{8,9},{9,8},{10,11... | collective-permute-start | bytes 3145736 | tf_op jit(solution)/shard_map/ppermute | solution.py:120
  462.4 35.5 %collective-permute-start.80 = (bf16[256,2048]{1,0:T(8,128)(2,1)S(1)}, bf16[256,2048]{1,0:T(8,128)(2,1)S(1)}, u32[]{:S(2)}, u32[]{:S(2)}) collective-permute-start(bf16[256,2048]{1,0:T(8,128)(2,1)S(1)} %get-tuple-element.203), channel_id=1, source_target_pairs={{0,1},{1,0},{2,3},{3,2},{4,5},{5,4},{6,7},{7,6},{8,9},{9,8},{10,11... | collective-permute-start | bytes 3145736 | tf_op jit(solution)/shard_map/ppermute | solution.py:119
  496.2 16.7 %collective-permute-start.151 = (bf16[128,1408]{1,0:T(8,128)(2,1)S(1)}, bf16[128,1408]{1,0:T(8,128)(2,1)S(1)}, u32[]{:S(2)}, u32[]{:S(2)}) collective-permute-start(bf16[128,1408]{1,0:T(8,128)(2,1)S(1)} %get-tuple-element.175), channel_id=1, source_target_pairs={{0,8},{8,16},{16,24},{24,28},{28,20},{20,12},{12,4},{4,0},{1,9},{9... | collective-permute-start | bytes 1081352 | tf_op jit(solution)/shard_map/ppermute | solution.py:84
  497.9 16.5 %collective-permute-start.158 = (bf16[128,1408]{1,0:T(8,128)(2,1)S(1)}, bf16[128,1408]{1,0:T(8,128)(2,1)S(1)}, u32[]{:S(2)}, u32[]{:S(2)}) collective-permute-start(bf16[128,1408]{1,0:T(8,128)(2,1)S(1)} %get-tuple-element.176), channel_id=1, source_target_pairs={{8,0},{16,8},{24,16},{28,24},{20,28},{12,20},{4,12},{0,4},{9,1},{1... | collective-permute-start | bytes 1081352 | tf_op jit(solution)/shard_map/ppermute | solution.py:84
  505.2 15.4 %collective-permute-start.137 = (bf16[128,1408]{1,0:T(8,128)(2,1)S(1)}, bf16[128,1408]{1,0:T(8,128)(2,1)S(1)}, u32[]{:S(2)}, u32[]{:S(2)}) collective-permute-start(bf16[128,1408]{1,0:T(8,128)(2,1)S(1)} %get-tuple-element.191), channel_id=1, source_target_pairs={{0,8},{8,16},{16,24},{24,28},{28,20},{20,12},{12,4},{4,0},{1,9},{9... | collective-permute-start | bytes 1081352 | tf_op jit(solution)/shard_map/ppermute | solution.py:84
  512.9 15.4 %collective-permute-start.166 = (bf16[128,1408]{1,0:T(8,128)(2,1)S(1)}, bf16[128,1408]{1,0:T(8,128)(2,1)S(1)}, u32[]{:S(2)}, u32[]{:S(2)}) collective-permute-start(bf16[128,1408]{1,0:T(8,128)(2,1)S(1)} %get-tuple-element.157), channel_id=1, source_target_pairs={{0,8},{8,16},{16,24},{24,28},{28,20},{20,12},{12,4},{4,0},{1,9},{9... | collective-permute-start | bytes 1081352 | tf_op jit(solution)/shard_map/ppermute | solution.py:84
  520.6 15.4 %collective-permute-start.152 = (bf16[128,1408]{1,0:T(8,128)(2,1)S(1)}, bf16[128,1408]{1,0:T(8,128)(2,1)S(1)}, u32[]{:S(2)}, u32[]{:S(2)}) collective-permute-start(bf16[128,1408]{1,0:T(8,128)(2,1)S(1)} %get-tuple-element.173), channel_id=1, source_target_pairs={{0,8},{8,16},{16,24},{24,28},{28,20},{20,12},{12,4},{4,0},{1,9},{9... | collective-permute-start | bytes 1081352 | tf_op jit(solution)/shard_map/ppermute | solution.py:84
  522.1 15.4 %collective-permute-start.159 = (bf16[128,1408]{1,0:T(8,128)(2,1)S(1)}, bf16[128,1408]{1,0:T(8,128)(2,1)S(1)}, u32[]{:S(2)}, u32[]{:S(2)}) collective-permute-start(bf16[128,1408]{1,0:T(8,128)(2,1)S(1)} %get-tuple-element.174), channel_id=1, source_target_pairs={{8,0},{16,8},{24,16},{28,24},{20,28},{12,20},{4,12},{0,4},{9,1},{1... | collective-permute-start | bytes 1081352 | tf_op jit(solution)/shard_map/ppermute | solution.py:84
  529.8 15.4 %collective-permute-start.145 = (bf16[128,1408]{1,0:T(8,128)(2,1)S(1)}, bf16[128,1408]{1,0:T(8,128)(2,1)S(1)}, u32[]{:S(2)}, u32[]{:S(2)}) collective-permute-start(bf16[128,1408]{1,0:T(8,128)(2,1)S(1)} %get-tuple-element.190), channel_id=1, source_target_pairs={{8,0},{16,8},{24,16},{28,24},{20,28},{12,20},{4,12},{0,4},{9,1},{1... | collective-permute-start | bytes 1081352 | tf_op jit(solution)/shard_map/ppermute | solution.py:84
  551.5 23.8 %collective-permute-start.79 = (bf16[256,2048]{1,0:T(8,128)(2,1)S(1)}, bf16[256,2048]{1,0:T(8,128)(2,1)S(1)}, u32[]{:S(2)}, u32[]{:S(2)}) collective-permute-start(bf16[256,2048]{1,0:T(8,128)(2,1)S(1)} %get-tuple-element.202), channel_id=1, source_target_pairs={{0,1},{1,0},{2,3},{3,2},{4,5},{5,4},{6,7},{7,6},{8,9},{9,8},{10,11... | collective-permute-start | bytes 3145736 | tf_op jit(solution)/shard_map/ppermute | solution.py:120
  553.0 26.1 %collective-permute-start.78 = (bf16[256,2048]{1,0:T(8,128)(2,1)S(1)}, bf16[256,2048]{1,0:T(8,128)(2,1)S(1)}, u32[]{:S(2)}, u32[]{:S(2)}) collective-permute-start(bf16[256,2048]{1,0:T(8,128)(2,1)S(1)} %fusion.24), channel_id=1, source_target_pairs={{0,2},{2,0},{1,3},{3,1},{4,6},{6,4},{5,7},{7,5},{8,10},{10,8},{9,1... | collective-permute-start | bytes 3145736 | tf_op jit(solution)/shard_map/ppermute | solution.py:121
  556.0 43.5 %collective-permute-start.81 = (bf16[256,2048]{1,0:T(8,128)(2,1)S(1)}, bf16[256,2048]{1,0:T(8,128)(2,1)S(1)}, u32[]{:S(2)}, u32[]{:S(2)}) collective-permute-start(bf16[256,2048]{1,0:T(8,128)(2,1)S(1)} %fusion.22), channel_id=1, source_target_pairs={{0,2},{2,0},{1,3},{3,1},{4,6},{6,4},{5,7},{7,5},{8,10},{10,8},{9,1... | collective-permute-start | bytes 3145736 | tf_op jit(solution)/shard_map/ppermute | solution.py:121
  572.3 39.9 %collective-permute-start.168 = (bf16[128,1408]{1,0:T(8,128)(2,1)}, bf16[128,1408]{1,0:T(8,128)(2,1)}, u32[]{:S(2)}, u32[]{:S(2)}) collective-permute-start(bf16[128,1408]{1,0:T(8,128)(2,1)} %get-tuple-element.153), channel_id=1, source_target_pairs={{0,8},{8,16},{16,24},{24,28},{28,20},{20,12},{12,4},{4,0},{1,9},{9... | collective-permute-start | bytes 1081352 | tf_op jit(solution)/shard_map/ppermute | solution.py:84
  574.5 38.4 %collective-permute-start.175 = (bf16[128,1408]{1,0:T(8,128)(2,1)}, bf16[128,1408]{1,0:T(8,128)(2,1)}, u32[]{:S(2)}, u32[]{:S(2)}) collective-permute-start(bf16[128,1408]{1,0:T(8,128)(2,1)} %get-tuple-element.154), channel_id=1, source_target_pairs={{8,0},{16,8},{24,16},{28,24},{20,28},{12,20},{4,12},{0,4},{9,1},{1... | collective-permute-start | bytes 1081352 | tf_op jit(solution)/shard_map/ppermute | solution.py:84
  575.4 39.2 %collective-permute-start.154 = (bf16[128,1408]{1,0:T(8,128)(2,1)}, bf16[128,1408]{1,0:T(8,128)(2,1)}, u32[]{:S(2)}, u32[]{:S(2)}) collective-permute-start(bf16[128,1408]{1,0:T(8,128)(2,1)} %get-tuple-element.169), channel_id=1, source_target_pairs={{0,8},{8,16},{16,24},{24,28},{28,20},{20,12},{12,4},{4,0},{1,9},{9... | collective-permute-start | bytes 1081352 | tf_op jit(solution)/shard_map/ppermute | solution.py:84
  579.1 35.9 %collective-permute-start.161 = (bf16[128,1408]{1,0:T(8,128)(2,1)}, bf16[128,1408]{1,0:T(8,128)(2,1)}, u32[]{:S(2)}, u32[]{:S(2)}) collective-permute-start(bf16[128,1408]{1,0:T(8,128)(2,1)} %get-tuple-element.170), channel_id=1, source_target_pairs={{8,0},{16,8},{24,16},{28,24},{20,28},{12,20},{4,12},{0,4},{9,1},{1... | collective-permute-start | bytes 1081352 | tf_op jit(solution)/shard_map/ppermute | solution.py:84
  600.5 17.5 %collective-permute-start.140 = (bf16[128,1408]{1,0:T(8,128)(2,1)}, bf16[128,1408]{1,0:T(8,128)(2,1)}, u32[]{:S(2)}, u32[]{:S(2)}) collective-permute-start(bf16[128,1408]{1,0:T(8,128)(2,1)} %get-tuple-element.185), channel_id=1, source_target_pairs={{0,8},{8,16},{16,24},{24,28},{28,20},{20,12},{12,4},{4,0},{1,9},{9... | collective-permute-start | bytes 1081352 | tf_op jit(solution)/shard_map/ppermute | solution.py:84
  612.9 33.4 %collective-permute-start.82 = (bf16[256,2048]{1,0:T(8,128)(2,1)S(1)}, bf16[256,2048]{1,0:T(8,128)(2,1)S(1)}, u32[]{:S(2)}, u32[]{:S(2)}) collective-permute-start(bf16[256,2048]{1,0:T(8,128)(2,1)S(1)} %get-tuple-element.110), channel_id=1, source_target_pairs={{0,1},{1,0},{2,3},{3,2},{4,5},{5,4},{6,7},{7,6},{8,9},{9,8},{10,11... | collective-permute-start | bytes 3145736 | tf_op jit(solution)/shard_map/ppermute | solution.py:101
  614.5 30.5 %collective-permute-start.83 = (bf16[256,2048]{1,0:T(8,128)(2,1)S(1)}, bf16[256,2048]{1,0:T(8,128)(2,1)S(1)}, u32[]{:S(2)}, u32[]{:S(2)}) collective-permute-start(bf16[256,2048]{1,0:T(8,128)(2,1)S(1)} %get-tuple-element.110), channel_id=1, source_target_pairs={{0,2},{2,0},{1,3},{3,1},{4,6},{6,4},{5,7},{7,5},{8,10},{10,8},{9,1... | collective-permute-start | bytes 3145736 | tf_op jit(solution)/shard_map/ppermute | solution.py:100
  660.7 63.3 %collective-permute-start.121 = (bf16[128,512]{1,0:T(8,128)(2,1)S(1)}, bf16[128,512]{1,0:T(8,128)(2,1)S(1)}, u32[]{:S(2)}, u32[]{:S(2)}) collective-permute-start(bf16[128,512]{1,0:T(8,128)(2,1)S(1)} %get-tuple-element.222), channel_id=1, source_target_pairs={{0,8},{8,16},{16,24},{24,28},{28,20},{20,12},{12,4},{4,0},{1,9},{9... | collective-permute-start | bytes 393224 | tf_op jit(solution)/shard_map/ppermute | solution.py:84
  662.5 61.5 %collective-permute-start.128 = (bf16[128,512]{1,0:T(8,128)(2,1)S(1)}, bf16[128,512]{1,0:T(8,128)(2,1)S(1)}, u32[]{:S(2)}, u32[]{:S(2)}) collective-permute-start(bf16[128,512]{1,0:T(8,128)(2,1)S(1)} %get-tuple-element.223), channel_id=1, source_target_pairs={{8,0},{16,8},{24,16},{28,24},{20,28},{12,20},{4,12},{0,4},{9,1},{1... | collective-permute-start | bytes 393224 | tf_op jit(solution)/shard_map/ppermute | solution.py:84
  706.0 24.3 %collective-permute-start.100 = (bf16[64,1536]{1,0:T(8,128)(2,1)S(1)}, bf16[64,1536]{1,0:T(8,128)(2,1)S(1)}, u32[]{:S(2)}, u32[]{:S(2)}) collective-permute-start(bf16[64,1536]{1,0:T(8,128)(2,1)S(1)} %get-tuple-element.148), channel_id=1, source_target_pairs={{8,0},{16,8},{24,16},{28,24},{20,28},{12,20},{4,12},{0,4},{9,1},{1... | collective-permute-start | bytes 589832 | tf_op jit(solution)/shard_map/ppermute | solution.py:84
  706.9 25.0 %collective-permute-start.107 = (bf16[64,1536]{1,0:T(8,128)(2,1)S(1)}, bf16[64,1536]{1,0:T(8,128)(2,1)S(1)}, u32[]{:S(2)}, u32[]{:S(2)}) collective-permute-start(bf16[64,1536]{1,0:T(8,128)(2,1)S(1)} %get-tuple-element.147), channel_id=1, source_target_pairs={{0,8},{8,16},{16,24},{24,28},{28,20},{20,12},{12,4},{4,0},{1,9},{9... | collective-permute-start | bytes 589832 | tf_op jit(solution)/shard_map/ppermute | solution.py:84
  708.0 24.4 %collective-permute-start.114 = (bf16[64,1536]{1,0:T(8,128)(2,1)S(1)}, bf16[64,1536]{1,0:T(8,128)(2,1)S(1)}, u32[]{:S(2)}, u32[]{:S(2)}) collective-permute-start(bf16[64,1536]{1,0:T(8,128)(2,1)S(1)} %get-tuple-element.146), channel_id=1, source_target_pairs={{8,0},{16,8},{24,16},{28,24},{20,28},{12,20},{4,12},{0,4},{9,1},{1... | collective-permute-start | bytes 589832 | tf_op jit(solution)/shard_map/ppermute | solution.py:84
  730.2 54.7 %collective-permute-start.86 = (bf16[256,2048]{1,0:T(8,128)(2,1)S(1)}, bf16[256,2048]{1,0:T(8,128)(2,1)S(1)}, u32[]{:S(2)}, u32[]{:S(2)}) collective-permute-start(bf16[256,2048]{1,0:T(8,128)(2,1)S(1)} %get-tuple-element.201), channel_id=1, source_target_pairs={{0,1},{1,0},{2,3},{3,2},{4,5},{5,4},{6,7},{7,6},{8,9},{9,8},{10,11... | collective-permute-start | bytes 3145736 | tf_op jit(solution)/shard_map/ppermute | solution.py:119
  778.2 32.5 %collective-permute-start.85 = (bf16[256,2048]{1,0:T(8,128)(2,1)S(1)}, bf16[256,2048]{1,0:T(8,128)(2,1)}, u32[]{:S(2)}, u32[]{:S(2)}) collective-permute-start(bf16[256,2048]{1,0:T(8,128)(2,1)S(1)} %get-tuple-element.200), channel_id=1, source_target_pairs={{0,1},{1,0},{2,3},{3,2},{4,5},{5,4},{6,7},{7,6},{8,9},{9,8},{10,11... | collective-permute-start | bytes 3145736 | tf_op jit(solution)/shard_map/ppermute | solution.py:120
  792.1 19.5 %collective-permute-start.87 = (bf16[256,2048]{1,0:T(8,128)(2,1)}, bf16[256,2048]{1,0:T(8,128)(2,1)}, u32[]{:S(2)}, u32[]{:S(2)}) collective-permute-start(bf16[256,2048]{1,0:T(8,128)(2,1)} %fusion.20), channel_id=1, source_target_pairs={{0,2},{2,0},{1,3},{3,1},{4,6},{6,4},{5,7},{7,5},{8,10},{10,8},{9,1... | collective-permute-start | bytes 3145736 | tf_op jit(solution)/shard_map/ppermute | solution.py:121
  (195 other events, 2378.8 us)

commit v3 on v2

--- a/solution.py
+++ b/solution.py
@@ -27,7 +27,7 @@
 class Ring:
     def __init__(self):
         self.n = lax.axis_size("dp")
-        self.ring = self.n % 2 == 0 and self.n <= 8
+        self.ring = self.n == 8 and lax.axis_size("tensor") == 4
         order = list(range(0, self.n, 2)) + list(range(self.n - 1, 0, -2))
         self.up = [(order[i], order[(i + 1) % self.n]) for i in range(self.n)]
         self.down = [(b, a) for a, b in self.up]
@@ -548,6 +548,372 @@
         name="enter",
     )(x, g, wq, wk, wv, wo, small)
 
+def attend_pair(pair, lin, bias_ref, cosine, sine, mask, q_all, k_all, v_all, logs, flat, mixed):
+    width, seq = q_all.shape
+
+    @pl.loop(0, 2)
+    def _(j):
+        head = pair * 2 + j
+        first = pl.multiple_of(head * HD, HD)
+        rows = pl.ds(first, HD)
+
+        def load(part):
+            at = pl.ds(pl.multiple_of(part * width + first, HD), HD)
+            return lin[at, :] + bias_ref[at, :]
+
+        q = rotate(load(0), cosine, sine, 1.0).astype(bf16)
+        k = rotate(load(1), cosine, sine, 1.0).astype(bf16)
+        values = load(2).astype(bf16)
+        q_all[rows, :] = q
+        k_all[rows, :] = k
+        v_all[rows, :] = values
+        keys = k.T
+        q = q * jnp.asarray(SCALE, bf16)
+        mine = pl.ds(pl.multiple_of(j * HD, HD), HD)
+        for start in range(0, seq, QB):
+            end = start + QB
+            scores = dot(keys[:end], q[:, start:end], ((1,), (0,))) + mask[:end, start:end]
+            top = jnp.max(scores, axis=0, keepdims=True)
+            expo = jnp.exp(scores - top)
+            total = jnp.sum(expo, axis=0, keepdims=True)
+            probs = (expo * (1.0 / total)).astype(bf16)
+            flat[mine, start:end] = dot(values[:, :end], probs, ((1,), (0,))).astype(bf16)
+            logs[pl.ds(head, 1), start:end] = top + jnp.log(total)
+
+    mixed[:, pair * 2 * HD : (pair + 1) * 2 * HD] = flat[...].T
+
+
+def build_mask(mask, seg_row, seg_col):
+    seq = mask.shape[0]
+
+    @pl.loop(0, seq // 32)
+    def _(i):
+        here = pl.ds(pl.multiple_of(i * 32, 32), 32)
+        key = lax.broadcasted_iota(jnp.int32, (32, seq), 0) + i * 32
+        query = lax.broadcasted_iota(jnp.int32, (32, seq), 1)
+        allowed = (key <= query) & (seg_col[here, :] == seg_row[...])
+        mask[here, :] = jnp.where(allowed, 0.0, NEG).astype(f32)
+
+
+def middle_kernel(
+    n,
+    lin_ref, bias_ref, cos_ref, sin_ref, seg_row, seg_col, x_ref, out_ref, small, gate_w, up_w, down_w, g_ref,
+    q_out, k_out, v_out, logs, mixed_out, att_out, second_out, gate_out, up_out, hidden_out, ffn_out, dgate_out, dup_out,
+    gate, up, down, second, near_send, near_recv, far_send, far_recv, attended,
+    send, recv, x_send, x_recv, local, stored, staged,
+):
+    place = Place(n)
+    t = place.t
+    rows, model = x_ref.shape
+    size, cols = gate_w.shape
+    seq = 4 * rows
+    width = out_ref.shape[1]
+    loads = [
+        pltpu.make_async_copy(gate_w, gate.at[place.me], local.at[0]),
+        pltpu.make_async_copy(up_w, up.at[place.me], local.at[1]),
+    ]
+    for load in loads:
+        load.start()
+    down[place.me] = down_w[...].T
+    place.barrier([place.up, place.down], [place.core, place.chip])
+    for load in loads:
+        load.wait()
+
+    half, quarter = size // 2, size // 4
+    lanes = [
+        [Lane(place, full, half * sub, half, way, send.at[2 * way + sub], recv.at[2 * way + sub]) for way, full in ((0, gate), (1, up))]
+        for sub in range(2)
+    ]
+    downs = [
+        [
+            Lane(place, down, half * way + quarter * sub, quarter, way, send.at[4 + 2 * way + sub], recv.at[4 + 2 * way + sub])
+            for way in range(2)
+        ]
+        for sub in range(2)
+    ]
+
+    def write(step):
+        gated, upped = place.owner(-step), place.owner(step)
+        return [
+            pltpu.make_async_copy(gate.at[gated], gate_out.at[gated], stored.at[0, step]),
+            pltpu.make_async_copy(up.at[upped], up_out.at[upped], stored.at[1, step]),
+        ]
+
+    def tick(kind, step, sub):
+        for lane in (downs if kind else lanes)[sub]:
+            if step > 1:
+                lane.arrive(step - 1)
+            if step < n:
+                lane.start(step)
+        if sub == 1 and not kind:
+            for copy in write(step - 1):
+                copy.start()
+
+    plan = [(0, step, sub) for step in range(1, n) for sub in range(2)]
+    plan += [(1, 1, 0), (1, 1, 1), (0, n, 0), (0, n, 1)]
+    plan += [(1, step, sub) for step in range(2, n + 1) for sub in range(2)]
+    plan = iter(plan)
+
+    def advance(count=1):
+        for _ in range(count):
+            tick(*next(plan))
+
+    swap = Exchange(x_send, x_recv)
+    near = [swap.copy(i, near_send.at[i], near_recv.at[i], place.core) for i in range(2)]
+    far = swap.copy(2, far_send, far_recv, place.chip)
+    to_chip = swap.copy(3, second.at[t], second.at[t], place.chip)
+    to_core = swap.copy(4, second.at[t], second.at[t], place.core)
+    relay = swap.copy(5, second.at[place.chip], second.at[place.chip], place.core)
+    copies = near + [far, to_chip, to_core, relay]
+
+    advance(2)
+
+    def attention(lin, mask, q_all, k_all, v_all, flat, mixed, out_t):
+        pairs = width // (2 * HD)
+        fetch = []
+        for part in range(3):
+            for pair in range(pairs):
+                at = pl.ds(part * width + pair * 2 * HD, 2 * HD)
+                fetch.append(pltpu.make_async_copy(lin_ref.at[at], lin.at[at], local.at[2 + part * pairs + pair]))
+        for pair in range(pairs):
+            for part in range(3):
+                fetch[part * pairs + pair].start()
+        weights = pltpu.make_async_copy(out_ref, out_t, local.at[2 + 3 * pairs])
+        weights.start()
+        build_mask(mask, seg_row, seg_col)
+        cosine, sine = cos_ref[...], sin_ref[...]
+        for pair in range(pairs):
+            for part in range(3):
+                fetch[part * pairs + pair].wait()
+            attend_pair(pair, lin, bias_ref, cosine, sine, mask, q_all, k_all, v_all, logs, flat, mixed)
+            advance()
+        keep = [
+            pltpu.make_async_copy(src, dst, local.at[3 + 3 * pairs + i])
+            for i, (src, dst) in enumerate(((q_all, q_out), (k_all, k_out), (v_all, v_out), (mixed, mixed_out)))
+        ]
+        for copy in keep:
+            copy.start()
+        weights.wait()
+
+        def project(block, j):
+            at = pl.ds(pl.multiple_of(block * rows, rows), rows)
+            return dot(mixed[at, :], out_t[j : j + 512, :], ((1,), (1,)))
+
+        for i, block in enumerate((place.cross, place.core)):
+            for j in range(0, model, 512):
+                near_send[i, :, j : j + 512] = project(block, j).astype(bf16)
+            near[i].start()
+        near[0].wait_recv()
+        for j in range(0, model, 512):
+            tile = slice(j, j + 512)
+            far_send[:, tile] = (project(place.chip, j) + near_recv[0, :, tile].astype(f32)).astype(bf16)
+        far.start()
+        own = pltpu.make_async_copy(x_ref, far_copy, local.at[7 + 3 * pairs])
+        own.start()
+        advance()
+        near[1].wait_recv()
+        own.wait()
+        for j in range(0, model, 512):
+            tile = slice(j, j + 512)
+            attended[:, tile] = far_copy[:, tile].astype(f32) + project(t, j) + near_recv[1, :, tile].astype(f32)
+        for copy in keep:
+            copy.wait()
+
+    far_copy = second.at[t]
+    pl.run_scoped(
+        attention,
+        pltpu.VMEM((3 * width, seq), f32),
+        pltpu.VMEM((seq, seq), f32),
+        pltpu.VMEM((width, seq), bf16),
+        pltpu.VMEM((width, seq), bf16),
+        pltpu.VMEM((width, seq), bf16),
+        pltpu.VMEM((2 * HD, seq), bf16),
+        pltpu.VMEM((seq, width), bf16),
+        pltpu.VMEM((model, width), bf16),
+    )
+    last = 7 + 3 * (width // (2 * HD))
+
+    def feed(gate_lin, up_lin, grad, hidden, g, stage):
+        g_load = pltpu.make_async_copy(g_ref, g, local.at[last + 1])
+        g_load.start()
+        gate_lin[...] = jnp.zeros_like(gate_lin)
+        up_lin[...] = jnp.zeros_like(up_lin)
+        grad[...] = jnp.zeros_like(grad)
+        count = small.shape[2]
+        gain = lane_vector(small, 2 * size // count, size // count)
+        shift = lane_vector(small, 3 * size // count, size // count)
+        advance(2)
+        far.wait_recv()
+
+        @pl.loop(0, rows // 16)
+        def _(i):
+            here = pl.ds(pl.multiple_of(i * 16, 16), 16)
+            value = attended[here, :] + far_recv[here, :].astype(f32)
+            attended[here, :] = value
+            second[t, here, :] = row_norm(value, gain, shift).astype(bf16)
+
+        to_chip.start()
+        to_core.start()
+        att_store = pltpu.make_async_copy(attended, att_out, local.at[last + 2])
+        att_store.start()
+
+        def add(block, low, high):
+            @pl.loop(low, high)
+            def _(step):
+                for full, total, whose in ((gate, gate_lin, place.owner(-step)), (up, up_lin, place.owner(step))):
+                    xs = second[block, :, pl.ds(pl.multiple_of(whose * size, size), size)]
+                    total[block] += dot(xs, full[whose], ((1,), (0,)))
+
+        advance()
+        ready = 5
+        add(t, 0, ready)
+        to_core.wait_recv()
+        advance()
+        add(place.core, 0, ready)
+        advance()
+        to_chip.wait_recv()
+        relay.start()
+        add(place.chip, 0, ready)
+        relay.wait_recv()
+        second_store = pltpu.make_async_copy(second, second_out, local.at[last + 3])
+        second_store.start()
+        advance()
+        add(place.cross, 0, ready)
+        every = lambda low, high: pl.loop(0, 4)(lambda block: add(block, low, high))
+        every(ready, n - 2)
+        advance(2)
+        advance()
+        every(n - 2, n - 1)
+        advance(2)
+        every(n - 1, n)
+
+        @pl.loop(0, 4 * rows // 16)
+        def _(i):
+            block = lax.div(i, rows // 16)
+            here = pl.ds(pl.multiple_of(lax.rem(i, rows // 16) * 16, 16), 16)
+            value = gate_lin[block, here, :]
+            hidden[block, here, :] = (value * jax.nn.sigmoid(value) * up_lin[block, here, :]).astype(bf16)
+
+        hidden_store = pltpu.make_async_copy(hidden, hidden_out, local.at[last + 4])
+        hidden_store.start()
+        g_load.wait()
+        stages = []
+
+        def use(whose):
+            number = len(stages)
+            slot = number % 2
+            if number >= 2:
+                stages[number - 2].wait()
+            at = pl.ds(pl.multiple_of(whose * size, size), size)
+
+            @pl.loop(0, 4)
+            def _(block):
+                grad[block] += dot(g[block, :, at], down[whose], ((1,), (0,)))
+                stage[slot, block] = dot(hidden[block], down[whose], ((1,), (1,))).astype(bf16)
+
+            stages.append(pltpu.make_async_copy(stage.at[slot], ffn_out.at[:, :, at], staged.at[number]))
+            stages[-1].start()
+
+        use(place.me)
+        for step in range(2, n + 1):
+            advance(2)
+            if step - 1 == n // 2:
+                use(place.owner(n // 2))
+            elif step - 1 > n // 2:
+                use(place.owner(step - 1))
+                use(place.owner(1 - step))
+        for lane in lanes[0] + lanes[1] + downs[0] + downs[1]:
+            lane.finish()
+        for step in range(n):
+            for copy in write(step):
+                copy.wait()
+
+        @pl.loop(0, 4 * rows // 16)
+        def _(i):
+            block = lax.div(i, rows // 16)
+            here = pl.ds(pl.multiple_of(lax.rem(i, rows // 16) * 16, 16), 16)
+            value = gate_lin[block, here, :]
+            sigma = jax.nn.sigmoid(value)
+            incoming = grad[block, here, :]
+            gate[block, here, :] = (incoming * up_lin[block, here, :] * sigma * (1.0 + value * (1.0 - sigma))).astype(bf16)
+            gate[4 + block, here, :] = (incoming * (value * sigma)).astype(bf16)
+
+        final = [
+            pltpu.make_async_copy(gate.at[pl.ds(0, 4)], dgate_out, local.at[last + 5]),
+            pltpu.make_async_copy(gate.at[pl.ds(4, 4)], dup_out, local.at[last + 6]),
+        ]
+        for copy in final:
+            copy.start()
+        for copy in final + stages[-2:] + [hidden_store, second_store, att_store]:
+            copy.wait()
+
+    pl.run_scoped(
+        feed,
+        pltpu.VMEM((4, rows, cols), f32),
+        pltpu.VMEM((4, rows, cols), f32),
+        pltpu.VMEM((4, rows, cols), f32),
+        pltpu.VMEM((4, rows, cols), bf16),
+        pltpu.VMEM((4, rows, model), bf16),
+        pltpu.VMEM((2, 4, rows, size), bf16),
+    )
+    for copy in copies:
+        copy.wait_send()
+
+
+def middle(lin, bias, cosine, sine, segments, x, out_t, small, gate, up, down, g, n):
+    rows, model = x.shape
+    size, cols = gate.shape
+    seq = 4 * rows
+    width = out_t.shape[1]
+    heads = width // HD
+    shape = jax.ShapeDtypeStruct
+    return pl.pallas_call(
+        lambda *refs: middle_kernel(n, *refs),
+        in_specs=[HBM] + [VMEM] * 5 + [HBM, HBM, VMEM, HBM, HBM, VMEM, HBM],
+        out_specs=[HBM, HBM, HBM, VMEM] + [HBM] * 9,
+        out_shape=[
+            shape((width, seq), bf16),
+            shape((width, seq), bf16),
+            shape((width, seq), bf16),
+            shape((heads, seq), f32),
+            shape((seq, width), bf16),
+            shape((rows, model), f32),
+            shape((4, rows, model), bf16),
+            shape((n, size, cols), bf16),
+            shape((n, size, cols), bf16),
+            shape((4, rows, cols), bf16),
+            shape((4, rows, model), bf16),
+            shape((4, rows, cols), bf16),
+            shape((4, rows, cols), bf16),
+        ],
+        scratch_shapes=[
+            pltpu.VMEM((n, size, cols), bf16),
+            pltpu.VMEM((n, size, cols), bf16),
+            pltpu.VMEM((n, size, cols), bf16),
+            pltpu.VMEM((4, rows, model), bf16),
+            pltpu.VMEM((2, rows, model), bf16),
+            pltpu.VMEM((2, rows, model), bf16),
+            pltpu.VMEM((rows, model), bf16),
+            pltpu.VMEM((rows, model), bf16),
+            pltpu.VMEM((rows, model), f32),
+            DMA((8, n - 1)),
+            DMA((8, n - 1)),
+            DMA((6,)),
+            DMA((6,)),
+            DMA((14 + 3 * width // (2 * HD),)),
+            DMA((2, n)),
+            DMA((n,)),
+        ],
+        compiler_params=pltpu.CompilerParams(collective_id=2, has_side_effects=True, vmem_limit_bytes=62 << 20),
+        cost_estimate=pl.CostEstimate(
+            flops=10 * seq * model * cols, bytes_accessed=60 << 20, transcendentals=heads * seq * seq
+        ),
+        name="middle",
+    )(
+        lin, bias[:, None], cosine, sine, segments[None, :], segments[:, None],
+        x, out_t, small, gate, up, down, g.reshape(4, rows, model),
+    )
+
 
 def norm_forward(rows):
     center = rows - jnp.mean(rows, axis=-1, keepdims=True)
@@ -605,10 +971,8 @@
         g_full = g_full.reshape(-1, model)
         qkv = qkv.reshape(model, -1)
         out_t = out_t.reshape(model, -1)
+        packed_small = small
         small = small.reshape(n, -1)[:, : 4 * part + 2 * heads * per]
-        gate, marks = ring.gather(gate_weight, after=lin)
-        up, marks = ring.gather(up_weight, pieces=2, after=marks[-2])
-        down_t, _ = ring.gather(down_weight.T, pieces=2, after=marks[-2])
     else:
         x_full = tensor_gather(layer_input)
         g_full = tensor_gather(out_grad, after=x_full)
@@ -630,7 +994,6 @@
         hat_full, _ = norm_forward(x_full.astype(f32))
         normed = (hat_full * gain_one + shift_one).astype(bf16)
         lin = dot(qkv, normed, ((0,), (1,)))
-    lin = lin + bias_lin[:, None]
 
     freqs = jnp.exp(-(2.0 / ROT) * jnp.arange(HALF).astype(f32) * math.log(10000.0))
     angles = freqs[:, None] * positions.astype(f32)[None, :]
@@ -638,23 +1001,34 @@
     index = jnp.arange(segments.shape[0], dtype=jnp.int32)
     allowed = (index[:, None] <= index[None, :]) & (segments[:, None] == segments[None, :])
     bias = jnp.where(allowed, 0.0, NEG).astype(f32)
-    mixed, q_rot, k_rot, v_heads, logs = attend_forward(lin, cosine, sine, bias)
     rows = layer_input.astype(f32)
-    attended = rows + tensor_scatter(dot(mixed, out_t, ((1,), (1,))))
-
-    hat_two, rstd_two = norm_forward(attended)
-    second = tensor_gather((hat_two * gain_two + shift_two).astype(bf16))
-    gate_lin = dot(second, gate, ((1,), (0,)))
-    up_lin = dot(second, up, ((1,), (0,)))
-    sigma = jax.nn.sigmoid(gate_lin)
-    activated = gate_lin * sigma
-    hidden = (activated * up_lin).astype(bf16)
-    layer_output = (attended + tensor_scatter(dot(hidden, down_t, ((1,), (1,))))).astype(bf16)
+    if ring.ring:
+        q_rot, k_rot, v_heads, logs, mixed, attended, second, gate, up, hidden, ffn, grad_gate, grad_up = middle(
+            lin, bias_lin, cosine, sine, segments, layer_input, out_t, packed_small, gate_weight, up_weight, down_weight, g_full, n
+        )
+        logs = logs.reshape(-1, 2, logs.shape[1])
+        second, gate, up = second.reshape(-1, model), gate.reshape(model, -1), up.reshape(model, -1)
+        hidden, ffn = hidden.reshape(second.shape[0], -1), ffn.reshape(-1, model)
+        grad_gate, grad_up = grad_gate.reshape(hidden.shape), grad_up.reshape(hidden.shape)
+        hat_two, rstd_two = norm_forward(attended)
+    else:
+        mixed, q_rot, k_rot, v_heads, logs = attend_forward(lin + bias_lin[:, None], cosine, sine, bias)
+        attended = rows + tensor_scatter(dot(mixed, out_t, ((1,), (1,))))
+
+        hat_two, rstd_two = norm_forward(attended)
+        second = tensor_gather((hat_two * gain_two + shift_two).astype(bf16))
+        gate_lin = dot(second, gate, ((1,), (0,)))
+        up_lin = dot(second, up, ((1,), (0,)))
+        sigma = jax.nn.sigmoid(gate_lin)
+        activated = gate_lin * sigma
+        hidden = (activated * up_lin).astype(bf16)
+        ffn = dot(hidden, down_t, ((1,), (1,)))
+        grad_hidden = dot(g_full, down_t, ((1,), (0,)))
+        grad_gate = (grad_hidden * up_lin * sigma * (1.0 + gate_lin * (1.0 - sigma))).astype(bf16)
+        grad_up = (grad_hidden * activated).astype(bf16)
+    layer_output = (attended + tensor_scatter(ffn.astype(f32))).astype(bf16)
 
     down_grad = dot(g_full, hidden, ((0,), (0,)))
-    grad_hidden = dot(g_full, down_t, ((1,), (0,)))
-    grad_gate = (grad_hidden * up_lin * sigma * (1.0 + gate_lin * (1.0 - sigma))).astype(bf16)
-    grad_up = (grad_hidden * activated).astype(bf16)
     grad_second = tensor_scatter(dot(grad_gate, gate, ((1,), (1,))) + dot(grad_up, up, ((1,), (1,))))
     gate_grad = dot(second, grad_gate, ((0,), (0,)))
     up_grad = dot(second, grad_up, ((0,), (0,)))

time: 850 us -> 773 us (0.909)
  Pallas kernels: 137 us -> 295 us
  starting transfers between devices: 188 us -> 95.4 us
  waiting for transfers between devices: 221 us -> 160 us
  matrix products: 124 us -> 74.7 us
  local copies, waits for them, and re-layouts: 96.2 us -> 74.5 us
    pallas_call x1, Pallas kernels: 22.1 us -> 180 us  [middle(): pl.pallas_call(lambda *refs: middle_kernel(n, *refs), in_specs=[HBM] + [V...]
    ppermute x70 -> x0, starting transfers between devices: 81.2 us -> none  [gather(): block = lax.ppermute(block, 'dp', self.down if way else self.up)]
    ppermute x70 -> x0, waiting for transfers between devices: 77.8 us -> none  [gather(): block = lax.ppermute(block, 'dp', self.down if way else self.up)]
    dot_general x14 -> x9, matrix products: 124 us -> 74.7 us  [dot(): lax.dot_general(a, b, ((dims[0], dims[1]), ((), ())), preferred_element_t...]
    dynamic_update_slice x73 -> x0, local copies, waits for them, and re-layouts: 20.3 us -> none  [the longest x70 19.2 us: gather(): full = lax.dynamic_update_slice(full, block[None], (whose, base, 0))]
    ppermute x84, waiting for transfers between devices: 112 us -> 120 us  [scatter(): got = lax.ppermute(moving.astype(bf16), 'dp', self.down if way else self.up)]
    unnamed x143 -> x99, local copies, waits for them, and re-layouts: 23 us -> 30.2 us
    ppermute x4 -> x3, waiting for transfers between devices: 23.4 us -> 28.2 us  [tensor_scatter(): lax.ppermute((block(2) + other.astype(f32)).astype(bf16), 'tensor', CHIP)]
  transfers between devices with their start and end apart: 177 -> 101, of which waited for: 96 -> 62; matrix products, arithmetic and copies ran while one was open for 26% -> 17% of each run, Pallas kernels for 5% -> 0%
where the time goes in v3:
time: 773 us; the launch traced here: 764 us
  Pallas kernels  295 us (38%)
  waiting for transfers between devices  160 us (21%)
  starting transfers between devices  95.4 us (12%)
  matrix products  74.7 us (10%)
  local copies, waits for them, and re-layouts  74.5 us (10%)
  other arithmetic  61.5 us (8%)
    pallas_call x1, Pallas kernels, middle(): pl.pallas_call(lambda *refs: middle_kernel(n, *refs), in_specs=[HBM] + [V...  180 us
    ppermute x84, waiting for transfers between devices, scatter(): got = lax.ppermute(moving.astype(bf16), 'dp', self.down if way else self.up)  120 us
    pallas_call x1, Pallas kernels, enter(): pl.pallas_call(kernel, in_specs=[HBM] * 5 + [VMEM, VMEM], out_specs=[HBM,...  92.5 us
    ppermute x84, starting transfers between devices, scatter(): got = lax.ppermute(moving.astype(bf16), 'dp', self.down if way else self.up)  85.2 us
    dot_general x9, matrix products, dot(): lax.dot_general(a, b, ((dims[0], dims[1]), ((), ())), preferred_element_t...  74.7 us
    unnamed x99, local copies, waits for them, and re-layouts  30.2 us
    ppermute x3, waiting for transfers between devices, tensor_scatter(): lax.ppermute((block(2) + other.astype(f32)).astype(bf16), 'tensor', CHIP)  28.2 us
    convert_element_type x30, other arithmetic, scatter(): got = lax.ppermute(moving.astype(bf16), 'dp', self.down if way else self.up)  25.3 us
  transfers between devices with their start and end apart: 101, of which 62 were waited for; matrix products, arithmetic and copies ran while one was open for 17% of the time, Pallas kernels for 0%

profile of v3, /device:TPU:0, one launch (start us, length us, event | category | flops | bytes accessed | tf_op | source)
XLA Modules:
  0.0 763.6 jit_solution(6214247760237236118)
XLA Ops:
  5.6 92.5 %enter.1 = (bf16[1024,2048]{1,0:T(8,128)(2,1)}, bf16[4,256,2048]{2,1,0:T(8,128)(2,1)}, bf16[8,256,1536]{2,1,0:T(8,128)(2,1)}, bf16[8,256,512]{2,1,0:T(8,128)(2,1...) custom-call(bf16[256,2048]{1,0:T(8,128)(2,1)} %refs_6_.1, bf16[256,2048]{1,0:T(8,128)(2,1)} %refs_1_.1, ...), custom_call_target="tpu_custom_call" | custom-call | flops 6442450944 | bytes 41943040 | tf_op jit(solution)/shard_map/enter/pallas_call | solution.py:519
  102.3 180.2 %middle.1 = (bf16[512,1024]{1,0:T(8,128)(2,1)}, bf16[512,1024]{1,0:T(8,128)(2,1)}, bf16[512,1024]{1,0:T(8,128)(2,1)}, f32[8,1024]{1,0:T(8,128)}, bf16[1024,512]{...) custom-call(f32[1536,1024]{1,0:T(8,128)} %get-tuple-element.39.refs_, ...), custom_call_target="tpu_custom_call" | custom-call | flops 29527900160 | bytes 62914560 | tf_op jit(solution)/shard_map/middle/pallas_call | solution.py:870
  282.5 11.6 %fusion.122 = f32[1024,2048]{1,0:T(8,128)} fusion(bf16[1024,1408]{1,0:T(8,128)(2,1)} %bitcast.540, bf16[2048,1408]{1,0:T(8,128)(2,1)} %bitcast.536), kind=kOutput, calls=%fused_computation.281 | convolution fusion | flops 5905580032 | bytes 17039360 | tf_op jit(solution)/shard_map/dot_general | solution.py:146
  294.0 10.8 %convolution_add_fusion = f32[1024,2048]{1,0:T(8,128)S(1)} fusion(f32[1024,2048]{1,0:T(8,128)} %fusion.122, bf16[1024,1408]{1,0:T(8,128)(2,1)} %bitcast.538, bf16[2048,1408]{1,0:T(8,128)(2,1)} %bitcast.535), kind=kOutput, calls=%fused_computation.3 | convolution fusion | flops 5907677184 | bytes 25427968 | tf_op jit(solution)/shard_map/dot_general | solution.py:146
  307.0 2.8 copy-done.16
  311.2 3.2 copy-done.5
  316.1 6.4 copy.55
  322.5 9.6 %fusion.125 = f32[8,256,1408]{2,1,0:T(8,128)S(1)} fusion(bf16[8,256,1024]{2,1,0:T(8,128)(2,1)} %bitcast.503, bf16[1024,1408,1]{1,0,2:T(8,128)(2,1)} %bitcast.541), kind=kOutput, calls=%fused_computation.284 | convolution fusion | flops 5905580032 | bytes 18612224 | tf_op jit(solution)/shard_map/dot_general | solution.py:146
  332.1 4.3 copy-done.9
  342.2 8.4 %fusion.126 = f32[8,256,1408]{2,1,0:T(8,128)S(1)} fusion(bf16[8,256,1024]{2,1,0:T(8,128)(2,1)} %bitcast.504, bf16[1024,1408,1]{1,0,2:T(8,128)(2,1)S(1)} %bitcast.539), kind=kOutput, calls=%fused_computation.285 | convolution fusion | flops 5905580032 | bytes 18612224 | tf_op jit(solution)/shard_map/dot_general | solution.py:146
  350.7 4.3 copy-done.12
  355.9 6.4 copy.56
  362.3 9.3 %fusion.127 = f32[8,256,1408]{2,1,0:T(8,128)S(1)} fusion(bf16[8,256,1024]{2,1,0:T(8,128)(2,1)} %bitcast.506, bf16[1024,1408,1]{1,0,2:T(8,128)(2,1)} %bitcast.537), kind=kOutput, calls=%fused_computation.286 | convolution fusion | flops 5905580032 | bytes 18612224 | tf_op jit(solution)/shard_map/dot_general | solution.py:146
  371.7 4.2 copy-done.10
  379.5 2.8 fusion.1.bias_ref
  385.9 6.9 collective-permute-done.73
  396.4 6.0 collective-permute-done.87
  406.1 4.9 collective-permute-done.60
  414.5 5.1 collective-permute-done.74
  423.7 5.3 collective-permute-done.88
  437.1 3.2 collective-permute-done.61
  444.3 3.8 collective-permute-done.75
  451.6 4.2 collective-permute-done.89
  458.0 5.5 collective-permute-done.62
  465.7 5.5 collective-permute-done.76
  474.8 4.2 collective-permute-done.90
  481.2 3.7 collective-permute-done.63
  491.7 5.5 collective-permute-done.91
  500.6 4.6 collective-permute-done.98
  508.6 3.1 collective-permute-done.5
  513.0 19.9 %collective-permute-done.2 = bf16[256,2048]{1,0:T(8,128)(2,1)S(1)} collective-permute-done((bf16[256,2048]{1,0:T(8,128)(2,1)S(1)}, bf16[256,2048]{1,0:T(8,128)(2,1)S(1)}, u32[]{:S(2)}, u32[]{:S(2)}) %collective-permute-start.2) | collective-permute-done | bytes 1048608 | tf_op jit(solution)/shard_map/ppermute | solution.py:121
  533.7 4.5 multiply_reduce_fusion
  553.2 3.3 collective-permute-done.65
  560.1 4.2 collective-permute-done.79
  579.1 3.4 convolution_convert_fusion.d_ref
  582.5 22.8 %attend_backward.1 = (bf16[512,1024]{1,0:T(8,128)(2,1)S(1)}, bf16[512,1024]{1,0:T(8,128)(2,1)S(1)}, bf16[512,1024]{1,0:T(8,128)(2,1)S(1)}, f32[4,128,128]{2,1,0:T(8,128)S(1)}) custom-call(bf16[512,1024]{1,0:T(8,128)(2,1)S(1)} %copy-done.2, bf16[512,1024]{1,0:T(8,128)(2,1)S(1)} %copy-done.3, bf16[512,1024]{1,0:T(8,128)(2,1)} %get-tuple-element.51.v_ref, ...), custom_call_target="tpu_custom_call" | custom-call | flops 5368709120 | bytes 31457280 | tf_op jit(solution)/shard_map/attend_backward/pallas_call | solution.py:249
  607.3 4.7 copy.59
  611.9 9.8 %fusion.123 = f32[4,256,2048]{2,1,0:T(8,128)S(1)} fusion(bf16[4,256,1536]{2,1,0:T(8,128)(2,1)} %bitcast.507, bf16[2048,1536,1]{1,0,2:T(8,128)(2,1)} %bitcast.534), kind=kOutput, calls=%fused_computation.282 | convolution fusion | flops 6442450944 | bytes 17825792 | tf_op jit(solution)/shard_map/dot_general | solution.py:146
  621.7 3.3 copy-done.17
  626.8 6.4 copy.60
  633.2 5.0 fusion.27
  640.5 6.8 fusion.124
  667.7 3.7 collective-permute-done.18
  712.5 2.9 fusion.13
  733.6 5.2 collective-permute-done.11
  738.8 3.5 fusion.11
  748.6 3.2 collective-permute-done.14
  752.7 3.1 collective-permute-done.15
  (384 shorter events, 217.5 us)
Async XLA Ops:
  306.5 124.7 %collective-permute-start.4 = (bf16[256,2048]{1,0:T(8,128)(2,1)}, bf16[256,2048]{1,0:T(8,128)(2,1)}, u32[]{:S(2)}, u32[]{:S(2)}) collective-permute-start(bf16[256,2048]{1,0:T(8,128)(2,1)} %get-tuple-element.206), channel_id=1, source_target_pairs={{0,1},{1,0},{2,3},{3,2},{4,5},{5,4},{6,7},{7,6},{8,9},{9,8},{10,11... | collective-permute-start | bytes 3145736 | tf_op jit(solution)/shard_map/ppermute | solution.py:119
  306.5 200.1 %collective-permute-start.3 = (bf16[256,2048]{1,0:T(8,128)(2,1)}, bf16[256,2048]{1,0:T(8,128)(2,1)}, u32[]{:S(2)}, u32[]{:S(2)}) collective-permute-start(bf16[256,2048]{1,0:T(8,128)(2,1)} %get-tuple-element.205), channel_id=1, source_target_pairs={{0,1},{1,0},{2,3},{3,2},{4,5},{5,4},{6,7},{7,6},{8,9},{9,8},{10,11... | collective-permute-start | bytes 3145736 | tf_op jit(solution)/shard_map/ppermute | solution.py:120
  316.1 118.3 %collective-permute-start.1 = (bf16[256,2048]{1,0:T(8,128)(2,1)}, bf16[256,2048]{1,0:T(8,128)(2,1)}, u32[]{:S(2)}, u32[]{:S(2)}) collective-permute-start(bf16[256,2048]{1,0:T(8,128)(2,1)} %get-tuple-element.208), channel_id=1, source_target_pairs={{0,1},{1,0},{2,3},{3,2},{4,5},{5,4},{6,7},{7,6},{8,9},{9,8},{10,11... | collective-permute-start | bytes 3145736 | tf_op jit(solution)/shard_map/ppermute | solution.py:119
  337.4 44.9 %collective-permute-start.59 = (bf16[128,1408]{1,0:T(8,128)(2,1)}, bf16[128,1408]{1,0:T(8,128)(2,1)S(1)}, u32[]{:S(2)}, u32[]{:S(2)}) collective-permute-start(bf16[128,1408]{1,0:T(8,128)(2,1)} %get-tuple-element.201), channel_id=1, source_target_pairs={{0,8},{8,16},{16,24},{24,28},{28,20},{20,12},{12,4},{4,0},{1,9},{9... | collective-permute-start | bytes 1081352 | tf_op jit(solution)/shard_map/ppermute | solution.py:84
  338.1 44.9 %collective-permute-start.66 = (bf16[128,1408]{1,0:T(8,128)(2,1)}, bf16[128,1408]{1,0:T(8,128)(2,1)}, u32[]{:S(2)}, u32[]{:S(2)}) collective-permute-start(bf16[128,1408]{1,0:T(8,128)(2,1)} %get-tuple-element.202), channel_id=1, source_target_pairs={{8,0},{16,8},{24,16},{28,24},{20,28},{12,20},{4,12},{0,4},{9,1},{1... | collective-permute-start | bytes 1081352 | tf_op jit(solution)/shard_map/ppermute | solution.py:84
  382.3 10.5 %collective-permute-start.73 = (bf16[128,1408]{1,0:T(8,128)(2,1)}, bf16[128,1408]{1,0:T(8,128)(2,1)S(1)}, u32[]{:S(2)}, u32[]{:S(2)}) collective-permute-start(bf16[128,1408]{1,0:T(8,128)(2,1)} %get-tuple-element.185), channel_id=1, source_target_pairs={{0,8},{8,16},{16,24},{24,28},{28,20},{20,12},{12,4},{4,0},{1,9},{9... | collective-permute-start | bytes 1081352 | tf_op jit(solution)/shard_map/ppermute | solution.py:84
  383.0 10.5 %collective-permute-start.80 = (bf16[128,1408]{1,0:T(8,128)(2,1)}, bf16[128,1408]{1,0:T(8,128)(2,1)S(1)}, u32[]{:S(2)}, u32[]{:S(2)}) collective-permute-start(bf16[128,1408]{1,0:T(8,128)(2,1)} %get-tuple-element.186), channel_id=1, source_target_pairs={{8,0},{16,8},{24,16},{28,24},{20,28},{12,20},{4,12},{0,4},{9,1},{1... | collective-permute-start | bytes 1081352 | tf_op jit(solution)/shard_map/ppermute | solution.py:84
  392.8 9.6 %collective-permute-start.87 = (bf16[128,1408]{1,0:T(8,128)(2,1)}, bf16[128,1408]{1,0:T(8,128)(2,1)S(1)}, u32[]{:S(2)}, u32[]{:S(2)}) collective-permute-start(bf16[128,1408]{1,0:T(8,128)(2,1)} %get-tuple-element.169), channel_id=1, source_target_pairs={{0,8},{8,16},{16,24},{24,28},{28,20},{20,12},{12,4},{4,0},{1,9},{9... | collective-permute-start | bytes 1081352 | tf_op jit(solution)/shard_map/ppermute | solution.py:84
  393.5 9.6 %collective-permute-start.94 = (bf16[128,1408]{1,0:T(8,128)(2,1)}, bf16[128,1408]{1,0:T(8,128)(2,1)S(1)}, u32[]{:S(2)}, u32[]{:S(2)}) collective-permute-start(bf16[128,1408]{1,0:T(8,128)(2,1)} %get-tuple-element.170), channel_id=1, source_target_pairs={{8,0},{16,8},{24,16},{28,24},{20,28},{12,20},{4,12},{0,4},{9,1},{1... | collective-permute-start | bytes 1081352 | tf_op jit(solution)/shard_map/ppermute | solution.py:84
  419.6 9.5 %collective-permute-start.88 = (bf16[128,1408]{1,0:T(8,128)(2,1)S(1)}, bf16[128,1408]{1,0:T(8,128)(2,1)S(1)}, u32[]{:S(2)}, u32[]{:S(2)}) collective-permute-start(bf16[128,1408]{1,0:T(8,128)(2,1)S(1)} %get-tuple-element.167), channel_id=1, source_target_pairs={{0,8},{8,16},{16,24},{24,28},{28,20},{20,12},{12,4},{4,0},{1,9},{9... | collective-permute-start | bytes 1081352 | tf_op jit(solution)/shard_map/ppermute | solution.py:84
  420.2 9.7 %collective-permute-start.95 = (bf16[128,1408]{1,0:T(8,128)(2,1)S(1)}, bf16[128,1408]{1,0:T(8,128)(2,1)S(1)}, u32[]{:S(2)}, u32[]{:S(2)}) collective-permute-start(bf16[128,1408]{1,0:T(8,128)(2,1)S(1)} %get-tuple-element.168), channel_id=1, source_target_pairs={{8,0},{16,8},{24,16},{28,24},{20,28},{12,20},{4,12},{0,4},{9,1},{1... | collective-permute-start | bytes 1081352 | tf_op jit(solution)/shard_map/ppermute | solution.py:84
  429.0 11.3 %collective-permute-start.61 = (bf16[128,1408]{1,0:T(8,128)(2,1)S(1)}, bf16[128,1408]{1,0:T(8,128)(2,1)S(1)}, u32[]{:S(2)}, u32[]{:S(2)}) collective-permute-start(bf16[128,1408]{1,0:T(8,128)(2,1)S(1)} %get-tuple-element.197), channel_id=1, source_target_pairs={{0,8},{8,16},{16,24},{24,28},{28,20},{20,12},{12,4},{4,0},{1,9},{9... | collective-permute-start | bytes 1081352 | tf_op jit(solution)/shard_map/ppermute | solution.py:84
  429.9 11.4 %collective-permute-start.68 = (bf16[128,1408]{1,0:T(8,128)(2,1)S(1)}, bf16[128,1408]{1,0:T(8,128)(2,1)S(1)}, u32[]{:S(2)}, u32[]{:S(2)}) collective-permute-start(bf16[128,1408]{1,0:T(8,128)(2,1)S(1)} %get-tuple-element.198), channel_id=1, source_target_pairs={{8,0},{16,8},{24,16},{28,24},{20,28},{12,20},{4,12},{0,4},{9,1},{1... | collective-permute-start | bytes 1081352 | tf_op jit(solution)/shard_map/ppermute | solution.py:84
  431.2 16.9 %collective-permute-start.75 = (bf16[128,1408]{1,0:T(8,128)(2,1)S(1)}, bf16[128,1408]{1,0:T(8,128)(2,1)S(1)}, u32[]{:S(2)}, u32[]{:S(2)}) collective-permute-start(bf16[128,1408]{1,0:T(8,128)(2,1)S(1)} %get-tuple-element.181), channel_id=1, source_target_pairs={{0,8},{8,16},{16,24},{24,28},{28,20},{20,12},{12,4},{4,0},{1,9},{9... | collective-permute-start | bytes 1081352 | tf_op jit(solution)/shard_map/ppermute | solution.py:84
  434.4 14.6 %collective-permute-start.82 = (bf16[128,1408]{1,0:T(8,128)(2,1)S(1)}, bf16[128,1408]{1,0:T(8,128)(2,1)S(1)}, u32[]{:S(2)}, u32[]{:S(2)}) collective-permute-start(bf16[128,1408]{1,0:T(8,128)(2,1)S(1)} %get-tuple-element.182), channel_id=1, source_target_pairs={{8,0},{16,8},{24,16},{28,24},{20,28},{12,20},{4,12},{0,4},{9,1},{1... | collective-permute-start | bytes 1081352 | tf_op jit(solution)/shard_map/ppermute | solution.py:84
  440.4 15.4 %collective-permute-start.89 = (bf16[128,1408]{1,0:T(8,128)(2,1)S(1)}, bf16[128,1408]{1,0:T(8,128)(2,1)S(1)}, u32[]{:S(2)}, u32[]{:S(2)}) collective-permute-start(bf16[128,1408]{1,0:T(8,128)(2,1)S(1)} %get-tuple-element.165), channel_id=1, source_target_pairs={{0,8},{8,16},{16,24},{24,28},{28,20},{20,12},{12,4},{4,0},{1,9},{9... | collective-permute-start | bytes 1081352 | tf_op jit(solution)/shard_map/ppermute | solution.py:84
  441.3 15.4 %collective-permute-start.96 = (bf16[128,1408]{1,0:T(8,128)(2,1)S(1)}, bf16[128,1408]{1,0:T(8,128)(2,1)S(1)}, u32[]{:S(2)}, u32[]{:S(2)}) collective-permute-start(bf16[128,1408]{1,0:T(8,128)(2,1)S(1)} %get-tuple-element.166), channel_id=1, source_target_pairs={{8,0},{16,8},{24,16},{28,24},{20,28},{12,20},{4,12},{0,4},{9,1},{1... | collective-permute-start | bytes 1081352 | tf_op jit(solution)/shard_map/ppermute | solution.py:84
  448.1 15.4 %collective-permute-start.62 = (bf16[128,1408]{1,0:T(8,128)(2,1)S(1)}, bf16[128,1408]{1,0:T(8,128)(2,1)S(1)}, u32[]{:S(2)}, u32[]{:S(2)}) collective-permute-start(bf16[128,1408]{1,0:T(8,128)(2,1)S(1)} %get-tuple-element.195), channel_id=1, source_target_pairs={{0,8},{8,16},{16,24},{24,28},{28,20},{20,12},{12,4},{4,0},{1,9},{9... | collective-permute-start | bytes 1081352 | tf_op jit(solution)/shard_map/ppermute | solution.py:84
  449.0 15.4 %collective-permute-start.69 = (bf16[128,1408]{1,0:T(8,128)(2,1)S(1)}, bf16[128,1408]{1,0:T(8,128)(2,1)S(1)}, u32[]{:S(2)}, u32[]{:S(2)}) collective-permute-start(bf16[128,1408]{1,0:T(8,128)(2,1)S(1)} %get-tuple-element.196), channel_id=1, source_target_pairs={{8,0},{16,8},{24,16},{28,24},{20,28},{12,20},{4,12},{0,4},{9,1},{1... | collective-permute-start | bytes 1081352 | tf_op jit(solution)/shard_map/ppermute | solution.py:84
  455.8 15.4 %collective-permute-start.76 = (bf16[128,1408]{1,0:T(8,128)(2,1)S(1)}, bf16[128,1408]{1,0:T(8,128)(2,1)S(1)}, u32[]{:S(2)}, u32[]{:S(2)}) collective-permute-start(bf16[128,1408]{1,0:T(8,128)(2,1)S(1)} %get-tuple-element.179), channel_id=1, source_target_pairs={{0,8},{8,16},{16,24},{24,28},{28,20},{20,12},{12,4},{4,0},{1,9},{9... | collective-permute-start | bytes 1081352 | tf_op jit(solution)/shard_map/ppermute | solution.py:84
  456.7 15.4 %collective-permute-start.83 = (bf16[128,1408]{1,0:T(8,128)(2,1)S(1)}, bf16[128,1408]{1,0:T(8,128)(2,1)S(1)}, u32[]{:S(2)}, u32[]{:S(2)}) collective-permute-start(bf16[128,1408]{1,0:T(8,128)(2,1)S(1)} %get-tuple-element.180), channel_id=1, source_target_pairs={{8,0},{16,8},{24,16},{28,24},{20,28},{12,20},{4,12},{0,4},{9,1},{1... | collective-permute-start | bytes 1081352 | tf_op jit(solution)/shard_map/ppermute | solution.py:84
  463.5 15.4 %collective-permute-start.90 = (bf16[128,1408]{1,0:T(8,128)(2,1)S(1)}, bf16[128,1408]{1,0:T(8,128)(2,1)S(1)}, u32[]{:S(2)}, u32[]{:S(2)}) collective-permute-start(bf16[128,1408]{1,0:T(8,128)(2,1)S(1)} %get-tuple-element.163), channel_id=1, source_target_pairs={{0,8},{8,16},{16,24},{24,28},{28,20},{20,12},{12,4},{4,0},{1,9},{9... | collective-permute-start | bytes 1081352 | tf_op jit(solution)/shard_map/ppermute | solution.py:84
  464.4 15.4 %collective-permute-start.97 = (bf16[128,1408]{1,0:T(8,128)(2,1)S(1)}, bf16[128,1408]{1,0:T(8,128)(2,1)S(1)}, u32[]{:S(2)}, u32[]{:S(2)}) collective-permute-start(bf16[128,1408]{1,0:T(8,128)(2,1)S(1)} %get-tuple-element.164), channel_id=1, source_target_pairs={{8,0},{16,8},{24,16},{28,24},{20,28},{12,20},{4,12},{0,4},{9,1},{1... | collective-permute-start | bytes 1081352 | tf_op jit(solution)/shard_map/ppermute | solution.py:84
  471.3 13.7 %collective-permute-start.63 = (bf16[128,1408]{1,0:T(8,128)(2,1)S(1)}, bf16[128,1408]{1,0:T(8,128)(2,1)S(1)}, u32[]{:S(2)}, u32[]{:S(2)}) collective-permute-start(bf16[128,1408]{1,0:T(8,128)(2,1)S(1)} %get-tuple-element.193), channel_id=1, source_target_pairs={{0,8},{8,16},{16,24},{24,28},{28,20},{20,12},{12,4},{4,0},{1,9},{9... | collective-permute-start | bytes 1081352 | tf_op jit(solution)/shard_map/ppermute | solution.py:84
  472.2 13.4 %collective-permute-start.70 = (bf16[128,1408]{1,0:T(8,128)(2,1)S(1)}, bf16[128,1408]{1,0:T(8,128)(2,1)S(1)}, u32[]{:S(2)}, u32[]{:S(2)}) collective-permute-start(bf16[128,1408]{1,0:T(8,128)(2,1)S(1)} %get-tuple-element.194), channel_id=1, source_target_pairs={{8,0},{16,8},{24,16},{28,24},{20,28},{12,20},{4,12},{0,4},{9,1},{1... | collective-permute-start | bytes 1081352 | tf_op jit(solution)/shard_map/ppermute | solution.py:84
  479.0 9.8 %collective-permute-start.77 = (bf16[128,1408]{1,0:T(8,128)(2,1)S(1)}, bf16[128,1408]{1,0:T(8,128)(2,1)S(1)}, u32[]{:S(2)}, u32[]{:S(2)}) collective-permute-start(bf16[128,1408]{1,0:T(8,128)(2,1)S(1)} %get-tuple-element.177), channel_id=1, source_target_pairs={{0,8},{8,16},{16,24},{24,28},{28,20},{20,12},{12,4},{4,0},{1,9},{9... | collective-permute-start | bytes 1081352 | tf_op jit(solution)/shard_map/ppermute | solution.py:84
  479.9 10.0 %collective-permute-start.84 = (bf16[128,1408]{1,0:T(8,128)(2,1)S(1)}, bf16[128,1408]{1,0:T(8,128)(2,1)S(1)}, u32[]{:S(2)}, u32[]{:S(2)}) collective-permute-start(bf16[128,1408]{1,0:T(8,128)(2,1)S(1)} %get-tuple-element.178), channel_id=1, source_target_pairs={{8,0},{16,8},{24,16},{28,24},{20,28},{12,20},{4,12},{0,4},{9,1},{1... | collective-permute-start | bytes 1081352 | tf_op jit(solution)/shard_map/ppermute | solution.py:84
  484.9 23.2 %collective-permute-start = (bf16[256,2048]{1,0:T(8,128)(2,1)S(1)}, bf16[256,2048]{1,0:T(8,128)(2,1)S(1)}, u32[]{:S(2)}, u32[]{:S(2)}) collective-permute-start(bf16[256,2048]{1,0:T(8,128)(2,1)S(1)} %copy-done.23), channel_id=1, source_target_pairs={{0,1},{1,0},{2,3},{3,2},{4,5},{5,4},{6,7},{7,6},{8,9},{9,8},{10,11... | collective-permute-start | bytes 3145736 | tf_op jit(solution)/shard_map/ppermute | solution.py:120
  485.6 26.0 %collective-permute-start.5 = (bf16[256,2048]{1,0:T(8,128)(2,1)S(1)}, bf16[256,2048]{1,0:T(8,128)(2,1)S(1)}, u32[]{:S(2)}, u32[]{:S(2)}) collective-permute-start(bf16[256,2048]{1,0:T(8,128)(2,1)S(1)} %fusion.15), channel_id=1, source_target_pairs={{0,2},{2,0},{1,3},{3,1},{4,6},{6,4},{5,7},{7,5},{8,10},{10,8},{9,1... | collective-permute-start | bytes 3145736 | tf_op jit(solution)/shard_map/ppermute | solution.py:121
  488.8 44.2 %collective-permute-start.2 = (bf16[256,2048]{1,0:T(8,128)(2,1)S(1)}, bf16[256,2048]{1,0:T(8,128)(2,1)S(1)}, u32[]{:S(2)}, u32[]{:S(2)}) collective-permute-start(bf16[256,2048]{1,0:T(8,128)(2,1)S(1)} %fusion.17), channel_id=1, source_target_pairs={{0,2},{2,0},{1,3},{3,1},{4,6},{6,4},{5,7},{7,5},{8,10},{10,8},{9,1... | collective-permute-start | bytes 3145736 | tf_op jit(solution)/shard_map/ppermute | solution.py:121
  505.2 36.3 %collective-permute-start.64 = (bf16[128,1408]{1,0:T(8,128)(2,1)}, bf16[128,1408]{1,0:T(8,128)(2,1)}, u32[]{:S(2)}, u32[]{:S(2)}) collective-permute-start(bf16[128,1408]{1,0:T(8,128)(2,1)} %get-tuple-element.191), channel_id=1, source_target_pairs={{0,8},{8,16},{16,24},{24,28},{28,20},{20,12},{12,4},{4,0},{1,9},{9... | collective-permute-start | bytes 1081352 | tf_op jit(solution)/shard_map/ppermute | solution.py:84
  506.6 36.3 %collective-permute-start.71 = (bf16[128,1408]{1,0:T(8,128)(2,1)}, bf16[128,1408]{1,0:T(8,128)(2,1)}, u32[]{:S(2)}, u32[]{:S(2)}) collective-permute-start(bf16[128,1408]{1,0:T(8,128)(2,1)} %get-tuple-element.192), channel_id=1, source_target_pairs={{8,0},{16,8},{24,16},{28,24},{20,28},{12,20},{4,12},{0,4},{9,1},{1... | collective-permute-start | bytes 1081352 | tf_op jit(solution)/shard_map/ppermute | solution.py:84
  508.1 36.0 %collective-permute-start.78 = (bf16[128,1408]{1,0:T(8,128)(2,1)}, bf16[128,1408]{1,0:T(8,128)(2,1)}, u32[]{:S(2)}, u32[]{:S(2)}) collective-permute-start(bf16[128,1408]{1,0:T(8,128)(2,1)} %get-tuple-element.175), channel_id=1, source_target_pairs={{0,8},{8,16},{16,24},{24,28},{28,20},{20,12},{12,4},{4,0},{1,9},{9... | collective-permute-start | bytes 1081352 | tf_op jit(solution)/shard_map/ppermute | solution.py:84
  511.6 33.7 %collective-permute-start.85 = (bf16[128,1408]{1,0:T(8,128)(2,1)}, bf16[128,1408]{1,0:T(8,128)(2,1)}, u32[]{:S(2)}, u32[]{:S(2)}) collective-permute-start(bf16[128,1408]{1,0:T(8,128)(2,1)} %get-tuple-element.176), channel_id=1, source_target_pairs={{8,0},{16,8},{24,16},{28,24},{20,28},{12,20},{4,12},{0,4},{9,1},{1... | collective-permute-start | bytes 1081352 | tf_op jit(solution)/shard_map/ppermute | solution.py:84
  533.0 14.9 %collective-permute-start.92 = (bf16[128,1408]{1,0:T(8,128)(2,1)}, bf16[128,1408]{1,0:T(8,128)(2,1)}, u32[]{:S(2)}, u32[]{:S(2)}) collective-permute-start(bf16[128,1408]{1,0:T(8,128)(2,1)} %get-tuple-element.159), channel_id=1, source_target_pairs={{0,8},{8,16},{16,24},{24,28},{28,20},{20,12},{12,4},{4,0},{1,9},{9... | collective-permute-start | bytes 1081352 | tf_op jit(solution)/shard_map/ppermute | solution.py:84
  542.9 34.5 %collective-permute-start.6 = (bf16[256,2048]{1,0:T(8,128)(2,1)S(1)}, bf16[256,2048]{1,0:T(8,128)(2,1)S(1)}, u32[]{:S(2)}, u32[]{:S(2)}) collective-permute-start(bf16[256,2048]{1,0:T(8,128)(2,1)S(1)} %get-tuple-element.120), channel_id=1, source_target_pairs={{0,1},{1,0},{2,3},{3,2},{4,5},{5,4},{6,7},{7,6},{8,9},{9,8},{10,11... | collective-permute-start | bytes 3145736 | tf_op jit(solution)/shard_map/ppermute | solution.py:101
  544.2 32.0 %collective-permute-start.7 = (bf16[256,2048]{1,0:T(8,128)(2,1)S(1)}, bf16[256,2048]{1,0:T(8,128)(2,1)S(1)}, u32[]{:S(2)}, u32[]{:S(2)}) collective-permute-start(bf16[256,2048]{1,0:T(8,128)(2,1)S(1)} %get-tuple-element.120), channel_id=1, source_target_pairs={{0,2},{2,0},{1,3},{3,1},{4,6},{6,4},{5,7},{7,5},{8,10},{10,8},{9,1... | collective-permute-start | bytes 3145736 | tf_op jit(solution)/shard_map/ppermute | solution.py:100
  545.3 11.2 %collective-permute-start.65 = (bf16[128,1408]{1,0:T(8,128)(2,1)S(1)}, bf16[128,1408]{1,0:T(8,128)(2,1)S(1)}, u32[]{:S(2)}, u32[]{:S(2)}) collective-permute-start(bf16[128,1408]{1,0:T(8,128)(2,1)S(1)} %get-tuple-element.189), channel_id=1, source_target_pairs={{0,8},{8,16},{16,24},{24,28},{28,20},{20,12},{12,4},{4,0},{1,9},{9... | collective-permute-start | bytes 1081352 | tf_op jit(solution)/shard_map/ppermute | solution.py:84
  547.8 10.5 %collective-permute-start.72 = (bf16[128,1408]{1,0:T(8,128)(2,1)S(1)}, bf16[128,1408]{1,0:T(8,128)(2,1)S(1)}, u32[]{:S(2)}, u32[]{:S(2)}) collective-permute-start(bf16[128,1408]{1,0:T(8,128)(2,1)S(1)} %get-tuple-element.190), channel_id=1, source_target_pairs={{8,0},{16,8},{24,16},{28,24},{20,28},{12,20},{4,12},{0,4},{9,1},{1... | collective-permute-start | bytes 1081352 | tf_op jit(solution)/shard_map/ppermute | solution.py:84
  550.2 14.1 %collective-permute-start.79 = (bf16[128,1408]{1,0:T(8,128)(2,1)S(1)}, bf16[128,1408]{1,0:T(8,128)(2,1)S(1)}, u32[]{:S(2)}, u32[]{:S(2)}) collective-permute-start(bf16[128,1408]{1,0:T(8,128)(2,1)S(1)} %get-tuple-element.173), channel_id=1, source_target_pairs={{0,8},{8,16},{16,24},{24,28},{28,20},{20,12},{12,4},{4,0},{1,9},{9... | collective-permute-start | bytes 1081352 | tf_op jit(solution)/shard_map/ppermute | solution.py:84
  556.6 9.5 %collective-permute-start.86 = (bf16[128,1408]{1,0:T(8,128)(2,1)S(1)}, bf16[128,1408]{1,0:T(8,128)(2,1)S(1)}, u32[]{:S(2)}, u32[]{:S(2)}) collective-permute-start(bf16[128,1408]{1,0:T(8,128)(2,1)S(1)} %get-tuple-element.174), channel_id=1, source_target_pairs={{8,0},{16,8},{24,16},{28,24},{20,28},{12,20},{4,12},{0,4},{9,1},{1... | collective-permute-start | bytes 1081352 | tf_op jit(solution)/shard_map/ppermute | solution.py:84
  558.4 13.0 %collective-permute-start.93 = (bf16[128,1408]{1,0:T(8,128)(2,1)S(1)}, bf16[128,1408]{1,0:T(8,128)(2,1)S(1)}, u32[]{:S(2)}, u32[]{:S(2)}) collective-permute-start(bf16[128,1408]{1,0:T(8,128)(2,1)S(1)} %get-tuple-element.157), channel_id=1, source_target_pairs={{0,8},{8,16},{16,24},{24,28},{28,20},{20,12},{12,4},{4,0},{1,9},{9... | collective-permute-start | bytes 1081352 | tf_op jit(solution)/shard_map/ppermute | solution.py:84
  564.3 9.3 %collective-permute-start.100 = (bf16[128,1408]{1,0:T(8,128)(2,1)S(1)}, bf16[128,1408]{1,0:T(8,128)(2,1)S(1)}, u32[]{:S(2)}, u32[]{:S(2)}) collective-permute-start(bf16[128,1408]{1,0:T(8,128)(2,1)S(1)} %get-tuple-element.158), channel_id=1, source_target_pairs={{8,0},{16,8},{24,16},{28,24},{20,28},{12,20},{4,12},{0,4},{9,1},{1... | collective-permute-start | bytes 1081352 | tf_op jit(solution)/shard_map/ppermute | solution.py:84
  626.3 85.1 %collective-permute-start.10 = (bf16[256,2048]{1,0:T(8,128)(2,1)S(1)}, bf16[256,2048]{1,0:T(8,128)(2,1)S(1)}, u32[]{:S(2)}, u32[]{:S(2)}) collective-permute-start(bf16[256,2048]{1,0:T(8,128)(2,1)S(1)} %get-tuple-element.204), channel_id=1, source_target_pairs={{0,1},{1,0},{2,3},{3,2},{4,5},{5,4},{6,7},{7,6},{8,9},{9,8},{10,11... | collective-permute-start | bytes 3145736 | tf_op jit(solution)/shard_map/ppermute | solution.py:119
  638.2 9.1 %collective-permute-start.45 = (bf16[128,512]{1,0:T(8,128)(2,1)S(1)}, bf16[128,512]{1,0:T(8,128)(2,1)S(1)}, u32[]{:S(2)}, u32[]{:S(2)}) collective-permute-start(bf16[128,512]{1,0:T(8,128)(2,1)S(1)} %get-tuple-element.223), channel_id=1, source_target_pairs={{0,8},{8,16},{16,24},{24,28},{28,20},{20,12},{12,4},{4,0},{1,9},{9... | collective-permute-start | bytes 393224 | tf_op jit(solution)/shard_map/ppermute | solution.py:84
  666.5 9.5 %collective-permute-start.25 = (bf16[64,1536]{1,0:T(8,128)(2,1)S(1)}, bf16[64,1536]{1,0:T(8,128)(2,1)S(1)}, u32[]{:S(2)}, u32[]{:S(2)}) collective-permute-start(bf16[64,1536]{1,0:T(8,128)(2,1)S(1)} %get-tuple-element.150), channel_id=1, source_target_pairs={{8,0},{16,8},{24,16},{28,24},{20,28},{12,20},{4,12},{0,4},{9,1},{1... | collective-permute-start | bytes 589832 | tf_op jit(solution)/shard_map/ppermute | solution.py:84
  705.0 28.6 %collective-permute-start.9 = (bf16[256,2048]{1,0:T(8,128)(2,1)}, bf16[256,2048]{1,0:T(8,128)(2,1)}, u32[]{:S(2)}, u32[]{:S(2)}) collective-permute-start(bf16[256,2048]{1,0:T(8,128)(2,1)} %get-tuple-element.203), channel_id=1, source_target_pairs={{0,1},{1,0},{2,3},{3,2},{4,5},{5,4},{6,7},{7,6},{8,9},{9,8},{10,11... | collective-permute-start | bytes 3145736 | tf_op jit(solution)/shard_map/ppermute | solution.py:120
  718.4 20.4 %collective-permute-start.11 = (bf16[256,2048]{1,0:T(8,128)(2,1)}, bf16[256,2048]{1,0:T(8,128)(2,1)}, u32[]{:S(2)}, u32[]{:S(2)}) collective-permute-start(bf16[256,2048]{1,0:T(8,128)(2,1)} %fusion.13), channel_id=1, source_target_pairs={{0,2},{2,0},{1,3},{3,1},{4,6},{6,4},{5,7},{7,5},{8,10},{10,8},{9,1... | collective-permute-start | bytes 3145736 | tf_op jit(solution)/shard_map/ppermute | solution.py:121
  (98 other events, 1384.4 us)

commit v4 on v3

--- a/solution.py
+++ b/solution.py
@@ -914,6 +914,353 @@
         x, out_t, small, gate, up, down, g.reshape(4, rows, model),
     )
 
+class Sum:
+    def __init__(self, place, slots, way, send, recv):
+        self.place, self.slots, self.way, self.send, self.recv = place, slots, way, send, recv
+
+    def whose(self, step):
+        return self.place.owner(1 + step if self.way else -1 - step)
+
+    def copy(self, step):
+        return pltpu.make_async_remote_copy(
+            src_ref=self.slots.at[step - 1],
+            dst_ref=self.slots.at[step],
+            send_sem=self.send.at[step - 1],
+            recv_sem=self.recv.at[step - 1],
+            device_id={"dp": self.place.down if self.way else self.place.up},
+            device_id_type=MESH,
+        )
+
+    def tick(self, step, left, right, final):
+        if step > 0:
+            self.copy(step).wait_recv()
+        cols = self.slots.shape[2]
+        for low in range(0, cols, 512):
+            tile = slice(low, min(low + 512, cols))
+            part = dot(left, right(tile), ((1,), (0,)))
+            if step > 0:
+                part = part + self.slots[step, :, tile].astype(f32)
+            if step == self.place.n - 1:
+                final(tile, part)
+            else:
+                self.slots[step, :, tile] = part.astype(bf16)
+        if step < self.place.n - 1:
+            self.copy(step + 1).start()
+
+    def finish(self):
+        for step in range(1, self.place.n):
+            self.copy(step).wait_send()
+
+
+def columns_of(left, whose, size, way):
+    half = size // 2
+    return left[:, pl.ds(pl.multiple_of(whose * size + way * half, half), half)].T
+
+
+def retreat_pair(pair, q_all, k_all, v_all, d_all, logs, cosine, sine, mask, dk_acc, dv_acc, tmp, vec):
+    width, seq = q_all.shape
+
+    @pl.loop(0, 2)
+    def _(j):
+        head = pair * 2 + j
+        rows = pl.ds(pl.multiple_of(head * HD, HD), HD)
+        q, k, v, d = q_all[rows, :], k_all[rows, :], v_all[rows, :], d_all[rows, :]
+        keys, values = k.T, v.T
+        q_small = q * jnp.asarray(SCALE, bf16)
+        dk_acc[...] = jnp.zeros_like(dk_acc)
+        dv_acc[...] = jnp.zeros_like(dv_acc)
+        cols = []
+        for start in range(0, seq, QB):
+            end = start + QB
+            here = slice(start, end)
+            scores = dot(keys[:end], q_small[:, here], ((1,), (0,))) + mask[:end, here]
+            probs = jnp.exp(scores - logs[pl.ds(head, 1), here])
+            grad = dot(values[:end], d[:, here], ((1,), (0,)))
+            both = probs * grad
+            inner = jnp.sum(both, axis=0, keepdims=True)
+            grad = ((both - probs * inner) * SCALE).astype(bf16)
+            probs = probs.astype(bf16)
+            cols.append(dot(k[:, :end], grad, ((1,), (0,))))
+            dk_acc[:, :end] += dot(q[:, here], grad, ((1,), (1,)))
+            dv_acc[:, :end] += dot(d[:, here], probs, ((1,), (1,)))
+        dq = rotate(jnp.concatenate(cols, axis=1), cosine, sine, -1.0)
+        dk = rotate(dk_acc[...], cosine, sine, -1.0)
+        dv = dv_acc[...]
+        mine = pl.ds(pl.multiple_of(j * HD, HD), HD)
+        for part, (out, value) in enumerate(((q_all, dq), (k_all, dk), (v_all, dv))):
+            out[rows, :] = value.astype(bf16)
+            lanes = value[:, :128]
+            for i in range(128, seq, 128):
+                lanes = lanes + value[:, i : i + 128]
+            tmp[part, mine, :] = lanes
+
+    for part in range(3):
+        at = part * width + pair * 2 * HD
+        vec[4:5, at : at + 2 * HD] = jnp.sum(tmp[part].T, axis=0, keepdims=True)
+
+
+def back_kernel(
+    n,
+    dgate_ref, dup_ref, hidden_ref, second_ref, g_ref, gate_ref, up_ref, att_ref, small, out_ref,
+    q_ref, k_ref, v_ref, logs, cos_ref, sin_ref, seg_row, seg_col,
+    down_sum, gate_sum, up_sum, datt_out, resid_out, dlin_out, vec,
+    slots, g, second, hidden, dgate, dup, near_send, near_recv, far_send, far_recv, datt, acc,
+    send, recv, x_send, x_recv, local,
+):
+    place = Place(n)
+    t = place.t
+    rows, model = att_ref.shape
+    size, cols = gate_ref.shape[1:]
+    seq, width = 4 * rows, out_ref.shape[1]
+    loads = [
+        pltpu.make_async_copy(src, dst, local.at[i])
+        for i, (src, dst) in enumerate(
+            ((g_ref, g), (hidden_ref, hidden), (second_ref, second), (dgate_ref, dgate), (dup_ref, dup))
+        )
+    ]
+    for load in loads:
+        load.start()
+    place.barrier([place.up, place.down], [place.core, place.chip])
+
+    lanes = [[Sum(place, slots.at[2 * i + way], way, send.at[2 * i + way], recv.at[2 * i + way]) for way in range(2)] for i in range(3)]
+    sources = ((g, hidden), (second, dgate), (second, dup))
+    sums = (down_sum, gate_sum, up_sum)
+
+    def stored(i):
+        return pltpu.make_async_copy(datt.at[:, pl.ds(0, cols)], sums[i], local.at[6 + i])
+
+    def tick(step, i):
+        left, right = sources[i]
+        if step == n - 1:
+            (stored(i - 1) if i else datt_copy()).wait()
+        for lane in lanes[i]:
+
+            def final(tile, total):
+                datt[lane.way * size // 2 : (lane.way + 1) * size // 2, tile] = total
+
+            lane.tick(step, columns_of(left, lane.whose(step), size, lane.way), lambda tile: right[:, tile], final)
+        if step == n - 1:
+            stored(i).start()
+
+    plan = iter([(step, i) for step in range(n) for i in range(3)])
+
+    def advance(count=1):
+        for _ in range(count):
+            tick(*next(plan))
+
+    def datt_copy():
+        return pltpu.make_async_copy(datt, datt_out, local.at[9])
+
+    swap = Exchange(x_send, x_recv)
+    near = [swap.copy(i, near_send.at[i], near_recv.at[i], place.core) for i in range(2)]
+    far = swap.copy(2, far_send, far_recv, place.chip)
+    to_chip = swap.copy(3, far_send, resid_out.at[t], place.chip)
+    to_core = swap.copy(4, far_send, resid_out.at[t], place.core)
+    relay = swap.copy(5, resid_out.at[place.chip], resid_out.at[place.chip], place.core)
+    keep = pltpu.make_async_copy(far_send, resid_out.at[t], local.at[10])
+    own = pl.ds(pl.multiple_of(t * rows, rows), rows)
+
+    def feed(gate, up):
+        weights = [
+            pltpu.make_async_copy(gate_ref, gate, local.at[11]),
+            pltpu.make_async_copy(up_ref, up, local.at[12]),
+        ]
+        for copy in weights:
+            copy.start()
+        loads[0].wait()
+        loads[1].wait()
+        advance()
+        loads[2].wait()
+        loads[3].wait()
+        advance()
+        loads[4].wait()
+        advance()
+        for copy in weights:
+            copy.wait()
+
+        def product(block, j):
+            at = pl.ds(pl.multiple_of(block * rows, rows), rows)
+            return dot(dgate[at, :], gate[j], ((1,), (1,))) + dot(dup[at, :], up[j], ((1,), (1,)))
+
+        for i, block in enumerate((place.cross, place.core)):
+            for j in range(n):
+                near_send[i, :, j * size : (j + 1) * size] = product(block, j).astype(bf16)
+            near[i].start()
+            advance()
+        near[0].wait_recv()
+        for j in range(n):
+            tile = slice(j * size, (j + 1) * size)
+            far_send[:, tile] = (product(place.chip, j) + near_recv[0, :, tile].astype(f32)).astype(bf16)
+        far.start()
+        advance()
+        near[1].wait_recv()
+        for j in range(n):
+            tile = slice(j * size, (j + 1) * size)
+            datt[:, tile] = product(t, j) + near_recv[1, :, tile].astype(f32)
+        advance()
+
+    pl.run_scoped(feed, pltpu.VMEM((n, size, cols), bf16), pltpu.VMEM((n, size, cols), bf16))
+
+    def attention(attended, mask, q_all, k_all, v_all, d_all, out_t, dk_acc, dv_acc, tmp):
+        load_attended = pltpu.make_async_copy(att_ref, attended, local.at[5])
+        load_attended.start()
+        fetch = [
+            pltpu.make_async_copy(src, dst, local.at[13 + i])
+            for i, (src, dst) in enumerate(((out_ref, out_t), (q_ref, q_all), (k_ref, k_all), (v_ref, v_all)))
+        ]
+        for copy in fetch:
+            copy.start()
+        build_mask(mask, seg_row, seg_col)
+        count = small.shape[2]
+        gain = lane_vector(small, 2 * size // count, size // count)
+        acc[...] = jnp.zeros_like(acc)
+        advance(1)
+        far.wait_recv()
+        far.wait_send()
+        load_attended.wait()
+
+        @pl.loop(0, rows // 16)
+        def _(i):
+            here = pl.ds(pl.multiple_of(i * 16, 16), 16)
+            value = attended[here, :]
+            center = value - jnp.mean(value, axis=1, keepdims=True)
+            rstd = lax.rsqrt(jnp.mean(center * center, axis=1, keepdims=True) + EPS)
+            hat = center * rstd
+            incoming = datt[here, :] + far_recv[here, :].astype(f32)
+            acc[0] += incoming * hat
+            acc[1] += incoming
+            scaled = incoming * gain
+            back = rstd * (
+                scaled - jnp.mean(scaled, axis=1, keepdims=True) - hat * jnp.mean(scaled * hat, axis=1, keepdims=True)
+            )
+            whole = g[pl.ds(pl.multiple_of(t * rows + i * 16, 16), 16), :].astype(f32) + back
+            datt[here, :] = whole
+            far_send[here, :] = whole.astype(bf16)
+
+        to_chip.start()
+        to_core.start()
+        keep.start()
+        datt_copy().start()
+        vec[...] = jnp.zeros_like(vec)
+        vec[2:3, :] = jnp.sum(acc[0], axis=0, keepdims=True)
+        vec[3:4, :] = jnp.sum(acc[1], axis=0, keepdims=True)
+        for copy in near:
+            copy.wait_send()
+        fetch[0].wait()
+
+        def mix(block, source):
+            value = dot(source[...], out_t[...], ((1,), (0,))).astype(bf16)
+            d_all[:, pl.ds(pl.multiple_of(block * rows, rows), rows)] = value.T
+
+        def bring(block, slot, number):
+            return pltpu.make_async_copy(resid_out.at[block], near_send.at[slot], local.at[number])
+
+        mix(t, far_send)
+        advance()
+        to_core.wait_recv()
+        first = bring(place.core, 0, 17)
+        first.start()
+        first.wait()
+        mix(place.core, near_send.at[0])
+        advance(2)
+        to_chip.wait_recv()
+        relay.start()
+        second_block = bring(place.chip, 1, 18)
+        second_block.start()
+        second_block.wait()
+        mix(place.chip, near_send.at[1])
+        relay.wait_recv()
+        third = bring(place.cross, 0, 19)
+        third.start()
+        third.wait()
+        mix(place.cross, near_send.at[0])
+        for copy in fetch[1:]:
+            copy.wait()
+        cosine, sine = cos_ref[...], sin_ref[...]
+        for pair in range(width // (2 * HD)):
+            advance()
+            retreat_pair(pair, q_all, k_all, v_all, d_all, logs, cosine, sine, mask, dk_acc, dv_acc, tmp, vec)
+        final = [
+            pltpu.make_async_copy(src, dlin_out.at[pl.ds(i * width, width)], local.at[20 + i])
+            for i, src in enumerate((q_all, k_all, v_all))
+        ]
+        for copy in final:
+            copy.start()
+        advance(2)
+        for copy in final:
+            copy.wait()
+
+    pl.run_scoped(
+        attention,
+        pltpu.VMEM((rows, model), f32),
+        pltpu.VMEM((seq, seq), f32),
+        pltpu.VMEM((width, seq), bf16),
+        pltpu.VMEM((width, seq), bf16),
+        pltpu.VMEM((width, seq), bf16),
+        pltpu.VMEM((width, seq), bf16),
+        pltpu.VMEM((model, width), bf16),
+        pltpu.VMEM((HD, seq), f32),
+        pltpu.VMEM((HD, seq), f32),
+        pltpu.VMEM((3, 2 * HD, 128), f32),
+    )
+    for step in plan:
+        tick(*step)
+    for pair in lanes:
+        for lane in pair:
+            lane.finish()
+    for copy in (to_chip, to_core, relay):
+        copy.wait_send()
+    keep.wait()
+    stored(2).wait()
+
+
+def back(dgate, dup, hidden, second, g, gate, up, attended, small, out_t, q, k, v, logs, cosine, sine, segments, n):
+    rows, model = attended.shape
+    size, cols = model // n, hidden.shape[1]
+    seq, width = 4 * rows, out_t.shape[1]
+    shape = jax.ShapeDtypeStruct
+    return pl.pallas_call(
+        lambda *refs: back_kernel(n, *refs),
+        in_specs=[HBM] * 8 + [VMEM] + [HBM] * 4 + [VMEM] * 5,
+        out_specs=[HBM] * 6 + [VMEM],
+        out_shape=[
+            shape((size, cols), f32),
+            shape((size, cols), f32),
+            shape((size, cols), f32),
+            shape((rows, model), f32),
+            shape((4, rows, model), bf16),
+            shape((3 * width, seq), bf16),
+            shape((8, model), f32),
+        ],
+        scratch_shapes=[
+            pltpu.VMEM((6, n, size // 2, cols), bf16),
+            pltpu.VMEM((seq, model), bf16),
+            pltpu.VMEM((seq, model), bf16),
+            pltpu.VMEM((seq, cols), bf16),
+            pltpu.VMEM((seq, cols), bf16),
+            pltpu.VMEM((seq, cols), bf16),
+            pltpu.VMEM((2, rows, model), bf16),
+            pltpu.VMEM((2, rows, model), bf16),
+            pltpu.VMEM((rows, model), bf16),
+            pltpu.VMEM((rows, model), bf16),
+            pltpu.VMEM((rows, model), f32),
+            pltpu.VMEM((2, 16, model), f32),
+            DMA((6, n - 1)),
+            DMA((6, n - 1)),
+            DMA((6,)),
+            DMA((6,)),
+            DMA((23,)),
+        ],
+        compiler_params=pltpu.CompilerParams(collective_id=3, has_side_effects=True, vmem_limit_bytes=62 << 20),
+        cost_estimate=pl.CostEstimate(
+            flops=14 * seq * model * cols, bytes_accessed=60 << 20, transcendentals=width // HD * seq * seq
+        ),
+        name="back",
+    )(
+        dgate, dup, hidden, second, g, gate.reshape(n, size, cols), up.reshape(n, size, cols), attended, small, out_t,
+        q, k, v, logs, cosine, sine, segments[None, :], segments[:, None],
+    )
+
 
 def norm_forward(rows):
     center = rows - jnp.mean(rows, axis=-1, keepdims=True)
@@ -1006,11 +1353,9 @@
         q_rot, k_rot, v_heads, logs, mixed, attended, second, gate, up, hidden, ffn, grad_gate, grad_up = middle(
             lin, bias_lin, cosine, sine, segments, layer_input, out_t, packed_small, gate_weight, up_weight, down_weight, g_full, n
         )
-        logs = logs.reshape(-1, 2, logs.shape[1])
         second, gate, up = second.reshape(-1, model), gate.reshape(model, -1), up.reshape(model, -1)
         hidden, ffn = hidden.reshape(second.shape[0], -1), ffn.reshape(-1, model)
         grad_gate, grad_up = grad_gate.reshape(hidden.shape), grad_up.reshape(hidden.shape)
-        hat_two, rstd_two = norm_forward(attended)
     else:
         mixed, q_rot, k_rot, v_heads, logs = attend_forward(lin + bias_lin[:, None], cosine, sine, bias)
         attended = rows + tensor_scatter(dot(mixed, out_t, ((1,), (1,))))
@@ -1028,37 +1373,41 @@
         grad_up = (grad_hidden * activated).astype(bf16)
     layer_output = (attended + tensor_scatter(ffn.astype(f32))).astype(bf16)
 
-    down_grad = dot(g_full, hidden, ((0,), (0,)))
-    grad_second = tensor_scatter(dot(grad_gate, gate, ((1,), (1,))) + dot(grad_up, up, ((1,), (1,))))
-    gate_grad = dot(second, grad_gate, ((0,), (0,)))
-    up_grad = dot(second, grad_up, ((0,), (0,)))
-    down_sum = ring.scatter(down_grad).T
-    gate_sum = ring.scatter(gate_grad)
-    up_sum = ring.scatter(up_grad)
-    grad_attended = out_grad.astype(f32) + norm_backward(grad_second, hat_two, rstd_two, gain_two)
-    residual = tensor_gather(grad_attended.astype(bf16))
-
-    grad_mixed = dot(out_t, residual, ((0,), (1,))).astype(bf16)
+    if ring.ring:
+        down_sum, gate_sum, up_sum, grad_attended, residual, grad_lin, vec = back(
+            grad_gate, grad_up, hidden, second, g_full, gate, up, attended, packed_small, out_t,
+            q_rot, k_rot, v_heads, logs, cosine, sine, segments, n
+        )
+        down_sum, residual = down_sum.T, residual.reshape(-1, model)
+        sums = vec[4, : 3 * width].reshape(3, width).T
+        second_vectors = vec[2:4]
+    else:
+        down_grad = dot(g_full, hidden, ((0,), (0,)))
+        grad_second = tensor_scatter(dot(grad_gate, gate, ((1,), (1,))) + dot(grad_up, up, ((1,), (1,))))
+        gate_grad = dot(second, grad_gate, ((0,), (0,)))
+        up_grad = dot(second, grad_up, ((0,), (0,)))
+        down_sum = ring.scatter(down_grad).T
+        gate_sum = ring.scatter(gate_grad)
+        up_sum = ring.scatter(up_grad)
+        grad_attended = out_grad.astype(f32) + norm_backward(grad_second, hat_two, rstd_two, gain_two)
+        residual = tensor_gather(grad_attended.astype(bf16))
+        grad_mixed = dot(out_t, residual, ((0,), (1,))).astype(bf16)
+        dq, dk, dv, sums = attend_backward(q_rot, k_rot, v_heads, grad_mixed, logs, cosine, sine, bias)
+        grad_lin = jnp.concatenate([dq, dk, dv], axis=0)
+        sums = sums.reshape(width, 128)[:, :3]
+        second_vectors = jnp.stack([jnp.sum(grad_second * hat_two, axis=0), jnp.sum(grad_second, axis=0)])
+
     out_grad_t = dot(residual, mixed, ((0,), (0,)))
     out_sum = ring.scatter(out_grad_t).T
-    dq, dk, dv, sums = attend_backward(q_rot, k_rot, v_heads, grad_mixed, logs, cosine, sine, bias)
-    grad_lin = jnp.concatenate([dq, dk, dv], axis=0)
     qkv_grad = dot(normed, grad_lin, ((0,), (1,)))
     qkv_sum = ring.scatter(qkv_grad, pieces=2)
     grad_first = tensor_scatter(dot(grad_lin, qkv, ((0,), (1,))))
     hat_one, rstd_one = norm_forward(rows)
     input_grad = grad_attended + norm_backward(grad_first, hat_one, rstd_one, gain_one)
 
-    vectors = jnp.stack(
-        [
-            jnp.sum(grad_first * hat_one, axis=0),
-            jnp.sum(grad_first, axis=0),
-            jnp.sum(grad_second * hat_two, axis=0),
-            jnp.sum(grad_second, axis=0),
-        ]
-    )
+    vectors = jnp.stack([jnp.sum(grad_first * hat_one, axis=0), jnp.sum(grad_first, axis=0)])
+    vectors = jnp.concatenate([vectors, second_vectors])
     vectors = sum_all(vectors, ["tensor"])
-    sums = sums.reshape(width, 128)[:, :3]
     packed = sum_all(jnp.concatenate([vectors.reshape(-1), sums.reshape(-1)]), ["dp"])
     each = model // (n * lax.axis_size("tensor"))
     at = ring.me * lax.axis_size("tensor") + lax.axis_index("tensor")

time: 773 us -> 686 us (0.89)
  Pallas kernels: 295 us -> 449 us
  waiting for transfers between devices: 160 us -> 58.7 us
  matrix products: 74.7 us -> 27.3 us
  starting transfers between devices: 95.4 us -> 50.4 us
  other arithmetic: 61.5 us -> 37.8 us
  local copies, waits for them, and re-layouts: 74.5 us -> 51.8 us
    pallas_call x1, Pallas kernels: 22.8 us -> 172 us  [back(): pl.pallas_call(lambda *refs: back_kernel(n, *refs), in_specs=[HBM] * 8 +...]
    ppermute x84 -> x42, waiting for transfers between devices: 120 us -> 27.4 us  [scatter(): got = lax.ppermute(moving.astype(bf16), 'dp', self.down if way else self.up)]
    dot_general x9 -> x3, matrix products: 74.7 us -> 27.3 us  [dot(): lax.dot_general(a, b, ((dims[0], dims[1]), ((), ())), preferred_element_t...]
    ppermute x84 -> x42, starting transfers between devices: 85.2 us -> 43.1 us  [scatter(): got = lax.ppermute(moving.astype(bf16), 'dp', self.down if way else self.up)]
    ppermute x3 -> x2, waiting for transfers between devices: 28.2 us -> 13.5 us  [tensor_scatter(): lax.ppermute((block(2) + other.astype(f32)).astype(bf16), 'tensor', CHIP)]
    unnamed x99 -> x54, local copies, waits for them, and re-layouts: 30.2 us -> 16.8 us
    dot_general x4 -> x2, local copies, waits for them, and re-layouts: 23.9 us -> 11.2 us  [dot(): lax.dot_general(a, b, ((dims[0], dims[1]), ((), ())), preferred_element_t...]
    convert_element_type x30 -> x12, other arithmetic: 25.3 us -> 13.2 us  [scatter(): got = lax.ppermute(moving.astype(bf16), 'dp', self.down if way else self.up)]
  transfers between devices with their start and end apart: 101 -> 53, of which waited for: 62 -> 27; matrix products, arithmetic and copies ran while one was open for 17% -> 11% of each run, Pallas kernels for 0% -> 0%
where the time goes in v4:
time: 686 us; the launch traced here: 676 us
  Pallas kernels  449 us (65%)
  waiting for transfers between devices  58.7 us (9%)
  local copies, waits for them, and re-layouts  51.8 us (8%)
  starting transfers between devices  50.4 us (7%)
  other arithmetic  37.8 us (6%)
  matrix products  27.3 us (4%)
    pallas_call x1, Pallas kernels, middle(): pl.pallas_call(lambda *refs: middle_kernel(n, *refs), in_specs=[HBM] + [V...  185 us
    pallas_call x1, Pallas kernels, back(): pl.pallas_call(lambda *refs: back_kernel(n, *refs), in_specs=[HBM] * 8 +...  172 us
    pallas_call x1, Pallas kernels, enter(): pl.pallas_call(kernel, in_specs=[HBM] * 5 + [VMEM, VMEM], out_specs=[HBM,...  92.4 us
    ppermute x42, starting transfers between devices, scatter(): got = lax.ppermute(moving.astype(bf16), 'dp', self.down if way else self.up)  43.1 us
    ppermute x42, waiting for transfers between devices, scatter(): got = lax.ppermute(moving.astype(bf16), 'dp', self.down if way else self.up)  27.4 us
    dot_general x3, matrix products, dot(): lax.dot_general(a, b, ((dims[0], dims[1]), ((), ())), preferred_element_t...  27.3 us
    ppermute x5, waiting for transfers between devices, sum_all(): lax.ppermute(vector, axis, [(i, i ^ step) for i in range(n)])  17.7 us
    unnamed x54, local copies, waits for them, and re-layouts  16.8 us
  transfers between devices with their start and end apart: 53, of which 27 were waited for; matrix products, arithmetic and copies ran while one was open for 11% of the time, Pallas kernels for 0%

profile of v4, /device:TPU:0, one launch (start us, length us, event | category | flops | bytes accessed | tf_op | source)
XLA Modules:
  0.0 676.5 jit_solution(13673684783759717229)
XLA Ops:
  2.2 2.8 concatenate.18
  5.6 92.4 %enter.1 = (bf16[1024,2048]{1,0:T(8,128)(2,1)}, bf16[4,256,2048]{2,1,0:T(8,128)(2,1)}, bf16[8,256,1536]{2,1,0:T(8,128)(2,1)}, bf16[8,256,512]{2,1,0:T(8,128)(2,1...) custom-call(bf16[256,2048]{1,0:T(8,128)(2,1)} %refs_6_.1, bf16[256,2048]{1,0:T(8,128)(2,1)} %refs_1_.1, ...), custom_call_target="tpu_custom_call" | custom-call | flops 6442450944 | bytes 41943040 | tf_op jit(solution)/shard_map/enter/pallas_call | solution.py:519
  102.8 184.5 %middle.1 = (bf16[512,1024]{1,0:T(8,128)(2,1)}, bf16[512,1024]{1,0:T(8,128)(2,1)}, bf16[512,1024]{1,0:T(8,128)(2,1)}, f32[8,1024]{1,0:T(8,128)}, bf16[1024,512]{...) custom-call(f32[1536,1024]{1,0:T(8,128)} %get-tuple-element.42.refs_, ...), custom_call_target="tpu_custom_call" | custom-call | flops 29527900160 | bytes 62914560 | tf_op jit(solution)/shard_map/middle/pallas_call | solution.py:870
  287.3 172.4 %back.1 = (f32[256,1408]{1,0:T(8,128)}, f32[256,1408]{1,0:T(8,128)}, f32[256,1408]{1,0:T(8,128)}, f32[256,2048]{1,0:T(8,128)}, bf16[4,256,2048]{2,1,0:T(8,128)(2...) custom-call(bf16[1024,1408]{1,0:T(8,128)(2,1)} %bitcast.294, bf16[1024,1408]{1,0:T(8,128)(2,1)} %bitcast.295, ...), custom_call_target="tpu_custom_call" | custom-call | flops 41339060224 | bytes 62914560 | tf_op jit(solution)/shard_map/back/pallas_call | solution.py:1222
  459.7 4.7 copy.58
  464.4 10.1 %fusion.73 = f32[4,256,2048]{2,1,0:T(8,128)S(1)} fusion(bf16[4,256,1536]{2,1,0:T(8,128)(2,1)} %bitcast.270, bf16[2048,1536,1]{1,0,2:T(8,128)(2,1)} %bitcast.290), kind=kOutput, calls=%fused_computation.158 | convolution fusion | flops 6442450944 | bytes 17825792 | tf_op jit(solution)/shard_map/dot_general | solution.py:146
  474.6 3.4 copy-done.2
  479.2 12.5 %fusion.74 = f32[2048,1536]{1,0:T(8,128)} fusion(bf16[1024,2048]{1,0:T(8,128)(2,1)} %get-tuple-element.62, bf16[1536,1024]{1,0:T(8,128)(2,1)} %get-tuple-element.59), kind=kOutput, calls=%fused_computation.159 | convolution fusion | flops 6442450944 | bytes 19922944 | tf_op jit(solution)/shard_map/dot_general | solution.py:146
  491.7 2.2 fusion.59
  496.0 6.5 copy.55
  502.5 4.6 fusion.21
  507.1 1.9 copy-done.3
  514.7 1.4 slice_reduce_fusion.1
  516.2 3.3 convert_element_type.368
  519.4 3.2 copy-done
  522.7 1.6 fusion.17
  526.8 1.5 copy.53
  528.3 1.7 reshape.171
  530.1 1.5 copy.57
  534.0 1.4 collective-permute-start.40
  536.6 2.4 collective-permute-done.40
  541.1 1.5 fusion.57
  546.1 1.4 collective-permute-done.18
  547.4 1.7 fusion.46
  553.3 2.5 collective-permute-done.12
  558.3 1.4 collective-permute-done.19
  559.8 1.6 fusion.45
  565.5 1.5 collective-permute-done.13
  569.6 1.4 collective-permute-done.20
  571.1 1.6 fusion.44
  576.8 1.5 collective-permute-done.14
  582.3 1.6 fusion.43
  588.0 1.5 collective-permute-done.15
  593.5 1.6 fusion.42
  599.3 1.5 collective-permute-done.16
  603.9 2.3 fusion.41
  607.3 3.2 fusion.11
  615.7 2.2 fusion.13
  618.0 1.7 collective-permute-done.38
  621.8 1.6 bitcast_add_fusion.25
  623.4 13.5 %collective-permute-done.5 = bf16[256,2048]{1,0:T(8,128)(2,1)} collective-permute-done((bf16[256,2048]{1,0:T(8,128)(2,1)}, bf16[256,2048]{1,0:T(8,128)(2,1)}, u32[]{:S(2)}, u32[]{:S(2)}) %collective-permute-start.5) | collective-permute-done | bytes 1048608 | tf_op jit(solution)/shard_map/ppermute | solution.py:121
  636.9 3.5 fusion.9
  644.2 12.9 %collective-permute-done.7 = f32[4,2048]{1,0:T(4,128)S(1)} collective-permute-done((f32[4,2048]{1,0:T(4,128)S(1)}, f32[4,2048]{1,0:T(4,128)S(1)}, u32[]{:S(2)}, u32[]{:S(2)}) %collective-permute-start.7) | collective-permute-done | bytes 32800 | tf_op jit(solution)/shard_map/ppermute | solution.py:133
  658.1 3.1 collective-permute-done.8
  662.4 2.1 fusion.8
  665.2 1.7 collective-permute-start.10
  666.9 3.2 fusion.16
  672.6 2.6 copy.67
  (194 shorter events, 83.3 us)
Async XLA Ops:
  479.2 128.1 %collective-permute-start.4 = (bf16[256,2048]{1,0:T(8,128)(2,1)}, bf16[256,2048]{1,0:T(8,128)(2,1)}, u32[]{:S(2)}, u32[]{:S(2)}) collective-permute-start(bf16[256,2048]{1,0:T(8,128)(2,1)} %get-tuple-element.154), channel_id=1, source_target_pairs={{0,1},{1,0},{2,3},{3,2},{4,5},{5,4},{6,7},{7,6},{8,9},{9,8},{10,11... | collective-permute-start | bytes 3145736 | tf_op jit(solution)/shard_map/ppermute | solution.py:119
  494.0 48.6 %collective-permute-start.11 = (bf16[64,1536]{1,0:T(8,128)(2,1)}, bf16[64,1536]{1,0:T(8,128)(2,1)}, u32[]{:S(2)}, u32[]{:S(2)}) collective-permute-start(bf16[64,1536]{1,0:T(8,128)(2,1)} %get-tuple-element.149), channel_id=1, source_target_pairs={{0,8},{8,16},{16,24},{24,28},{28,20},{20,12},{12,4},{4,0},{1,9},{9... | collective-permute-start | bytes 589832 | tf_op jit(solution)/shard_map/ppermute | solution.py:84
  495.3 48.4 %collective-permute-start.32 = (bf16[64,1536]{1,0:T(8,128)(2,1)}, bf16[64,1536]{1,0:T(8,128)(2,1)}, u32[]{:S(2)}, u32[]{:S(2)}) collective-permute-start(bf16[64,1536]{1,0:T(8,128)(2,1)} %get-tuple-element.150), channel_id=1, source_target_pairs={{8,0},{16,8},{24,16},{28,24},{20,28},{12,20},{4,12},{0,4},{9,1},{1... | collective-permute-start | bytes 589832 | tf_op jit(solution)/shard_map/ppermute | solution.py:84
  509.8 23.0 %collective-permute-start.39 = (bf16[128,512]{1,0:T(8,128)(2,1)}, bf16[128,512]{1,0:T(8,128)(2,1)}, u32[]{:S(2)}, u32[]{:S(2)}) collective-permute-start(bf16[128,512]{1,0:T(8,128)(2,1)} %get-tuple-element.171), channel_id=1, source_target_pairs={{0,8},{8,16},{16,24},{24,28},{28,20},{20,12},{12,4},{4,0},{1,9},{9... | collective-permute-start | bytes 393224 | tf_op jit(solution)/shard_map/ppermute | solution.py:84
  511.1 21.7 %collective-permute-start.46 = (bf16[128,512]{1,0:T(8,128)(2,1)}, bf16[128,512]{1,0:T(8,128)(2,1)}, u32[]{:S(2)}, u32[]{:S(2)}) collective-permute-start(bf16[128,512]{1,0:T(8,128)(2,1)} %get-tuple-element.172), channel_id=1, source_target_pairs={{8,0},{16,8},{24,16},{28,24},{20,28},{12,20},{4,12},{0,4},{9,1},{1... | collective-permute-start | bytes 393224 | tf_op jit(solution)/shard_map/ppermute | solution.py:84
  534.0 5.0 collective-permute-start.40
  539.0 7.1 %collective-permute-start.25 = (bf16[64,1536]{1,0:T(8,128)(2,1)S(1)}, bf16[64,1536]{1,0:T(8,128)(2,1)S(1)}, u32[]{:S(2)}, u32[]{:S(2)}) collective-permute-start(bf16[64,1536]{1,0:T(8,128)(2,1)S(1)} %copy-done.11), channel_id=1, source_target_pairs={{0,8},{8,16},{16,24},{24,28},{28,20},{20,12},{12,4},{4,0},{1,9},{9... | collective-permute-start | bytes 589832 | tf_op jit(solution)/shard_map/ppermute | solution.py:84
  540.3 7.1 %collective-permute-start.18 = (bf16[64,1536]{1,0:T(8,128)(2,1)S(1)}, bf16[64,1536]{1,0:T(8,128)(2,1)S(1)}, u32[]{:S(2)}, u32[]{:S(2)}) collective-permute-start(bf16[64,1536]{1,0:T(8,128)(2,1)S(1)} %copy-done.10), channel_id=1, source_target_pairs={{8,0},{16,8},{24,16},{28,24},{20,28},{12,20},{4,12},{0,4},{9,1},{1... | collective-permute-start | bytes 589832 | tf_op jit(solution)/shard_map/ppermute | solution.py:84
  542.6 8.6 %collective-permute-start.41 = (bf16[128,512]{1,0:T(8,128)(2,1)S(1)}, bf16[128,512]{1,0:T(8,128)(2,1)S(1)}, u32[]{:S(2)}, u32[]{:S(2)}) collective-permute-start(bf16[128,512]{1,0:T(8,128)(2,1)S(1)} %get-tuple-element.167), channel_id=1, source_target_pairs={{0,8},{8,16},{16,24},{24,28},{28,20},{20,12},{12,4},{4,0},{1,9},{9... | collective-permute-start | bytes 393224 | tf_op jit(solution)/shard_map/ppermute | solution.py:84
  543.7 8.2 %collective-permute-start.48 = (bf16[128,512]{1,0:T(8,128)(2,1)S(1)}, bf16[128,512]{1,0:T(8,128)(2,1)S(1)}, u32[]{:S(2)}, u32[]{:S(2)}) collective-permute-start(bf16[128,512]{1,0:T(8,128)(2,1)S(1)} %get-tuple-element.168), channel_id=1, source_target_pairs={{8,0},{16,8},{24,16},{28,24},{20,28},{12,20},{4,12},{0,4},{9,1},{1... | collective-permute-start | bytes 393224 | tf_op jit(solution)/shard_map/ppermute | solution.py:84
  549.1 6.7 collective-permute-start.12
  549.9 6.9 %collective-permute-start.33 = (bf16[64,1536]{1,0:T(8,128)(2,1)S(1)}, bf16[64,1536]{1,0:T(8,128)(2,1)S(1)}, u32[]{:S(2)}, u32[]{:S(2)}) collective-permute-start(bf16[64,1536]{1,0:T(8,128)(2,1)S(1)} %get-tuple-element.146), channel_id=1, source_target_pairs={{8,0},{16,8},{24,16},{28,24},{20,28},{12,20},{4,12},{0,4},{9,1},{1... | collective-permute-start | bytes 589832 | tf_op jit(solution)/shard_map/ppermute | solution.py:84
  551.2 7.1 %collective-permute-start.26 = (bf16[64,1536]{1,0:T(8,128)(2,1)S(1)}, bf16[64,1536]{1,0:T(8,128)(2,1)S(1)}, u32[]{:S(2)}, u32[]{:S(2)}) collective-permute-start(bf16[64,1536]{1,0:T(8,128)(2,1)S(1)} %get-tuple-element.147), channel_id=1, source_target_pairs={{0,8},{8,16},{16,24},{24,28},{28,20},{20,12},{12,4},{4,0},{1,9},{9... | collective-permute-start | bytes 589832 | tf_op jit(solution)/shard_map/ppermute | solution.py:84
  552.0 7.8 %collective-permute-start.19 = (bf16[64,1536]{1,0:T(8,128)(2,1)S(1)}, bf16[64,1536]{1,0:T(8,128)(2,1)S(1)}, u32[]{:S(2)}, u32[]{:S(2)}) collective-permute-start(bf16[64,1536]{1,0:T(8,128)(2,1)S(1)} %get-tuple-element.148), channel_id=1, source_target_pairs={{8,0},{16,8},{24,16},{28,24},{20,28},{12,20},{4,12},{0,4},{9,1},{1... | collective-permute-start | bytes 589832 | tf_op jit(solution)/shard_map/ppermute | solution.py:84
  555.8 7.6 %collective-permute-start.42 = (bf16[128,512]{1,0:T(8,128)(2,1)S(1)}, bf16[128,512]{1,0:T(8,128)(2,1)S(1)}, u32[]{:S(2)}, u32[]{:S(2)}) collective-permute-start(bf16[128,512]{1,0:T(8,128)(2,1)S(1)} %get-tuple-element.165), channel_id=1, source_target_pairs={{0,8},{8,16},{16,24},{24,28},{28,20},{20,12},{12,4},{4,0},{1,9},{9... | collective-permute-start | bytes 393224 | tf_op jit(solution)/shard_map/ppermute | solution.py:84
  556.9 7.6 %collective-permute-start.49 = (bf16[128,512]{1,0:T(8,128)(2,1)S(1)}, bf16[128,512]{1,0:T(8,128)(2,1)S(1)}, u32[]{:S(2)}, u32[]{:S(2)}) collective-permute-start(bf16[128,512]{1,0:T(8,128)(2,1)S(1)} %get-tuple-element.166), channel_id=1, source_target_pairs={{8,0},{16,8},{24,16},{28,24},{20,28},{12,20},{4,12},{0,4},{9,1},{1... | collective-permute-start | bytes 393224 | tf_op jit(solution)/shard_map/ppermute | solution.py:84
  561.3 5.7 collective-permute-start.13
  562.5 5.7 collective-permute-start.34
  563.4 6.2 collective-permute-start.27
  564.5 6.5 collective-permute-start.20
  567.1 7.7 %collective-permute-start.43 = (bf16[128,512]{1,0:T(8,128)(2,1)S(1)}, bf16[128,512]{1,0:T(8,128)(2,1)S(1)}, u32[]{:S(2)}, u32[]{:S(2)}) collective-permute-start(bf16[128,512]{1,0:T(8,128)(2,1)S(1)} %get-tuple-element.163), channel_id=1, source_target_pairs={{0,8},{8,16},{16,24},{24,28},{28,20},{20,12},{12,4},{4,0},{1,9},{9... | collective-permute-start | bytes 393224 | tf_op jit(solution)/shard_map/ppermute | solution.py:84
  568.2 7.6 %collective-permute-start.50 = (bf16[128,512]{1,0:T(8,128)(2,1)S(1)}, bf16[128,512]{1,0:T(8,128)(2,1)S(1)}, u32[]{:S(2)}, u32[]{:S(2)}) collective-permute-start(bf16[128,512]{1,0:T(8,128)(2,1)S(1)} %get-tuple-element.164), channel_id=1, source_target_pairs={{8,0},{16,8},{24,16},{28,24},{20,28},{12,20},{4,12},{0,4},{9,1},{1... | collective-permute-start | bytes 393224 | tf_op jit(solution)/shard_map/ppermute | solution.py:84
  572.6 5.7 collective-permute-start.14
  573.7 5.7 collective-permute-start.35
  574.7 6.2 collective-permute-start.28
  575.7 6.5 collective-permute-start.21
  578.3 7.6 %collective-permute-start.44 = (bf16[128,512]{1,0:T(8,128)(2,1)S(1)}, bf16[128,512]{1,0:T(8,128)(2,1)S(1)}, u32[]{:S(2)}, u32[]{:S(2)}) collective-permute-start(bf16[128,512]{1,0:T(8,128)(2,1)S(1)} %get-tuple-element.161), channel_id=1, source_target_pairs={{0,8},{8,16},{16,24},{24,28},{28,20},{20,12},{12,4},{4,0},{1,9},{9... | collective-permute-start | bytes 393224 | tf_op jit(solution)/shard_map/ppermute | solution.py:84
  579.4 7.5 %collective-permute-start.51 = (bf16[128,512]{1,0:T(8,128)(2,1)S(1)}, bf16[128,512]{1,0:T(8,128)(2,1)S(1)}, u32[]{:S(2)}, u32[]{:S(2)}) collective-permute-start(bf16[128,512]{1,0:T(8,128)(2,1)S(1)} %get-tuple-element.162), channel_id=1, source_target_pairs={{8,0},{16,8},{24,16},{28,24},{20,28},{12,20},{4,12},{0,4},{9,1},{1... | collective-permute-start | bytes 393224 | tf_op jit(solution)/shard_map/ppermute | solution.py:84
  583.9 5.7 collective-permute-start.15
  584.8 5.8 collective-permute-start.36
  585.9 6.2 collective-permute-start.29
  586.9 6.6 collective-permute-start.22
  589.6 7.6 %collective-permute-start.45 = (bf16[128,512]{1,0:T(8,128)(2,1)S(1)}, bf16[128,512]{1,0:T(8,128)(2,1)S(1)}, u32[]{:S(2)}, u32[]{:S(2)}) collective-permute-start(bf16[128,512]{1,0:T(8,128)(2,1)S(1)} %get-tuple-element.159), channel_id=1, source_target_pairs={{0,8},{8,16},{16,24},{24,28},{28,20},{20,12},{12,4},{4,0},{1,9},{9... | collective-permute-start | bytes 393224 | tf_op jit(solution)/shard_map/ppermute | solution.py:84
  590.6 7.5 %collective-permute-start.52 = (bf16[128,512]{1,0:T(8,128)(2,1)S(1)}, bf16[128,512]{1,0:T(8,128)(2,1)S(1)}, u32[]{:S(2)}, u32[]{:S(2)}) collective-permute-start(bf16[128,512]{1,0:T(8,128)(2,1)S(1)} %get-tuple-element.160), channel_id=1, source_target_pairs={{8,0},{16,8},{24,16},{28,24},{20,28},{12,20},{4,12},{0,4},{9,1},{1... | collective-permute-start | bytes 393224 | tf_op jit(solution)/shard_map/ppermute | solution.py:84
  595.1 5.7 collective-permute-start.16
  596.1 5.7 collective-permute-start.37
  597.2 5.7 collective-permute-start.30
  598.1 5.7 collective-permute-start.23
  600.8 12.9 %collective-permute-start.1 = (bf16[256,2048]{1,0:T(8,128)(2,1)}, bf16[256,2048]{1,0:T(8,128)(2,1)}, u32[]{:S(2)}, u32[]{:S(2)}) collective-permute-start(bf16[256,2048]{1,0:T(8,128)(2,1)} %get-tuple-element.156), channel_id=1, source_target_pairs={{0,1},{1,0},{2,3},{3,2},{4,5},{5,4},{6,7},{7,6},{8,9},{9,8},{10,11... | collective-permute-start | bytes 3145736 | tf_op jit(solution)/shard_map/ppermute | solution.py:119
  601.8 21.6 %collective-permute-start.3 = (bf16[256,2048]{1,0:T(8,128)(2,1)S(1)}, bf16[256,2048]{1,0:T(8,128)(2,1)}, u32[]{:S(2)}, u32[]{:S(2)}) collective-permute-start(bf16[256,2048]{1,0:T(8,128)(2,1)S(1)} %get-tuple-element.153), channel_id=1, source_target_pairs={{0,1},{1,0},{2,3},{3,2},{4,5},{5,4},{6,7},{7,6},{8,9},{9,8},{10,11... | collective-permute-start | bytes 3145736 | tf_op jit(solution)/shard_map/ppermute | solution.py:120
  606.2 8.6 %collective-permute-start.17 = (bf16[64,1536]{1,0:T(8,128)(2,1)}, bf16[64,1536]{1,0:T(8,128)(2,1)S(1)}, u32[]{:S(2)}, u32[]{:S(2)}) collective-permute-start(bf16[64,1536]{1,0:T(8,128)(2,1)} %get-tuple-element.125), channel_id=1, source_target_pairs={{0,8},{8,16},{16,24},{24,28},{28,20},{20,12},{12,4},{4,0},{1,9},{9... | collective-permute-start | bytes 589832 | tf_op jit(solution)/shard_map/ppermute | solution.py:84
  610.5 26.4 %collective-permute-start.5 = (bf16[256,2048]{1,0:T(8,128)(2,1)}, bf16[256,2048]{1,0:T(8,128)(2,1)}, u32[]{:S(2)}, u32[]{:S(2)}) collective-permute-start(bf16[256,2048]{1,0:T(8,128)(2,1)} %fusion.11), channel_id=1, source_target_pairs={{0,2},{2,0},{1,3},{3,1},{4,6},{6,4},{5,7},{7,5},{8,10},{10,8},{9,1... | collective-permute-start | bytes 3145736 | tf_op jit(solution)/shard_map/ppermute | solution.py:121
  612.7 7.0 %collective-permute-start.38 = (bf16[64,1536]{1,0:T(8,128)(2,1)}, bf16[64,1536]{1,0:T(8,128)(2,1)S(1)}, u32[]{:S(2)}, u32[]{:S(2)}) collective-permute-start(bf16[64,1536]{1,0:T(8,128)(2,1)} %get-tuple-element.126), channel_id=1, source_target_pairs={{8,0},{16,8},{24,16},{28,24},{20,28},{12,20},{4,12},{0,4},{9,1},{1... | collective-permute-start | bytes 589832 | tf_op jit(solution)/shard_map/ppermute | solution.py:84
  613.7 6.0 collective-permute-start.31
  614.8 7.0 %collective-permute-start.24 = (bf16[64,1536]{1,0:T(8,128)(2,1)}, bf16[64,1536]{1,0:T(8,128)(2,1)S(1)}, u32[]{:S(2)}, u32[]{:S(2)}) collective-permute-start(bf16[64,1536]{1,0:T(8,128)(2,1)} %get-tuple-element.128), channel_id=1, source_target_pairs={{8,0},{16,8},{24,16},{28,24},{20,28},{12,20},{4,12},{0,4},{9,1},{1... | collective-permute-start | bytes 589832 | tf_op jit(solution)/shard_map/ppermute | solution.py:84
  619.7 47.2 %collective-permute-start = (bf16[256,2048]{1,0:T(8,128)(2,1)S(1)}, bf16[256,2048]{1,0:T(8,128)(2,1)S(1)}, u32[]{:S(2)}, u32[]{:S(2)}) collective-permute-start(bf16[256,2048]{1,0:T(8,128)(2,1)S(1)} %copy-done.9), channel_id=1, source_target_pairs={{0,1},{1,0},{2,3},{3,2},{4,5},{5,4},{6,7},{7,6},{8,9},{9,8},{10,11... | collective-permute-start | bytes 3145736 | tf_op jit(solution)/shard_map/ppermute | solution.py:120
  619.7 47.2 %collective-permute-start.2 = (bf16[256,2048]{1,0:T(8,128)(2,1)S(1)}, bf16[256,2048]{1,0:T(8,128)(2,1)S(1)}, u32[]{:S(2)}, u32[]{:S(2)}) collective-permute-start(bf16[256,2048]{1,0:T(8,128)(2,1)S(1)} %fusion.13), channel_id=1, source_target_pairs={{0,2},{2,0},{1,3},{3,1},{4,6},{6,4},{5,7},{7,5},{8,10},{10,8},{9,1... | collective-permute-start | bytes 3145736 | tf_op jit(solution)/shard_map/ppermute | solution.py:121
  641.8 15.3 %collective-permute-start.7 = (f32[4,2048]{1,0:T(4,128)S(1)}, f32[4,2048]{1,0:T(4,128)S(1)}, u32[]{:S(2)}, u32[]{:S(2)}) collective-permute-start(f32[4,2048]{1,0:T(4,128)S(1)} %fusion.69), channel_id=1, source_target_pairs={{0,2},{1,3},{2,0},{3,1},{4,6},{5,7},{6,4},{7,5},{8,10},{9,11},{10,... | collective-permute-start | bytes 98312 | tf_op jit(solution)/shard_map/ppermute | solution.py:133
  (28 other events, 478.7 us)

commit v5 on v4

--- a/solution.py
+++ b/solution.py
@@ -931,13 +931,13 @@
             device_id_type=MESH,
         )
 
-    def tick(self, step, left, right, final):
+    def tick(self, step, product, final):
         if step > 0:
             self.copy(step).wait_recv()
         cols = self.slots.shape[2]
         for low in range(0, cols, 512):
             tile = slice(low, min(low + 512, cols))
-            part = dot(left, right(tile), ((1,), (0,)))
+            part = product(tile)
             if step > 0:
                 part = part + self.slots[step, :, tile].astype(f32)
             if step == self.place.n - 1:
@@ -1038,7 +1038,8 @@
             def final(tile, total):
                 datt[lane.way * size // 2 : (lane.way + 1) * size // 2, tile] = total
 
-            lane.tick(step, columns_of(left, lane.whose(step), size, lane.way), lambda tile: right[:, tile], final)
+            block = columns_of(left, lane.whose(step), size, lane.way)
+            lane.tick(step, lambda tile: dot(block, right[:, tile], ((1,), (0,))), final)
         if step == n - 1:
             stored(i).start()
 
@@ -1261,6 +1262,266 @@
         q, k, v, logs, cosine, sine, segments[None, :], segments[:, None],
     )
 
+def leave_kernel(
+    n,
+    normed_ref, dlin_ref, qkv_ref, mixed_ref, resid_ref, datt_ref, x_ref, att_ref, ffn_ref, small, vec_ref,
+    layer_out, input_out, query_sum, key_sum, value_sum, out_sum, vec_out,
+    wide, narrow, normed, dlin, qkv, mixed, resid, datt, attended, x, first, near_send, near_recv, far_send, far_recv,
+    ffn_own, ffn_recv, ffn_send, ffn_far, layer, acc, totals, wsum, osum, vecs, vec_recv,
+    send, recv, x_send, x_recv, v_send, v_recv, local,
+):
+    place = Place(n)
+    t, me = place.t, place.me
+    rows, model = att_ref.shape
+    size = model // n
+    total_cols = dlin_ref.shape[0]
+    width = total_cols // 3
+    part = total_cols // 2
+    loads = [
+        pltpu.make_async_copy(src, dst, local.at[i])
+        for i, (src, dst) in enumerate(
+            (
+                (normed_ref, normed),
+                (dlin_ref, dlin),
+                (resid_ref, resid),
+                (mixed_ref, mixed),
+                (qkv_ref, qkv),
+                (ffn_ref.at[place.chip], ffn_own.at[0]),
+                (ffn_ref.at[t], ffn_own.at[1]),
+                (att_ref, attended),
+                (x_ref, x),
+                (datt_ref, datt),
+            )
+        )
+    ]
+    for load in loads:
+        load.start()
+    hops = [1, 2, 4]
+    partners = [me + hop - 2 * hop * lax.rem(lax.div(me, hop), 2) for hop in hops]
+    place.barrier([place.up, place.down] + partners, [place.core, place.chip])
+
+    lanes = [
+        [Sum(place, wide.at[2 * i + way], way, send.at[2 * i + way], recv.at[2 * i + way]) for way in range(2)] for i in range(2)
+    ] + [[Sum(place, narrow.at[way], way, send.at[4 + way], recv.at[4 + way]) for way in range(2)]]
+
+    swap = Exchange(x_send, x_recv)
+    near = [swap.copy(i, near_send.at[i], near_recv.at[i], place.core) for i in range(2)]
+    far = swap.copy(2, far_send, far_recv, place.chip)
+    outs = [swap.copy(3 + i, ffn_ref.at[block], ffn_recv.at[i], place.core) for i, block in enumerate((place.cross, place.core))]
+    outs_far = swap.copy(5, ffn_send, ffn_far, place.chip)
+    for copy in outs:
+        copy.start()
+
+    def tick(step, i):
+        for lane in lanes[i]:
+            half = slice(lane.way * size // 2, (lane.way + 1) * size // 2)
+            if i == 2:
+
+                def product(left, tile):
+                    return dot(left, mixed[:, tile], ((1,), (0,)))
+
+                def final(tile, total):
+                    osum[half, tile] = total
+
+            else:
+
+                def product(left, tile):
+                    return dot(left, dlin[part * i + tile.start : part * i + tile.stop, :], ((1,), (1,)))
+
+                def final(tile, total):
+                    wsum[half, part * i + tile.start : part * i + tile.stop] = total
+
+            left = columns_of(resid if i == 2 else normed, lane.whose(step), size, lane.way)
+            lane.tick(step, lambda tile: product(left, tile), final)
+
+    plan = iter([(step, i) for step in range(n) for i in range(3)])
+
+    def advance(count=1):
+        for _ in range(count):
+            tick(*next(plan))
+
+    loads[0].wait()
+    loads[1].wait()
+    advance(2)
+    loads[2].wait()
+    loads[3].wait()
+    advance()
+    outs[0].wait_recv()
+    loads[5].wait()
+    for j in range(0, rows, 64):
+        tile = slice(j, j + 64)
+        ffn_send[tile, :] = (ffn_own[0, tile, :].astype(f32) + ffn_recv[0, tile, :].astype(f32)).astype(bf16)
+    outs_far.start()
+    loads[4].wait()
+
+    def product(block, use):
+        left = dlin[:, pl.ds(pl.multiple_of(block * rows, rows), rows)].T
+        for j in range(n):
+            use(slice(j * size, (j + 1) * size), dot(left, qkv[j], ((1,), (1,))))
+
+    for i, block in enumerate((place.cross, place.core)):
+
+        def use_near(tile, value):
+            near_send[i, :, tile] = value.astype(bf16)
+
+        product(block, use_near)
+        near[i].start()
+        advance()
+    near[0].wait_recv()
+
+    def use_far(tile, value):
+        far_send[:, tile] = (value + near_recv[0, :, tile].astype(f32)).astype(bf16)
+
+    product(place.chip, use_far)
+    far.start()
+    advance()
+    near[1].wait_recv()
+
+    def use_own(tile, value):
+        first[:, tile] = value + near_recv[1, :, tile].astype(f32)
+
+    product(t, use_own)
+    advance()
+
+    outs[1].wait_recv()
+    outs_far.wait_recv()
+    loads[6].wait()
+    loads[7].wait()
+    for j in range(0, rows, 64):
+        tile = slice(j, j + 64)
+        layer[tile, :] = (
+            attended[tile, :]
+            + ffn_own[1, tile, :].astype(f32)
+            + ffn_recv[1, tile, :].astype(f32)
+            + ffn_far[tile, :].astype(f32)
+        ).astype(bf16)
+    layer_store = pltpu.make_async_copy(layer, layer_out, local.at[10])
+    layer_store.start()
+    advance()
+
+    count = small.shape[2]
+    gain = lane_vector(small, 0, size // count)
+    acc[...] = jnp.zeros_like(acc)
+    loads[8].wait()
+    loads[9].wait()
+    advance(2)
+    far.wait_recv()
+
+    @pl.loop(0, rows // 16)
+    def _(i):
+        here = pl.ds(pl.multiple_of(i * 16, 16), 16)
+        value = x[here, :].astype(f32)
+        center = value - jnp.mean(value, axis=1, keepdims=True)
+        rstd = lax.rsqrt(jnp.mean(center * center, axis=1, keepdims=True) + EPS)
+        hat = center * rstd
+        incoming = first[here, :] + far_recv[here, :].astype(f32)
+        acc[0] += incoming * hat
+        acc[1] += incoming
+        scaled = incoming * gain
+        back_rows = rstd * (
+            scaled - jnp.mean(scaled, axis=1, keepdims=True) - hat * jnp.mean(scaled * hat, axis=1, keepdims=True)
+        )
+        totals[here, :] = datt[here, :] + back_rows
+
+    input_store = pltpu.make_async_copy(totals, input_out, local.at[11])
+    input_store.start()
+    vecs[0] = vec_ref[...]
+    vecs[0, 0:1, :] = jnp.sum(acc[0], axis=0, keepdims=True)
+    vecs[0, 1:2, :] = jnp.sum(acc[1], axis=0, keepdims=True)
+
+    def hop(number):
+        there = {"tensor": (place.core, place.chip)[number]} if number < 2 else {"dp": partners[number - 2]}
+        return pltpu.make_async_remote_copy(
+            src_ref=vecs.at[number],
+            dst_ref=vec_recv.at[number],
+            send_sem=v_send.at[number],
+            recv_sem=v_recv.at[number],
+            device_id=there,
+            device_id_type=MESH,
+        )
+
+    for number in range(5):
+        hop(number).start()
+        advance(2)
+        hop(number).wait_recv()
+        summed = vecs[number] + vec_recv[number]
+        if number < 2:
+            row = lax.broadcasted_iota(jnp.int32, summed.shape, 0)
+            summed = jnp.where(row < 4, summed, vecs[number])
+        vecs[number + 1] = summed
+    vec_out[...] = vecs[5]
+    for item in plan:
+        tick(*item)
+    results = [
+        pltpu.make_async_copy(wsum.at[:, pl.ds(i * width, width)], out, local.at[12 + i])
+        for i, out in enumerate((query_sum, key_sum, value_sum))
+    ] + [pltpu.make_async_copy(osum, out_sum, local.at[15])]
+    for copy in results:
+        copy.start()
+    for group in lanes:
+        for lane in group:
+            lane.finish()
+    for copy in near + [far] + outs + [outs_far]:
+        copy.wait_send()
+    for number in range(5):
+        hop(number).wait_send()
+    for copy in results + [layer_store, input_store]:
+        copy.wait()
+
+
+def leave(normed, dlin, qkv, mixed, resid, datt, x, attended, ffn, small, vec, n):
+    rows, model = x.shape
+    size = model // n
+    seq, width = mixed.shape
+    shape = jax.ShapeDtypeStruct
+    own = lambda kind: pltpu.VMEM((rows, model), kind)
+    return pl.pallas_call(
+        lambda *refs: leave_kernel(n, *refs),
+        in_specs=[HBM] * 9 + [VMEM] * 2,
+        out_specs=[HBM] * 6 + [VMEM],
+        out_shape=[shape((rows, model), bf16), shape((rows, model), f32)]
+        + [shape((size, width), f32)] * 4
+        + [shape((8, model), f32)],
+        scratch_shapes=[
+            pltpu.VMEM((4, n, size // 2, 3 * width // 2), bf16),
+            pltpu.VMEM((2, n, size // 2, width), bf16),
+            pltpu.VMEM((seq, model), bf16),
+            pltpu.VMEM((3 * width, seq), bf16),
+            pltpu.VMEM((n, size, 3 * width), bf16),
+            pltpu.VMEM((seq, width), bf16),
+            pltpu.VMEM((seq, model), bf16),
+            own(f32),
+            own(f32),
+            own(bf16),
+            own(f32),
+            pltpu.VMEM((2, rows, model), bf16),
+            pltpu.VMEM((2, rows, model), bf16),
+            own(bf16),
+            own(bf16),
+            pltpu.VMEM((2, rows, model), bf16),
+            pltpu.VMEM((2, rows, model), bf16),
+            own(bf16),
+            own(bf16),
+            own(bf16),
+            pltpu.VMEM((2, 16, model), f32),
+            own(f32),
+            pltpu.VMEM((size, 3 * width), f32),
+            pltpu.VMEM((size, width), f32),
+            pltpu.VMEM((6, 8, model), f32),
+            pltpu.VMEM((5, 8, model), f32),
+            DMA((6, n - 1)),
+            DMA((6, n - 1)),
+            DMA((6,)),
+            DMA((6,)),
+            DMA((5,)),
+            DMA((5,)),
+            DMA((16,)),
+        ],
+        compiler_params=pltpu.CompilerParams(collective_id=4, has_side_effects=True, vmem_limit_bytes=62 << 20),
+        cost_estimate=pl.CostEstimate(flops=14 * seq * model * width, bytes_accessed=40 << 20, transcendentals=0),
+        name="leave",
+    )(normed, dlin, qkv.reshape(n, size, 3 * width), mixed, resid, datt, x, attended, ffn.reshape(4, rows, model), small, vec)
+
 
 def norm_forward(rows):
     center = rows - jnp.mean(rows, axis=-1, keepdims=True)
@@ -1371,16 +1632,17 @@
         grad_hidden = dot(g_full, down_t, ((1,), (0,)))
         grad_gate = (grad_hidden * up_lin * sigma * (1.0 + gate_lin * (1.0 - sigma))).astype(bf16)
         grad_up = (grad_hidden * activated).astype(bf16)
-    layer_output = (attended + tensor_scatter(ffn.astype(f32))).astype(bf16)
-
     if ring.ring:
         down_sum, gate_sum, up_sum, grad_attended, residual, grad_lin, vec = back(
             grad_gate, grad_up, hidden, second, g_full, gate, up, attended, packed_small, out_t,
             q_rot, k_rot, v_heads, logs, cosine, sine, segments, n
         )
-        down_sum, residual = down_sum.T, residual.reshape(-1, model)
-        sums = vec[4, : 3 * width].reshape(3, width).T
-        second_vectors = vec[2:4]
+        layer_output, input_grad, query_sum, key_sum, value_sum, out_sum, vec = leave(
+            normed, grad_lin, qkv, mixed, residual.reshape(-1, model), grad_attended, layer_input, attended, ffn, packed_small, vec, n
+        )
+        down_sum, out_sum = down_sum.T, out_sum.T
+        vectors = vec[:4]
+        sums = vec[4, : 3 * width].reshape(3, width)
     else:
         down_grad = dot(g_full, hidden, ((0,), (0,)))
         grad_second = tensor_scatter(dot(grad_gate, gate, ((1,), (1,))) + dot(grad_up, up, ((1,), (1,))))
@@ -1395,38 +1657,42 @@
         dq, dk, dv, sums = attend_backward(q_rot, k_rot, v_heads, grad_mixed, logs, cosine, sine, bias)
         grad_lin = jnp.concatenate([dq, dk, dv], axis=0)
         sums = sums.reshape(width, 128)[:, :3]
-        second_vectors = jnp.stack([jnp.sum(grad_second * hat_two, axis=0), jnp.sum(grad_second, axis=0)])
-
-    out_grad_t = dot(residual, mixed, ((0,), (0,)))
-    out_sum = ring.scatter(out_grad_t).T
-    qkv_grad = dot(normed, grad_lin, ((0,), (1,)))
-    qkv_sum = ring.scatter(qkv_grad, pieces=2)
-    grad_first = tensor_scatter(dot(grad_lin, qkv, ((0,), (1,))))
-    hat_one, rstd_one = norm_forward(rows)
-    input_grad = grad_attended + norm_backward(grad_first, hat_one, rstd_one, gain_one)
-
-    vectors = jnp.stack([jnp.sum(grad_first * hat_one, axis=0), jnp.sum(grad_first, axis=0)])
-    vectors = jnp.concatenate([vectors, second_vectors])
-    vectors = sum_all(vectors, ["tensor"])
-    packed = sum_all(jnp.concatenate([vectors.reshape(-1), sums.reshape(-1)]), ["dp"])
+        out_sum = ring.scatter(dot(residual, mixed, ((0,), (0,)))).T
+        qkv_sum = ring.scatter(dot(normed, grad_lin, ((0,), (1,))))
+        query_sum, key_sum, value_sum = (qkv_sum[:, i * width : (i + 1) * width] for i in range(3))
+        grad_first = tensor_scatter(dot(grad_lin, qkv, ((0,), (1,))))
+        hat_one, rstd_one = norm_forward(rows)
+        input_grad = grad_attended + norm_backward(grad_first, hat_one, rstd_one, gain_one)
+        layer_output = (attended + tensor_scatter(ffn.astype(f32))).astype(bf16)
+        vectors = jnp.stack(
+            [
+                jnp.sum(grad_first * hat_one, axis=0),
+                jnp.sum(grad_first, axis=0),
+                jnp.sum(grad_second * hat_two, axis=0),
+                jnp.sum(grad_second, axis=0),
+            ]
+        )
+        packed = sum_all(jnp.concatenate([sum_all(vectors, ["tensor"]).reshape(-1), sums.T.reshape(-1)]), ["dp"])
+        vectors, sums = packed[: 4 * model].reshape(4, model), packed[4 * model :].reshape(3, width)
+
     each = model // (n * lax.axis_size("tensor"))
     at = ring.me * lax.axis_size("tensor") + lax.axis_index("tensor")
-    vectors = lax.dynamic_slice(packed[: 4 * model].reshape(4, -1, each), (0, at, 0), (4, 1, each))[:, 0]
-    sums = packed[4 * model :].reshape(heads, n, per, 3)
-    mine = lax.dynamic_slice(sums, (0, ring.me, 0, 0), (heads, 1, per, 3))[:, 0]
-    key_sum = sums[..., 1].reshape(heads, HD)[:, :ROT]
+    vectors = lax.dynamic_slice(vectors.reshape(4, -1, each), (0, at, 0), (4, 1, each))[:, 0]
+    sums = sums.reshape(3, heads, n, per)
+    mine = lax.dynamic_slice(sums, (0, 0, ring.me, 0), (3, heads, 1, per))[:, :, 0]
+    key_bias_sum = sums[1].reshape(heads, HD)[:, :ROT]
 
     return (
         layer_output,
         input_grad,
         vectors[0],
         vectors[1],
-        qkv_sum[:, :width],
-        qkv_sum[:, width : 2 * width],
-        qkv_sum[:, 2 * width :],
-        mine[..., 0],
+        query_sum,
         key_sum,
-        mine[..., 2],
+        value_sum,
+        mine[0],
+        key_bias_sum,
+        mine[2],
         out_sum,
         vectors[2],
         vectors[3],

time: 686 us -> 598 us (0.87)
  Pallas kernels: 449 us -> 558 us
  waiting for transfers between devices: 58.7 us -> 0 us
  starting transfers between devices: 50.4 us -> 0 us
  other arithmetic: 37.8 us -> 0.86 us
  matrix products: 27.3 us -> 0 us
  local copies, waits for them, and re-layouts: 51.8 us -> 28.8 us
    pallas_call x0 -> x1, Pallas kernels: none -> 109 us  [leave(): pl.pallas_call(lambda *refs: leave_kernel(n, *refs), in_specs=[HBM] * 9 +...]
    ppermute x53 -> x0, waiting for transfers between devices: 58.7 us -> none  [the longest x42 27.4 us: scatter(): got = lax.ppermute(moving.astype(bf16), 'dp', self.down if way else self.up)]
    ppermute x53 -> x0, starting transfers between devices: 50.4 us -> none  [the longest x42 43.1 us: scatter(): got = lax.ppermute(moving.astype(bf16), 'dp', self.down if way else self.up)]
    dot_general x3 -> x0, matrix products: 27.3 us -> none  [dot(): lax.dot_general(a, b, ((dims[0], dims[1]), ((), ())), preferred_element_t...]
    convert_element_type x16 -> x0, other arithmetic: 25.1 us -> none  [the longest x12 13.2 us: scatter(): got = lax.ppermute(moving.astype(bf16), 'dp', self.down if way else self.up)]
    dot_general x2 -> x0, local copies, waits for them, and re-layouts: 11.2 us -> none  [dot(): lax.dot_general(a, b, ((dims[0], dims[1]), ((), ())), preferred_element_t...]
    unnamed x54 -> x30, local copies, waits for them, and re-layouts: 16.8 us -> 12.6 us
  transfers between devices with their start and end apart: 53 -> 0, of which waited for: 27 -> 0; matrix products, arithmetic and copies ran while one was open for 11% -> 0% of each run, Pallas kernels for 0% -> 0%
where the time goes in v5:
time: 598 us; the launch traced here: 589 us
  Pallas kernels  558 us (93%)
  local copies, waits for them, and re-layouts  28.8 us (5%)
    pallas_call x1, Pallas kernels, middle(): pl.pallas_call(lambda *refs: middle_kernel(n, *refs), in_specs=[HBM] + [V...  184 us
    pallas_call x1, Pallas kernels, back(): pl.pallas_call(lambda *refs: back_kernel(n, *refs), in_specs=[HBM] * 8 +...  172 us
    pallas_call x1, Pallas kernels, leave(): pl.pallas_call(lambda *refs: leave_kernel(n, *refs), in_specs=[HBM] * 9 +...  109 us
    pallas_call x1, Pallas kernels, enter(): pl.pallas_call(kernel, in_specs=[HBM] * 5 + [VMEM, VMEM], out_specs=[HBM,...  92.4 us
    unnamed x30, local copies, waits for them, and re-layouts  12.6 us

profile of v5, /device:TPU:0, one launch (start us, length us, event | category | flops | bytes accessed | tf_op | source)
XLA Modules:
  0.0 588.8 jit_solution(4493777343137879813)
XLA Ops:
  0.6 0.8 reshape.104
  1.4 0.8 reshape.105
  2.2 2.8 concatenate.6
  4.9 0.6 pad.9.refs_6_
  5.5 0.0 copy-start.9
  5.5 0.0 copy-start.8
  5.5 0.0 copy-start.7
  5.5 92.4 %enter.1 = (bf16[1024,2048]{1,0:T(8,128)(2,1)}, bf16[4,256,2048]{2,1,0:T(8,128)(2,1)}, bf16[8,256,1536]{2,1,0:T(8,128)(2,1)}, bf16[8,256,512]{2,1,0:T(8,128)(2,1...) custom-call(bf16[256,2048]{1,0:T(8,128)(2,1)} %refs_6_.3, bf16[256,2048]{1,0:T(8,128)(2,1)} %refs_1_.1, ...), custom_call_target="tpu_custom_call" | custom-call | flops 6442450944 | bytes 41943040 | tf_op jit(solution)/shard_map/enter/pallas_call | solution.py:519
  98.0 0.8 copy.56
  98.8 0.1 reshape.120
  98.9 0.1 squeeze.26
  99.0 0.1 squeeze.27
  99.1 0.0 copy-done.9
  99.1 0.1 reshape.119
  99.2 1.2 broadcast_in_dim.16.refs_1_
  100.3 0.0 copy-done.8
  100.3 0.8 multiply_sine_fusion
  101.2 0.0 copy-done.7
  101.2 1.0 copy.46.refs_5_.refs_17_
  102.2 184.4 %middle.1 = (bf16[512,1024]{1,0:T(8,128)(2,1)}, bf16[512,1024]{1,0:T(8,128)(2,1)}, bf16[512,1024]{1,0:T(8,128)(2,1)}, f32[8,1024]{1,0:T(8,128)}, bf16[1024,512]{...) custom-call(f32[1536,1024]{1,0:T(8,128)} %get-tuple-element.50.refs_, ...), custom_call_target="tpu_custom_call" | custom-call | flops 29527900160 | bytes 62914560 | tf_op jit(solution)/shard_map/middle/pallas_call | solution.py:870
  286.6 172.4 %back.1 = (f32[256,1408]{1,0:T(8,128)}, f32[256,1408]{1,0:T(8,128)}, f32[256,1408]{1,0:T(8,128)}, f32[256,2048]{1,0:T(8,128)}, bf16[4,256,2048]{2,1,0:T(8,128)(2...) custom-call(bf16[1024,1408]{1,0:T(8,128)(2,1)} %bitcast.53, bf16[1024,1408]{1,0:T(8,128)(2,1)} %bitcast.54, ...), custom_call_target="tpu_custom_call" | custom-call | flops 41339060224 | bytes 62914560 | tf_op jit(solution)/shard_map/back/pallas_call | solution.py:1223
  459.0 0.0 copy-start.3
  459.0 109.0 %leave.1 = (bf16[256,2048]{1,0:T(8,128)(2,1)}, f32[256,2048]{1,0:T(8,128)}, f32[256,512]{1,0:T(8,128)}, f32[256,512]{1,0:T(8,128)}, f32[256,512]{1,0:T(8,128)}, /*index=5*/f32[256,512]{1,0:T(8,128)}, f32[8,2048]{1,0:T(8,128)}) custom-call(bf16[1024,2048]{1,0:T(8,128)(2,1)} %get-tuple-element.49.refs_0_, bf16[1536,1024]{1,0:T(8,128)(2,1)} %get-tuple-element.65.refs_1_, ...), custom_call_target="tpu_custom_call" | custom-call | flops 15032385536 | bytes 41943040 | tf_op jit(solution)/shard_map/leave/pallas_call | solution.py:1478
  568.0 2.0 copy.49
  570.0 0.0 copy-start
  570.0 1.0 slice_reduce_fusion
  571.0 0.7 reshape_reshape_squeeze.3
  571.7 1.4 constant_dynamic-slice_fusion.4
  573.1 1.5 slice.54
  574.6 1.5 reshape.117
  576.1 1.3 fusion
  577.3 0.7 slice_reduce_fusion.1
  578.1 0.7 reshape_squeeze.3
  578.7 0.0 copy-done.3
  578.7 1.5 copy.50
  580.3 2.4 copy.64
  582.6 0.0 copy-done
  582.7 1.3 copy.65
  584.0 0.0 copy-done.6
  584.0 0.8 copy.66
  584.8 0.0 copy-done.5
  584.8 0.8 copy.67
  585.6 0.0 copy-done.4
  585.6 0.8 copy.68
  586.4 0.0 copy-done.2
  586.4 1.1 copy.69
  587.5 0.0 copy-done.1
  587.5 1.1 copy.70
  (13 shorter events, 0.1 us)
Async XLA Ops:
  5.5 93.5 %copy-start.9 = (bf16[8,16]{1,0:T(8,128)(2,1)S(1)}, bf16[8,16]{1,0:T(8,128)(2,1)}, u32[]{:S(2)}) copy-start(bf16[8,16]{1,0:T(8,128)(2,1)} %param.27) | copy-start | bytes 772
  5.5 94.8 %copy-start.8 = (s32[1024]{0:T(1024)S(1)}, s32[1024]{0:T(1024)}, u32[]{:S(2)}) copy-start(s32[1024]{0:T(1024)} %param.20) | copy-start | bytes 12292
  5.5 95.6 %copy-start.7 = (s32[1024]{0:T(1024)S(1)}, s32[1024]{0:T(1024)}, u32[]{:S(2)}) copy-start(s32[1024]{0:T(1024)} %param.19) | copy-start | bytes 12292
  459.0 119.8 %copy-start.3 = (f32[256,1408]{1,0:T(8,128)S(1)}, f32[256,1408]{1,0:T(8,128)}, u32[]{:S(2)}) copy-start(f32[256,1408]{1,0:T(8,128)} %get-tuple-element.81) | copy-start | bytes 4325380
  570.0 12.6 %copy-start = (f32[256,2048]{1,0:T(8,128)S(1)}, f32[256,2048]{1,0:T(8,128)}, u32[]{:S(2)}) copy-start(f32[256,2048]{1,0:T(8,128)} %get-tuple-element.157) | copy-start | bytes 6291460
  580.3 3.7 copy-start.6
  582.6 2.1 copy-start.5
  582.6 2.9 copy-start.4
  582.6 3.7 copy-start.2
  584.0 3.5 copy-start.1

commit v6 on v5

--- a/solution.py
+++ b/solution.py
@@ -347,16 +347,16 @@
 
 
 def lane_vector(full, first, count):
-    pieces = [full[d, r : r + 1, :].astype(f32) for d in range(full.shape[0]) for r in range(first, first + count)]
+    pieces = [full[d, r : r + 1, :] for d in range(full.shape[0]) for r in range(first, first + count)]
     return jnp.concatenate(pieces, axis=1)
 
 
 def enter_kernel(
     n,
-    x_ref, g_ref, wq, wk, wv, wo, small_ref,
-    normed_out, g_out, qkv_out, out_out, lin, small_full,
-    x_full, normed, left, right, outs,
-    small_send, small_recv, send, recv, x_send, x_recv, local, stored,
+    x_ref, g_ref, wq, wk, wv, wo, gain_one, shift_one, gain_two, shift_two, bias_q, bias_v,
+    normed_out, g_out, qkv_out, out_out, lin_out, small_full,
+    x_full, normed, left, right, outs, lin, small_ref,
+    small_send, small_recv, send, recv, x_send, x_recv, local, stored, lin_stored,
 ):
     place = Place(n)
     rows = x_ref.shape[0]
@@ -375,6 +375,15 @@
     for load in loads:
         load.start()
     outs[me] = wo[...].T
+    count = small_ref.shape[1]
+    each = size // count
+    small_ref[...] = jnp.zeros_like(small_ref)
+    for i, vector in enumerate((gain_one, shift_one, gain_two, shift_two)):
+        for r in range(each):
+            small_ref[i * each + r, :] = vector[r * count : (r + 1) * count].astype(f32)
+    heads, per = bias_q.shape
+    small_ref[4 * each : 4 * each + heads, 0:per] = bias_q[...].astype(f32)
+    small_ref[4 * each : 4 * each + heads, per : 2 * per] = bias_v[...].astype(f32)
     small_full[me] = small_ref[...]
     place.barrier([place.owner(k) for k in range(1, n)], [place.core, place.chip])
 
@@ -460,14 +469,19 @@
                     lin[where, :] = part
                 else:
                     lin[where, :] += part
+                if step == n - 1:
+                    lin_store(base + j).start()
+
+    def lin_store(first):
+        at = pl.ds(first, 256)
+        return pltpu.make_async_copy(lin.at[at], lin_out.at[at], lin_stored.at[first // 256])
 
     tick(1)
     loads[4].wait()
     for small in smalls:
         small.wait_recv()
-    count = small_ref.shape[1]
-    gain = lane_vector(small_full, 0, size // count)
-    shift = lane_vector(small_full, size // count, size // count)
+    gain = lane_vector(small_full, 0, each)
+    shift = lane_vector(small_full, each, each)
     norm(t)
     to_core.wait_recv()
     norm(place.core)
@@ -509,24 +523,26 @@
     for write in writes:
         write.wait()
     normed_store.wait()
-
-
-def enter(x, g, wq, wk, wv, wo, small, n):
+    for first in range(0, 3 * width, 256):
+        lin_store(first).wait()
+
+
+def enter(x, g, wq, wk, wv, wo, vectors, biases, n):
     rows, model = x.shape
     size, width = wq.shape
     big = 3 * width // 2
     kernel = lambda *refs: enter_kernel(n, *refs)
     return pl.pallas_call(
         kernel,
-        in_specs=[HBM] * 5 + [VMEM, VMEM],
-        out_specs=[HBM, HBM, HBM, HBM, VMEM, VMEM],
+        in_specs=[HBM] * 5 + [VMEM] * 7,
+        out_specs=[HBM, HBM, HBM, HBM, HBM, VMEM],
         out_shape=[
             jax.ShapeDtypeStruct((4 * rows, model), bf16),
             jax.ShapeDtypeStruct((4, rows, model), bf16),
             jax.ShapeDtypeStruct((n, size, 3 * width), bf16),
             jax.ShapeDtypeStruct((n, size, width), bf16),
             jax.ShapeDtypeStruct((3 * width, 4 * rows), f32),
-            jax.ShapeDtypeStruct((n,) + small.shape, bf16),
+            jax.ShapeDtypeStruct((n, 16, 128), f32),
         ],
         scratch_shapes=[
             pltpu.VMEM((4, rows, model), bf16),
@@ -534,6 +550,8 @@
             pltpu.VMEM((n, size, big), bf16),
             pltpu.VMEM((n, size, big), bf16),
             pltpu.VMEM((n, size, width), bf16),
+            pltpu.VMEM((3 * width, 4 * rows), f32),
+            pltpu.VMEM((16, 128), f32),
             DMA((n - 1,)),
             DMA((n - 1,)),
             DMA((6, n - 1)),
@@ -542,11 +560,12 @@
             DMA((6,)),
             DMA((7,)),
             DMA((4, n)),
+            DMA((3 * width // 256,)),
         ],
         compiler_params=pltpu.CompilerParams(collective_id=1, has_side_effects=True, vmem_limit_bytes=56 << 20),
         cost_estimate=pl.CostEstimate(flops=6 * width * rows * 4 * model, bytes_accessed=40 << 20, transcendentals=0),
         name="enter",
-    )(x, g, wq, wk, wv, wo, small)
+    )(x, g, wq, wk, wv, wo, *vectors, *biases)
 
 def attend_pair(pair, lin, bias_ref, cosine, sine, mask, q_all, k_all, v_all, logs, flat, mixed):
     width, seq = q_all.shape
@@ -583,21 +602,23 @@
     mixed[:, pair * 2 * HD : (pair + 1) * 2 * HD] = flat[...].T
 
 
-def build_mask(mask, seg_row, seg_col):
+def build_mask(mask, column, seg_row):
     seq = mask.shape[0]
+    segments = seg_row[...].astype(f32)
+    column[...] = jnp.broadcast_to(segments, (128, seq)).T
 
     @pl.loop(0, seq // 32)
     def _(i):
         here = pl.ds(pl.multiple_of(i * 32, 32), 32)
         key = lax.broadcasted_iota(jnp.int32, (32, seq), 0) + i * 32
         query = lax.broadcasted_iota(jnp.int32, (32, seq), 1)
-        allowed = (key <= query) & (seg_col[here, :] == seg_row[...])
+        allowed = (key <= query) & (column[here, 0:1] == segments)
         mask[here, :] = jnp.where(allowed, 0.0, NEG).astype(f32)
 
 
 def middle_kernel(
     n,
-    lin_ref, bias_ref, cos_ref, sin_ref, seg_row, seg_col, x_ref, out_ref, small, gate_w, up_w, down_w, g_ref,
+    lin_ref, key_bias, cos_ref, sin_ref, seg_row, x_ref, out_ref, small, gate_w, up_w, down_w, g_ref,
     q_out, k_out, v_out, logs, mixed_out, att_out, second_out, gate_out, up_out, hidden_out, ffn_out, dgate_out, dup_out,
     gate, up, down, second, near_send, near_recv, far_send, far_recv, attended,
     send, recv, x_send, x_recv, local, stored, staged,
@@ -668,7 +689,7 @@
 
     advance(2)
 
-    def attention(lin, mask, q_all, k_all, v_all, flat, mixed, out_t):
+    def attention(lin, mask, q_all, k_all, v_all, flat, mixed, out_t, bias_ref, column):
         pairs = width // (2 * HD)
         fetch = []
         for part in range(3):
@@ -680,7 +701,21 @@
                 fetch[part * pairs + pair].start()
         weights = pltpu.make_async_copy(out_ref, out_t, local.at[2 + 3 * pairs])
         weights.start()
-        build_mask(mask, seg_row, seg_col)
+        build_mask(mask, column, seg_row)
+        heads, per = width // HD, HD // n
+        first = small.shape[1] - heads
+        turned = [small[d, first:, :].T for d in range(n)]
+        keys = key_bias[...].astype(f32).T
+        for head in range(heads):
+            for part in range(3):
+                if part == 1:
+                    rest = jnp.zeros((HD - ROT, 1), f32)
+                    piece = jnp.concatenate([keys[:, head : head + 1], rest], axis=0)
+                else:
+                    at = part // 2 * per
+                    piece = jnp.concatenate([turned[d][at : at + per, head : head + 1] for d in range(n)], axis=0)
+                where = part * width + head * HD
+                bias_ref[where : where + HD, :] = piece
         cosine, sine = cos_ref[...], sin_ref[...]
         for pair in range(pairs):
             for part in range(3):
@@ -730,6 +765,8 @@
         pltpu.VMEM((2 * HD, seq), bf16),
         pltpu.VMEM((seq, width), bf16),
         pltpu.VMEM((model, width), bf16),
+        pltpu.VMEM((3 * width, 1), f32),
+        pltpu.VMEM((seq, 128), f32),
     )
     last = 7 + 3 * (width // (2 * HD))
 
@@ -860,7 +897,7 @@
         copy.wait_send()
 
 
-def middle(lin, bias, cosine, sine, segments, x, out_t, small, gate, up, down, g, n):
+def middle(lin, key_bias, cosine, sine, segments, x, out_t, small, gate, up, down, g, n):
     rows, model = x.shape
     size, cols = gate.shape
     seq = 4 * rows
@@ -869,7 +906,7 @@
     shape = jax.ShapeDtypeStruct
     return pl.pallas_call(
         lambda *refs: middle_kernel(n, *refs),
-        in_specs=[HBM] + [VMEM] * 5 + [HBM, HBM, VMEM, HBM, HBM, VMEM, HBM],
+        in_specs=[HBM] + [VMEM] * 4 + [HBM, HBM, VMEM, HBM, HBM, VMEM, HBM],
         out_specs=[HBM, HBM, HBM, VMEM] + [HBM] * 9,
         out_shape=[
             shape((width, seq), bf16),
@@ -910,7 +947,7 @@
         ),
         name="middle",
     )(
-        lin, bias[:, None], cosine, sine, segments[None, :], segments[:, None],
+        lin, key_bias, cosine, sine, segments[None, :],
         x, out_t, small, gate, up, down, g.reshape(4, rows, model),
     )
 
@@ -1002,7 +1039,7 @@
 def back_kernel(
     n,
     dgate_ref, dup_ref, hidden_ref, second_ref, g_ref, gate_ref, up_ref, att_ref, small, out_ref,
-    q_ref, k_ref, v_ref, logs, cos_ref, sin_ref, seg_row, seg_col,
+    q_ref, k_ref, v_ref, logs, cos_ref, sin_ref, seg_row,
     down_sum, gate_sum, up_sum, datt_out, resid_out, dlin_out, vec,
     slots, g, second, hidden, dgate, dup, near_send, near_recv, far_send, far_recv, datt, acc,
     send, recv, x_send, x_recv, local,
@@ -1018,7 +1055,7 @@
             ((g_ref, g), (hidden_ref, hidden), (second_ref, second), (dgate_ref, dgate), (dup_ref, dup))
         )
     ]
-    for load in loads:
+    for load in loads[:2]:
         load.start()
     place.barrier([place.up, place.down], [place.core, place.chip])
 
@@ -1066,13 +1103,15 @@
             pltpu.make_async_copy(gate_ref, gate, local.at[11]),
             pltpu.make_async_copy(up_ref, up, local.at[12]),
         ]
-        for copy in weights:
-            copy.start()
         loads[0].wait()
         loads[1].wait()
+        for load in loads[2:]:
+            load.start()
         advance()
         loads[2].wait()
         loads[3].wait()
+        for copy in weights:
+            copy.start()
         advance()
         loads[4].wait()
         advance()
@@ -1102,7 +1141,7 @@
 
     pl.run_scoped(feed, pltpu.VMEM((n, size, cols), bf16), pltpu.VMEM((n, size, cols), bf16))
 
-    def attention(attended, mask, q_all, k_all, v_all, d_all, out_t, dk_acc, dv_acc, tmp):
+    def attention(attended, mask, q_all, k_all, v_all, d_all, out_t, dk_acc, dv_acc, tmp, column):
         load_attended = pltpu.make_async_copy(att_ref, attended, local.at[5])
         load_attended.start()
         fetch = [
@@ -1111,7 +1150,7 @@
         ]
         for copy in fetch:
             copy.start()
-        build_mask(mask, seg_row, seg_col)
+        build_mask(mask, column, seg_row)
         count = small.shape[2]
         gain = lane_vector(small, 2 * size // count, size // count)
         acc[...] = jnp.zeros_like(acc)
@@ -1203,6 +1242,7 @@
         pltpu.VMEM((HD, seq), f32),
         pltpu.VMEM((HD, seq), f32),
         pltpu.VMEM((3, 2 * HD, 128), f32),
+        pltpu.VMEM((seq, 128), f32),
     )
     for step in plan:
         tick(*step)
@@ -1222,7 +1262,7 @@
     shape = jax.ShapeDtypeStruct
     return pl.pallas_call(
         lambda *refs: back_kernel(n, *refs),
-        in_specs=[HBM] * 8 + [VMEM] + [HBM] * 4 + [VMEM] * 5,
+        in_specs=[HBM] * 8 + [VMEM] + [HBM] * 4 + [VMEM] * 4,
         out_specs=[HBM] * 6 + [VMEM],
         out_shape=[
             shape((size, cols), f32),
@@ -1259,7 +1299,7 @@
         name="back",
     )(
         dgate, dup, hidden, second, g, gate.reshape(n, size, cols), up.reshape(n, size, cols), attended, small, out_t,
-        q, k, v, logs, cosine, sine, segments[None, :], segments[:, None],
+        q, k, v, logs, cosine, sine, segments[None, :],
     )
 
 def leave_kernel(
@@ -1294,7 +1334,7 @@
             )
         )
     ]
-    for load in loads:
+    for load in loads[:2]:
         load.start()
     hops = [1, 2, 4]
     partners = [me + hop - 2 * hop * lax.rem(lax.div(me, hop), 2) for hop in hops]
@@ -1309,8 +1349,6 @@
     far = swap.copy(2, far_send, far_recv, place.chip)
     outs = [swap.copy(3 + i, ffn_ref.at[block], ffn_recv.at[i], place.core) for i, block in enumerate((place.cross, place.core))]
     outs_far = swap.copy(5, ffn_send, ffn_far, place.chip)
-    for copy in outs:
-        copy.start()
 
     def tick(step, i):
         for lane in lanes[i]:
@@ -1342,9 +1380,46 @@
 
     loads[0].wait()
     loads[1].wait()
+    for load in loads[2:5]:
+        load.start()
     advance(2)
+    for load in loads[5:]:
+        load.start()
     loads[2].wait()
     loads[3].wait()
+    advance()
+    loads[4].wait()
+
+    def product(block, use):
+        left = dlin[:, pl.ds(pl.multiple_of(block * rows, rows), rows)].T
+        for j in range(n):
+            use(slice(j * size, (j + 1) * size), dot(left, qkv[j], ((1,), (1,))))
+
+    for i, block in enumerate((place.cross, place.core)):
+
+        def use_near(tile, value):
+            near_send[i, :, tile] = value.astype(bf16)
+
+        product(block, use_near)
+        near[i].start()
+        advance()
+    near[0].wait_recv()
+
+    def use_far(tile, value):
+        far_send[:, tile] = (value + near_recv[0, :, tile].astype(f32)).astype(bf16)
+
+    product(place.chip, use_far)
+    far.start()
+    advance()
+    near[1].wait_recv()
+
+    def use_own(tile, value):
+        first[:, tile] = value + near_recv[1, :, tile].astype(f32)
+
+    product(t, use_own)
+    advance()
+    for copy in outs:
+        copy.start()
     advance()
     outs[0].wait_recv()
     loads[5].wait()
@@ -1352,59 +1427,13 @@
         tile = slice(j, j + 64)
         ffn_send[tile, :] = (ffn_own[0, tile, :].astype(f32) + ffn_recv[0, tile, :].astype(f32)).astype(bf16)
     outs_far.start()
-    loads[4].wait()
-
-    def product(block, use):
-        left = dlin[:, pl.ds(pl.multiple_of(block * rows, rows), rows)].T
-        for j in range(n):
-            use(slice(j * size, (j + 1) * size), dot(left, qkv[j], ((1,), (1,))))
-
-    for i, block in enumerate((place.cross, place.core)):
-
-        def use_near(tile, value):
-            near_send[i, :, tile] = value.astype(bf16)
-
-        product(block, use_near)
-        near[i].start()
-        advance()
-    near[0].wait_recv()
-
-    def use_far(tile, value):
-        far_send[:, tile] = (value + near_recv[0, :, tile].astype(f32)).astype(bf16)
-
-    product(place.chip, use_far)
-    far.start()
-    advance()
-    near[1].wait_recv()
-
-    def use_own(tile, value):
-        first[:, tile] = value + near_recv[1, :, tile].astype(f32)
-
-    product(t, use_own)
-    advance()
-
-    outs[1].wait_recv()
-    outs_far.wait_recv()
-    loads[6].wait()
-    loads[7].wait()
-    for j in range(0, rows, 64):
-        tile = slice(j, j + 64)
-        layer[tile, :] = (
-            attended[tile, :]
-            + ffn_own[1, tile, :].astype(f32)
-            + ffn_recv[1, tile, :].astype(f32)
-            + ffn_far[tile, :].astype(f32)
-        ).astype(bf16)
-    layer_store = pltpu.make_async_copy(layer, layer_out, local.at[10])
-    layer_store.start()
-    advance()
 
     count = small.shape[2]
     gain = lane_vector(small, 0, size // count)
     acc[...] = jnp.zeros_like(acc)
     loads[8].wait()
     loads[9].wait()
-    advance(2)
+    advance(4)
     far.wait_recv()
 
     @pl.loop(0, rows // 16)
@@ -1442,7 +1471,7 @@
 
     for number in range(5):
         hop(number).start()
-        advance(2)
+        advance(1 if number < 2 else 2)
         hop(number).wait_recv()
         summed = vecs[number] + vec_recv[number]
         if number < 2:
@@ -1450,6 +1479,21 @@
             summed = jnp.where(row < 4, summed, vecs[number])
         vecs[number + 1] = summed
     vec_out[...] = vecs[5]
+    advance(2)
+    outs[1].wait_recv()
+    outs_far.wait_recv()
+    loads[6].wait()
+    loads[7].wait()
+    for j in range(0, rows, 64):
+        tile = slice(j, j + 64)
+        layer[tile, :] = (
+            attended[tile, :]
+            + ffn_own[1, tile, :].astype(f32)
+            + ffn_recv[1, tile, :].astype(f32)
+            + ffn_far[tile, :].astype(f32)
+        ).astype(bf16)
+    layer_store = pltpu.make_async_copy(layer, layer_out, local.at[10])
+    layer_store.start()
     for item in plan:
         tick(*item)
     results = [
@@ -1522,6 +1566,107 @@
         name="leave",
     )(normed, dlin, qkv.reshape(n, size, 3 * width), mixed, resid, datt, x, attended, ffn.reshape(4, rows, model), small, vec)
 
+def finish_kernel(
+    n,
+    layer, input_grad, query_sum, key_sum, value_sum, out_sum, gate_sum, up_sum, down_sum, vec,
+    layer_out, input_out, gain_one, shift_one, query_out, key_out, value_out, bias_q, bias_k, bias_v, out_out, gain_two, shift_two,
+    gate_out, up_out, down_out,
+    out_in, out_turned, down_in, down_turned, held_input, held_layer, held, small_held, sems,
+):
+    loads = [
+        pltpu.make_async_copy(src, dst, sems.at[i])
+        for i, (src, dst) in enumerate(
+            (
+                (down_sum, down_in),
+                (out_sum, out_in),
+                (input_grad, held_input),
+                (layer, held_layer),
+                (gate_sum, held.at[0]),
+                (up_sum, held.at[1]),
+                (query_sum, small_held.at[0]),
+                (key_sum, small_held.at[1]),
+                (value_sum, small_held.at[2]),
+            )
+        )
+    ]
+    for load in loads:
+        load.start()
+    me, t = lax.axis_index("dp"), lax.axis_index("tensor")
+    each = gain_one.shape[1]
+    at = me * 4 + t
+    fit = 128 // each
+    for r, out in enumerate((gain_one, shift_one, gain_two, shift_two)):
+        wide = vec[r : r + 1, pl.ds(pl.multiple_of(lax.div(at, fit) * 128, 128), 128)]
+        value = wide[:, 0:each]
+        for i in range(1, fit):
+            value = jnp.where(lax.rem(at, fit) == i, wide[:, i * each : (i + 1) * each], value)
+        out[...] = value
+    heads, per = bias_q.shape
+    row = vec[4:5, :]
+    for part, out in ((0, bias_q), (2, bias_v)):
+        base = part * heads * HD
+        own = jnp.concatenate([row[:, base + h * HD : base + (h + 1) * HD] for h in range(heads)], axis=0)
+        value = own[:, 0:per]
+        for d in range(1, n):
+            value = jnp.where(me == d, own[:, d * per : (d + 1) * per], value)
+        out[...] = value
+    base = heads * HD
+    bias_k[...] = jnp.concatenate([row[:, base + h * HD : base + h * HD + ROT] for h in range(heads)], axis=0)
+    stores = []
+
+    def store(src, dst):
+        stores.append(pltpu.make_async_copy(src, dst, sems.at[9 + len(stores)]))
+        stores[-1].start()
+
+    loads[0].wait()
+    down_turned[...] = down_in[...].T
+    store(down_turned, down_out)
+    loads[1].wait()
+    out_turned[...] = out_in[...].T
+    store(out_turned, out_out)
+    for load, src, dst in zip(
+        loads[2:],
+        (held_input, held_layer, held.at[0], held.at[1], small_held.at[0], small_held.at[1], small_held.at[2]),
+        (input_out, layer_out, gate_out, up_out, query_out, key_out, value_out),
+    ):
+        load.wait()
+        store(src, dst)
+    for copy in stores:
+        copy.wait()
+
+
+def finish(layer, input_grad, query_sum, key_sum, value_sum, out_sum, gate_sum, up_sum, down_sum, vec, n):
+    shape = jax.ShapeDtypeStruct
+    size, width = query_sum.shape
+    heads, model = width // HD, vec.shape[1]
+    each = shape((1, model // (4 * n)), f32)
+    bias = shape((heads, HD // n), f32)
+    like = lambda value: shape(value.shape, value.dtype)
+    results = pl.pallas_call(
+        lambda *refs: finish_kernel(n, *refs),
+        in_specs=[HBM] * 9 + [VMEM],
+        out_specs=[HBM, HBM, VMEM, VMEM, HBM, HBM, HBM, VMEM, VMEM, VMEM, HBM, VMEM, VMEM, HBM, HBM, HBM],
+        out_shape=[
+            like(layer), like(input_grad), each, each, like(query_sum), like(key_sum), like(value_sum),
+            bias, shape((heads, ROT), f32), bias, shape((width, size), f32), each, each,
+            like(gate_sum), like(up_sum), shape(down_sum.shape[::-1], f32),
+        ],
+        scratch_shapes=[
+            pltpu.VMEM(out_sum.shape, f32),
+            pltpu.VMEM(out_sum.shape[::-1], f32),
+            pltpu.VMEM(down_sum.shape, f32),
+            pltpu.VMEM(down_sum.shape[::-1], f32),
+            pltpu.VMEM(input_grad.shape, f32),
+            pltpu.VMEM(layer.shape, bf16),
+            pltpu.VMEM((2,) + gate_sum.shape, f32),
+            pltpu.VMEM((3,) + query_sum.shape, f32),
+            DMA((18,)),
+        ],
+        compiler_params=pltpu.CompilerParams(vmem_limit_bytes=62 << 20),
+        name="finish",
+    )(layer, input_grad, query_sum, key_sum, value_sum, out_sum, gate_sum, up_sum, down_sum, vec)
+    return tuple(r.reshape(-1) if r.shape[0] == 1 else r for r in results)
+
 
 def norm_forward(rows):
     center = rows - jnp.mean(rows, axis=-1, keepdims=True)
@@ -1564,41 +1709,28 @@
     heads = width // HD
     model = layer_input.shape[1]
 
-    bias_key = jnp.pad(key_bias.astype(f32), ((0, 0), (0, HD - ROT))).reshape(-1)
-    part = model // n
     per = HD // n
     if ring.ring:
-        lanes = 128
-        small = jnp.concatenate(
-            [first_gain, first_shift, second_gain, second_shift, query_bias.reshape(-1), value_bias.reshape(-1)]
-        )
-        small = jnp.pad(small.reshape(-1, lanes), ((0, 16 - small.shape[0] // lanes), (0, 0)))
         normed, g_full, qkv, out_t, lin, small = enter(
-            layer_input, out_grad, query_weight, key_weight, value_weight, out_weight, small, n
+            layer_input, out_grad, query_weight, key_weight, value_weight, out_weight,
+            (first_gain, first_shift, second_gain, second_shift), (query_bias, value_bias), n
         )
         g_full = g_full.reshape(-1, model)
         qkv = qkv.reshape(model, -1)
         out_t = out_t.reshape(model, -1)
-        packed_small = small
-        small = small.reshape(n, -1)[:, : 4 * part + 2 * heads * per]
     else:
+        gather = lambda vector: lax.all_gather(vector, "dp", axis=0, tiled=True).astype(f32)
+        gain_one, shift_one, gain_two, shift_two = map(gather, (first_gain, first_shift, second_gain, second_shift))
+        bias_query, bias_value = (gather(b.T).T.reshape(-1) for b in (query_bias, value_bias))
+        bias_key = jnp.pad(key_bias.astype(f32), ((0, 0), (0, HD - ROT))).reshape(-1)
+        bias_lin = jnp.concatenate([bias_query, bias_key, bias_value])
         x_full = tensor_gather(layer_input)
         g_full = tensor_gather(out_grad, after=x_full)
-        small = jnp.concatenate(
-            [first_gain, first_shift, second_gain, second_shift, query_bias.reshape(-1), value_bias.reshape(-1)]
-        )
-        small = lax.all_gather(small.reshape(1, -1), "dp", axis=0, tiled=True)
         qkv, _ = ring.gather(jnp.concatenate([query_weight, key_weight, value_weight], axis=1))
         out_t, _ = ring.gather(out_weight.T)
         gate, _ = ring.gather(gate_weight)
         up, _ = ring.gather(up_weight)
         down_t, _ = ring.gather(down_weight.T)
-    gain_one, shift_one, gain_two, shift_two = (
-        small[:, i * part : (i + 1) * part].reshape(model).astype(f32) for i in range(4)
-    )
-    biases = small[:, 4 * part :].reshape(n, 2, heads, per).transpose(1, 2, 0, 3).reshape(2, width).astype(f32)
-    bias_lin = jnp.concatenate([biases[0], bias_key, biases[1]])
-    if not ring.ring:
         hat_full, _ = norm_forward(x_full.astype(f32))
         normed = (hat_full * gain_one + shift_one).astype(bf16)
         lin = dot(qkv, normed, ((0,), (1,)))
@@ -1606,18 +1738,18 @@
     freqs = jnp.exp(-(2.0 / ROT) * jnp.arange(HALF).astype(f32) * math.log(10000.0))
     angles = freqs[:, None] * positions.astype(f32)[None, :]
     cosine, sine = jnp.cos(angles), jnp.sin(angles)
-    index = jnp.arange(segments.shape[0], dtype=jnp.int32)
-    allowed = (index[:, None] <= index[None, :]) & (segments[:, None] == segments[None, :])
-    bias = jnp.where(allowed, 0.0, NEG).astype(f32)
     rows = layer_input.astype(f32)
     if ring.ring:
         q_rot, k_rot, v_heads, logs, mixed, attended, second, gate, up, hidden, ffn, grad_gate, grad_up = middle(
-            lin, bias_lin, cosine, sine, segments, layer_input, out_t, packed_small, gate_weight, up_weight, down_weight, g_full, n
+            lin, key_bias, cosine, sine, segments, layer_input, out_t, small, gate_weight, up_weight, down_weight, g_full, n
         )
         second, gate, up = second.reshape(-1, model), gate.reshape(model, -1), up.reshape(model, -1)
         hidden, ffn = hidden.reshape(second.shape[0], -1), ffn.reshape(-1, model)
         grad_gate, grad_up = grad_gate.reshape(hidden.shape), grad_up.reshape(hidden.shape)
     else:
+        index = jnp.arange(segments.shape[0], dtype=jnp.int32)
+        allowed = (index[:, None] <= index[None, :]) & (segments[:, None] == segments[None, :])
+        bias = jnp.where(allowed, 0.0, NEG).astype(f32)
         mixed, q_rot, k_rot, v_heads, logs = attend_forward(lin + bias_lin[:, None], cosine, sine, bias)
         attended = rows + tensor_scatter(dot(mixed, out_t, ((1,), (1,))))
 
@@ -1634,15 +1766,15 @@
         grad_up = (grad_hidden * activated).astype(bf16)
     if ring.ring:
         down_sum, gate_sum, up_sum, grad_attended, residual, grad_lin, vec = back(
-            grad_gate, grad_up, hidden, second, g_full, gate, up, attended, packed_small, out_t,
+            grad_gate, grad_up, hidden, second, g_full, gate, up, attended, small, out_t,
             q_rot, k_rot, v_heads, logs, cosine, sine, segments, n
         )
         layer_output, input_grad, query_sum, key_sum, value_sum, out_sum, vec = leave(
-            normed, grad_lin, qkv, mixed, residual.reshape(-1, model), grad_attended, layer_input, attended, ffn, packed_small, vec, n
+            normed, grad_lin, qkv, mixed, residual.reshape(-1, model), grad_attended, layer_input, attended, ffn, small, vec, n
         )
-        down_sum, out_sum = down_sum.T, out_sum.T
-        vectors = vec[:4]
-        sums = vec[4, : 3 * width].reshape(3, width)
+        return finish(
+            layer_output, input_grad, query_sum, key_sum, value_sum, out_sum, gate_sum, up_sum, down_sum, vec, n
+        )
     else:
         down_grad = dot(g_full, hidden, ((0,), (0,)))
         grad_second = tensor_scatter(dot(grad_gate, gate, ((1,), (1,))) + dot(grad_up, up, ((1,), (1,))))

time: 598 us -> 566 us (0.946)
  local copies, waits for them, and re-layouts: 28.8 us -> 0 us
    pallas_call x1, Pallas kernels: 109 us -> 96.2 us  [leave(): pl.pallas_call(lambda *refs: leave_kernel(n, *refs), in_specs=[HBM] * 9 +...]
    unnamed x30 -> x0, local copies, waits for them, and re-layouts: 12.6 us -> none
    pallas_call x1 -> x2, Pallas kernels: 92.4 us -> 102 us  [the longest x1 93 us: enter(): pl.pallas_call(kernel, in_specs=[HBM] * 5 + [VMEM] * 7, out_specs=[HBM, H...]
where the time goes in v6:
time: 566 us; the launch traced here: 557 us
  Pallas kernels  555 us (98%)
    pallas_call x1, Pallas kernels, middle(): pl.pallas_call(lambda *refs: middle_kernel(n, *refs), in_specs=[HBM] + [V...  184 us
    pallas_call x1, Pallas kernels, back(): pl.pallas_call(lambda *refs: back_kernel(n, *refs), in_specs=[HBM] * 8 +...  172 us
    pallas_call x1, Pallas kernels, leave(): pl.pallas_call(lambda *refs: leave_kernel(n, *refs), in_specs=[HBM] * 9 +...  96.2 us
    pallas_call x1, Pallas kernels, enter(): pl.pallas_call(kernel, in_specs=[HBM] * 5 + [VMEM] * 7, out_specs=[HBM, H...  93 us

profile of v6, /device:TPU:0, one launch (start us, length us, event | category | flops | bytes accessed | tf_op | source)
XLA Modules:
  0.0 557.0 jit_solution(10456316821229183957)
XLA Ops:
  0.7 0.7 convert_element_type.11
  1.3 0.8 multiply_sine_fusion
  2.2 93.0 %enter.1 = (bf16[1024,2048]{1,0:T(8,128)(2,1)}, bf16[4,256,2048]{2,1,0:T(8,128)(2,1)}, bf16[8,256,1536]{2,1,0:T(8,128)(2,1)}, bf16[8,256,512]{2,1,0:T(8,128)(2,1...) custom-call(bf16[256,2048]{1,0:T(8,128)(2,1)} %refs_6_.3, bf16[256,2048]{1,0:T(8,128)(2,1)} %refs_1_.2, ...), custom_call_target="tpu_custom_call" | custom-call | flops 6442450944 | bytes 41943040 | tf_op jit(solution)/shard_map/enter/pallas_call | solution.py:535
  95.2 184.1 %middle.1 = (bf16[512,1024]{1,0:T(8,128)(2,1)}, bf16[512,1024]{1,0:T(8,128)(2,1)}, bf16[512,1024]{1,0:T(8,128)(2,1)}, f32[8,1024]{1,0:T(8,128)}, bf16[1024,512]{...) custom-call(f32[1536,1024]{1,0:T(8,128)} %get-tuple-element.66.refs_, ...), custom_call_target="tpu_custom_call" | custom-call | flops 29527900160 | bytes 62914560 | tf_op jit(solution)/shard_map/middle/pallas_call | solution.py:907
  279.3 172.3 %back.1 = (f32[256,1408]{1,0:T(8,128)}, f32[256,1408]{1,0:T(8,128)}, f32[256,1408]{1,0:T(8,128)}, f32[256,2048]{1,0:T(8,128)}, bf16[4,256,2048]{2,1,0:T(8,128)(2...) custom-call(bf16[1024,1408]{1,0:T(8,128)(2,1)} %bitcast.22, bf16[1024,1408]{1,0:T(8,128)(2,1)} %bitcast.23, ...), custom_call_target="tpu_custom_call" | custom-call | flops 41339060224 | bytes 62914560 | tf_op jit(solution)/shard_map/back/pallas_call | solution.py:1263
  451.6 96.2 %leave.1 = (bf16[256,2048]{1,0:T(8,128)(2,1)}, f32[256,2048]{1,0:T(8,128)}, f32[256,512]{1,0:T(8,128)}, f32[256,512]{1,0:T(8,128)}, f32[256,512]{1,0:T(8,128)}, /*index=5*/f32[256,512]{1,0:T(8,128)}, f32[8,2048]{1,0:T(8,128)}) custom-call(bf16[1024,2048]{1,0:T(8,128)(2,1)} %get-tuple-element.65.refs_0_, bf16[1536,1024]{1,0:T(8,128)(2,1)} %get-tuple-element.81.refs_1_, ...), custom_call_target="tpu_custom_call" | custom-call | flops 15032385536 | bytes 41943040 | tf_op jit(solution)/shard_map/leave/pallas_call | solution.py:1522
  547.8 9.0 %finish.1 = (bf16[256,2048]{1,0:T(8,128)(2,1)}, f32[256,2048]{1,0:T(8,128)}, f32[1,64]{1,0:T(1,128)}, f32[1,64]{1,0:T(1,128)}, f32[256,512]{1,0:T(8,128)}, /*ind...) custom-call(bf16[256,2048]{1,0:T(8,128)(2,1)} %get-tuple-element.88., ...), custom_call_target="tpu_custom_call" | custom-call | tf_op jit(solution)/shard_map/finish/pallas_call | solution.py:1645
  (1 shorter events, 0.0 us)

commit v7 on v6

--- a/solution.py
+++ b/solution.py
@@ -829,58 +829,80 @@
             block = lax.div(i, rows // 16)
             here = pl.ds(pl.multiple_of(lax.rem(i, rows // 16) * 16, 16), 16)
             value = gate_lin[block, here, :]
-            hidden[block, here, :] = (value * jax.nn.sigmoid(value) * up_lin[block, here, :]).astype(bf16)
+            sigma = jax.nn.sigmoid(value)
+            activated = value * sigma
+            upward = up_lin[block, here, :]
+            hidden[block, here, :] = (activated * upward).astype(bf16)
+            gate_lin[block, here, :] = activated
+            up_lin[block, here, :] = upward * sigma * (1.0 + value * (1.0 - sigma))
 
         hidden_store = pltpu.make_async_copy(hidden, hidden_out, local.at[last + 4])
         hidden_store.start()
         g_load.wait()
         stages = []
 
-        def use(whose):
+        def output(whose, base, count):
             number = len(stages)
             slot = number % 2
             if number >= 2:
                 stages[number - 2].wait()
-            at = pl.ds(pl.multiple_of(whose * size, size), size)
+
+            right = down[whose, base : base + count].T
+            for block in range(4):
+                tile = dot(hidden[block], right, ((1,), (0,)))
+                stage[slot, block, :, 0:count] = tile.astype(bf16)
+
+            at = pl.ds(pl.multiple_of(whose * size + base, count), count)
+            stages.append(pltpu.make_async_copy(stage.at[slot, :, :, pl.ds(0, count)], ffn_out.at[:, :, at], staged.at[number]))
+            stages[-1].start()
+
+        def collect(whose, base, count):
+            at = pl.ds(pl.multiple_of(whose * size + base, count), count)
 
             @pl.loop(0, 4)
             def _(block):
-                grad[block] += dot(g[block, :, at], down[whose], ((1,), (0,)))
-                stage[slot, block] = dot(hidden[block], down[whose], ((1,), (1,))).astype(bf16)
-
-            stages.append(pltpu.make_async_copy(stage.at[slot], ffn_out.at[:, :, at], staged.at[number]))
-            stages[-1].start()
-
+                grad[block] += dot(g[block, :, at], down[whose, base : base + count], ((1,), (0,)))
+
+        def use(whose, base=0, count=size):
+            collect(whose, base, count)
+            output(whose, base, count)
+
+        after, before = place.owner(n - 1), place.owner(1 - n)
         use(place.me)
-        for step in range(2, n + 1):
+        for step in range(2, n):
             advance(2)
             if step - 1 == n // 2:
                 use(place.owner(n // 2))
+                use(after, 0, half)
+                use(before, half, half)
             elif step - 1 > n // 2:
                 use(place.owner(step - 1))
                 use(place.owner(1 - step))
-        for lane in lanes[0] + lanes[1] + downs[0] + downs[1]:
+        for lane in lanes[0] + lanes[1]:
             lane.finish()
         for step in range(n):
             for copy in write(step):
                 copy.wait()
-
-        @pl.loop(0, 4 * rows // 16)
-        def _(i):
-            block = lax.div(i, rows // 16)
-            here = pl.ds(pl.multiple_of(lax.rem(i, rows // 16) * 16, 16), 16)
-            value = gate_lin[block, here, :]
-            sigma = jax.nn.sigmoid(value)
-            incoming = grad[block, here, :]
-            gate[block, here, :] = (incoming * up_lin[block, here, :] * sigma * (1.0 + value * (1.0 - sigma))).astype(bf16)
-            gate[4 + block, here, :] = (incoming * (value * sigma)).astype(bf16)
-
-        final = [
-            pltpu.make_async_copy(gate.at[pl.ds(0, 4)], dgate_out, local.at[last + 5]),
-            pltpu.make_async_copy(gate.at[pl.ds(4, 4)], dup_out, local.at[last + 6]),
-        ]
-        for copy in final:
-            copy.start()
+        advance(2)
+        collect(before, 0, half)
+        collect(after, half, half)
+        final = []
+        for block in range(4):
+
+            @pl.loop(0, rows // 16)
+            def _(i):
+                here = pl.ds(pl.multiple_of(i * 16, 16), 16)
+                incoming = grad[block, here, :]
+                gate[block, here, :] = (incoming * up_lin[block, here, :]).astype(bf16)
+                gate[4 + block, here, :] = (incoming * gate_lin[block, here, :]).astype(bf16)
+
+            for first, out in ((0, dgate_out), (4, dup_out)):
+                final.append(pltpu.make_async_copy(gate.at[first + block], out.at[block], local.at[last + 5 + len(final)]))
+                final[-1].start()
+        output(before, 0, half)
+        output(after, half, half)
+        for lane in downs[0] + downs[1]:
+            lane.finish()
         for copy in final + stages[-2:] + [hidden_store, second_store, att_store]:
             copy.wait()
 
@@ -937,9 +959,9 @@
             DMA((8, n - 1)),
             DMA((6,)),
             DMA((6,)),
-            DMA((14 + 3 * width // (2 * HD),)),
+            DMA((20 + 3 * width // (2 * HD),)),
             DMA((2, n)),
-            DMA((n,)),
+            DMA((2 * n,)),
         ],
         compiler_params=pltpu.CompilerParams(collective_id=2, has_side_effects=True, vmem_limit_bytes=62 << 20),
         cost_estimate=pl.CostEstimate(
@@ -1220,9 +1242,23 @@
         for pair in range(width // (2 * HD)):
             advance()
             retreat_pair(pair, q_all, k_all, v_all, d_all, logs, cosine, sine, mask, dk_acc, dv_acc, tmp, vec)
+            here = slice(pair * 2 * HD, (pair + 1) * 2 * HD)
+            out_t[0:seq, here] = q_all[here, :].T
+            out_t[seq : 2 * seq, here] = k_all[here, :].T
+            turned = v_all[here, :].T
+            for block in range(4):
+                at = block * width + pair * 2 * HD
+                near_recv[0, :, at : at + 2 * HD] = turned[block * rows : (block + 1) * rows]
         final = [
-            pltpu.make_async_copy(src, dlin_out.at[pl.ds(i * width, width)], local.at[20 + i])
-            for i, src in enumerate((q_all, k_all, v_all))
+            pltpu.make_async_copy(out_t.at[pl.ds(i * seq, seq)], dlin_out.at[:, pl.ds(i * width, width)], local.at[20 + i])
+            for i in range(2)
+        ] + [
+            pltpu.make_async_copy(
+                near_recv.at[0, :, pl.ds(block * width, width)],
+                dlin_out.at[pl.ds(block * rows, rows), pl.ds(2 * width, width)],
+                local.at[22 + block],
+            )
+            for block in range(4)
         ]
         for copy in final:
             copy.start()
@@ -1270,7 +1306,7 @@
             shape((size, cols), f32),
             shape((rows, model), f32),
             shape((4, rows, model), bf16),
-            shape((3 * width, seq), bf16),
+            shape((seq, 3 * width), bf16),
             shape((8, model), f32),
         ],
         scratch_shapes=[
@@ -1290,7 +1326,7 @@
             DMA((6, n - 1)),
             DMA((6,)),
             DMA((6,)),
-            DMA((23,)),
+            DMA((26,)),
         ],
         compiler_params=pltpu.CompilerParams(collective_id=3, has_side_effects=True, vmem_limit_bytes=62 << 20),
         cost_estimate=pl.CostEstimate(
@@ -1306,7 +1342,7 @@
     n,
     normed_ref, dlin_ref, qkv_ref, mixed_ref, resid_ref, datt_ref, x_ref, att_ref, ffn_ref, small, vec_ref,
     layer_out, input_out, query_sum, key_sum, value_sum, out_sum, vec_out,
-    wide, narrow, normed, dlin, qkv, mixed, resid, datt, attended, x, first, near_send, near_recv, far_send, far_recv,
+    wide, narrow, normed, dlin, qkv, turned, mixed, resid, datt, attended, x, first, near_send, near_recv, far_send, far_recv,
     ffn_own, ffn_recv, ffn_send, ffn_far, layer, acc, totals, wsum, osum, vecs, vec_recv,
     send, recv, x_send, x_recv, v_send, v_recv, local,
 ):
@@ -1314,7 +1350,7 @@
     t, me = place.t, place.me
     rows, model = att_ref.shape
     size = model // n
-    total_cols = dlin_ref.shape[0]
+    total_cols = dlin_ref.shape[1]
     width = total_cols // 3
     part = total_cols // 2
     loads = [
@@ -1359,12 +1395,12 @@
                     return dot(left, mixed[:, tile], ((1,), (0,)))
 
                 def final(tile, total):
-                    osum[half, tile] = total
+                    osum[tile, half] = total.T
 
             else:
 
                 def product(left, tile):
-                    return dot(left, dlin[part * i + tile.start : part * i + tile.stop, :], ((1,), (1,)))
+                    return dot(left, dlin[:, part * i + tile.start : part * i + tile.stop], ((1,), (0,)))
 
                 def final(tile, total):
                     wsum[half, part * i + tile.start : part * i + tile.stop] = total
@@ -1390,11 +1426,15 @@
     advance()
     loads[4].wait()
 
+    def lines(block):
+        return dlin[pl.ds(pl.multiple_of(block * rows, rows), rows), :]
+
     def product(block, use):
-        left = dlin[:, pl.ds(pl.multiple_of(block * rows, rows), rows)].T
         for j in range(n):
-            use(slice(j * size, (j + 1) * size), dot(left, qkv[j], ((1,), (1,))))
-
+            use(slice(j * size, (j + 1) * size), dot(lines(block), turned[j], ((1,), (0,))))
+
+    for j in range(n):
+        turned[j] = qkv[j].T
     for i, block in enumerate((place.cross, place.core)):
 
         def use_near(tile, value):
@@ -1411,12 +1451,12 @@
     product(place.chip, use_far)
     far.start()
     advance()
+
+    def use_own(tile, value):
+        first[:, tile] = value
+
+    product(t, use_own)
     near[1].wait_recv()
-
-    def use_own(tile, value):
-        first[:, tile] = value + near_recv[1, :, tile].astype(f32)
-
-    product(t, use_own)
     advance()
     for copy in outs:
         copy.start()
@@ -1443,7 +1483,7 @@
         center = value - jnp.mean(value, axis=1, keepdims=True)
         rstd = lax.rsqrt(jnp.mean(center * center, axis=1, keepdims=True) + EPS)
         hat = center * rstd
-        incoming = first[here, :] + far_recv[here, :].astype(f32)
+        incoming = first[here, :] + near_recv[1, here, :].astype(f32) + far_recv[here, :].astype(f32)
         acc[0] += incoming * hat
         acc[1] += incoming
         scaled = incoming * gain
@@ -1494,14 +1534,16 @@
         ).astype(bf16)
     layer_store = pltpu.make_async_copy(layer, layer_out, local.at[10])
     layer_store.start()
-    for item in plan:
-        tick(*item)
     results = [
         pltpu.make_async_copy(wsum.at[:, pl.ds(i * width, width)], out, local.at[12 + i])
         for i, out in enumerate((query_sum, key_sum, value_sum))
     ] + [pltpu.make_async_copy(osum, out_sum, local.at[15])]
-    for copy in results:
-        copy.start()
+    for item in plan:
+        tick(*item)
+        if item == (n - 1, 1):
+            for copy in results[:-1]:
+                copy.start()
+    results[-1].start()
     for group in lanes:
         for lane in group:
             lane.finish()
@@ -1524,14 +1566,15 @@
         in_specs=[HBM] * 9 + [VMEM] * 2,
         out_specs=[HBM] * 6 + [VMEM],
         out_shape=[shape((rows, model), bf16), shape((rows, model), f32)]
-        + [shape((size, width), f32)] * 4
-        + [shape((8, model), f32)],
+        + [shape((size, width), f32)] * 3
+        + [shape((width, size), f32), shape((8, model), f32)],
         scratch_shapes=[
             pltpu.VMEM((4, n, size // 2, 3 * width // 2), bf16),
             pltpu.VMEM((2, n, size // 2, width), bf16),
             pltpu.VMEM((seq, model), bf16),
-            pltpu.VMEM((3 * width, seq), bf16),
+            pltpu.VMEM((seq, 3 * width), bf16),
             pltpu.VMEM((n, size, 3 * width), bf16),
+            pltpu.VMEM((n, 3 * width, size), bf16),
             pltpu.VMEM((seq, width), bf16),
             pltpu.VMEM((seq, model), bf16),
             own(f32),
@@ -1550,7 +1593,7 @@
             pltpu.VMEM((2, 16, model), f32),
             own(f32),
             pltpu.VMEM((size, 3 * width), f32),
-            pltpu.VMEM((size, width), f32),
+            pltpu.VMEM((width, size), f32),
             pltpu.VMEM((6, 8, model), f32),
             pltpu.VMEM((5, 8, model), f32),
             DMA((6, n - 1)),
@@ -1571,7 +1614,7 @@
     layer, input_grad, query_sum, key_sum, value_sum, out_sum, gate_sum, up_sum, down_sum, vec,
     layer_out, input_out, gain_one, shift_one, query_out, key_out, value_out, bias_q, bias_k, bias_v, out_out, gain_two, shift_two,
     gate_out, up_out, down_out,
-    out_in, out_turned, down_in, down_turned, held_input, held_layer, held, small_held, sems,
+    out_in, down_in, down_turned, held_input, held_layer, held, small_held, sems,
 ):
     loads = [
         pltpu.make_async_copy(src, dst, sems.at[i])
@@ -1622,8 +1665,7 @@
     down_turned[...] = down_in[...].T
     store(down_turned, down_out)
     loads[1].wait()
-    out_turned[...] = out_in[...].T
-    store(out_turned, out_out)
+    store(out_in, out_out)
     for load, src, dst in zip(
         loads[2:],
         (held_input, held_layer, held.at[0], held.at[1], small_held.at[0], small_held.at[1], small_held.at[2]),
@@ -1648,12 +1690,11 @@
         out_specs=[HBM, HBM, VMEM, VMEM, HBM, HBM, HBM, VMEM, VMEM, VMEM, HBM, VMEM, VMEM, HBM, HBM, HBM],
         out_shape=[
             like(layer), like(input_grad), each, each, like(query_sum), like(key_sum), like(value_sum),
-            bias, shape((heads, ROT), f32), bias, shape((width, size), f32), each, each,
+            bias, shape((heads, ROT), f32), bias, like(out_sum), each, each,
             like(gate_sum), like(up_sum), shape(down_sum.shape[::-1], f32),
         ],
         scratch_shapes=[
             pltpu.VMEM(out_sum.shape, f32),
-            pltpu.VMEM(out_sum.shape[::-1], f32),
             pltpu.VMEM(down_sum.shape, f32),
             pltpu.VMEM(down_sum.shape[::-1], f32),
             pltpu.VMEM(input_grad.shape, f32),

time: 566 us -> 555 us (0.981)
  Pallas kernels: 555 us -> 544 us
    pallas_call x1, Pallas kernels: 184 us -> 178 us  [middle(): pl.pallas_call(lambda *refs: middle_kernel(n, *refs), in_specs=[HBM] + [V...]
where the time goes in v7:
time: 555 us; the launch traced here: 546 us
  Pallas kernels  544 us (98%)
    pallas_call x1, Pallas kernels, middle(): pl.pallas_call(lambda *refs: middle_kernel(n, *refs), in_specs=[HBM] + [V...  178 us
    pallas_call x1, Pallas kernels, back(): pl.pallas_call(lambda *refs: back_kernel(n, *refs), in_specs=[HBM] * 8 +...  172 us
    pallas_call x1, Pallas kernels, enter(): pl.pallas_call(kernel, in_specs=[HBM] * 5 + [VMEM] * 7, out_specs=[HBM, H...  93 us
    pallas_call x1, Pallas kernels, leave(): pl.pallas_call(lambda *refs: leave_kernel(n, *refs), in_specs=[HBM] * 9 +...  92.3 us

profile of v7, /device:TPU:0, one launch (start us, length us, event | category | flops | bytes accessed | tf_op | source)
XLA Modules:
  0.0 546.4 jit_solution(11539615105340966822)
XLA Ops:
  0.7 0.7 convert_element_type.11
  1.3 0.8 multiply_sine_fusion
  2.2 93.0 %enter.1 = (bf16[1024,2048]{1,0:T(8,128)(2,1)}, bf16[4,256,2048]{2,1,0:T(8,128)(2,1)}, bf16[8,256,1536]{2,1,0:T(8,128)(2,1)}, bf16[8,256,512]{2,1,0:T(8,128)(2,1...) custom-call(bf16[256,2048]{1,0:T(8,128)(2,1)} %refs_6_.3, bf16[256,2048]{1,0:T(8,128)(2,1)} %refs_1_.2, ...), custom_call_target="tpu_custom_call" | custom-call | flops 6442450944 | bytes 41943040 | tf_op jit(solution)/shard_map/enter/pallas_call | solution.py:535
  95.2 177.7 %middle.1 = (bf16[512,1024]{1,0:T(8,128)(2,1)}, bf16[512,1024]{1,0:T(8,128)(2,1)}, bf16[512,1024]{1,0:T(8,128)(2,1)}, f32[8,1024]{1,0:T(8,128)}, bf16[1024,512]{...) custom-call(f32[1536,1024]{1,0:T(8,128)} %get-tuple-element.66.refs_, ...), custom_call_target="tpu_custom_call" | custom-call | flops 29527900160 | bytes 62914560 | tf_op jit(solution)/shard_map/middle/pallas_call | solution.py:929
  272.9 171.9 %back.1 = (f32[256,1408]{1,0:T(8,128)}, f32[256,1408]{1,0:T(8,128)}, f32[256,1408]{1,0:T(8,128)}, f32[256,2048]{1,0:T(8,128)}, bf16[4,256,2048]{2,1,0:T(8,128)(2...) custom-call(bf16[1024,1408]{1,0:T(8,128)(2,1)} %bitcast.22, bf16[1024,1408]{1,0:T(8,128)(2,1)} %bitcast.23, ...), custom_call_target="tpu_custom_call" | custom-call | flops 41339060224 | bytes 62914560 | tf_op jit(solution)/shard_map/back/pallas_call | solution.py:1299
  444.9 92.3 %leave.1 = (bf16[256,2048]{1,0:T(8,128)(2,1)}, f32[256,2048]{1,0:T(8,128)}, f32[256,512]{1,0:T(8,128)}, f32[256,512]{1,0:T(8,128)}, f32[256,512]{1,0:T(8,128)}, /*index=5*/f32[512,256]{1,0:T(8,128)}, f32[8,2048]{1,0:T(8,128)}) custom-call(bf16[1024,2048]{1,0:T(8,128)(2,1)} %get-tuple-element.65.refs_0_, bf16[1024,1536]{1,0:T(8,128)(2,1)} %get-tuple-element.81.refs_1_, ...), custom_call_target="tpu_custom_call" | custom-call | flops 15032385536 | bytes 41943040 | tf_op jit(solution)/shard_map/leave/pallas_call | solution.py:1564
  537.2 9.0 %finish.1 = (bf16[256,2048]{1,0:T(8,128)(2,1)}, f32[256,2048]{1,0:T(8,128)}, f32[1,64]{1,0:T(1,128)}, f32[1,64]{1,0:T(1,128)}, f32[256,512]{1,0:T(8,128)}, /*ind...) custom-call(bf16[256,2048]{1,0:T(8,128)(2,1)} %get-tuple-element.88., ...), custom_call_target="tpu_custom_call" | custom-call | tf_op jit(solution)/shard_map/finish/pallas_call | solution.py:1687
  (1 shorter events, 0.0 us)

commit v8 on v7

--- a/solution.py
+++ b/solution.py
@@ -876,8 +876,17 @@
                 use(after, 0, half)
                 use(before, half, half)
             elif step - 1 > n // 2:
-                use(place.owner(step - 1))
-                use(place.owner(1 - step))
+                one, other = place.owner(step - 1), place.owner(1 - step)
+                first_at, other_at = (pl.ds(pl.multiple_of(whose * size, size), size) for whose in (one, other))
+
+                @pl.loop(0, 4)
+                def _(block):
+                    both = dot(g[block, :, first_at], down[one], ((1,), (0,)))
+                    both = both + dot(g[block, :, other_at], down[other], ((1,), (0,)))
+                    grad[block] += both
+
+                output(one, 0, size)
+                output(other, 0, size)
         for lane in lanes[0] + lanes[1]:
             lane.finish()
         for step in range(n):
@@ -1344,7 +1353,7 @@
     layer_out, input_out, query_sum, key_sum, value_sum, out_sum, vec_out,
     wide, narrow, normed, dlin, qkv, turned, mixed, resid, datt, attended, x, first, near_send, near_recv, far_send, far_recv,
     ffn_own, ffn_recv, ffn_send, ffn_far, layer, acc, totals, wsum, osum, vecs, vec_recv,
-    send, recv, x_send, x_recv, v_send, v_recv, local,
+    send, recv, x_send, x_recv, v_send, v_recv, local, blocks,
 ):
     place = Place(n)
     t, me = place.t, place.me
@@ -1357,9 +1366,8 @@
         pltpu.make_async_copy(src, dst, local.at[i])
         for i, (src, dst) in enumerate(
             (
-                (normed_ref, normed),
-                (dlin_ref, dlin),
-                (resid_ref, resid),
+                (dlin_ref.at[:, pl.ds(0, part)], dlin.at[:, pl.ds(0, part)]),
+                (dlin_ref.at[:, pl.ds(part, part)], dlin.at[:, pl.ds(part, part)]),
                 (mixed_ref, mixed),
                 (qkv_ref, qkv),
                 (ffn_ref.at[place.chip], ffn_own.at[0]),
@@ -1370,11 +1378,8 @@
             )
         )
     ]
-    for load in loads[:2]:
-        load.start()
     hops = [1, 2, 4]
     partners = [me + hop - 2 * hop * lax.rem(lax.div(me, hop), 2) for hop in hops]
-    place.barrier([place.up, place.down] + partners, [place.core, place.chip])
 
     lanes = [
         [Sum(place, wide.at[2 * i + way], way, send.at[2 * i + way], recv.at[2 * i + way]) for way in range(2)] for i in range(2)
@@ -1386,7 +1391,30 @@
     outs = [swap.copy(3 + i, ffn_ref.at[block], ffn_recv.at[i], place.core) for i, block in enumerate((place.cross, place.core))]
     outs_far = swap.copy(5, ffn_send, ffn_far, place.chip)
 
+    def block_of(step, way, i):
+        lane = lanes[0][way]
+        at = pl.ds(pl.multiple_of(lane.whose(step) * size + way * (size // 2), size // 2), size // 2)
+        src, dst = ((normed_ref, normed), (resid_ref, resid))[i]
+        return pltpu.make_async_copy(src.at[:, at], dst.at[:, at], blocks.at[i, way, step])
+
+    def fetch(steps, i):
+        for step in steps:
+            for way in range(2):
+                block_of(step, way, i).start()
+
+    fetch(range(1), 0)
+    loads[0].start()
+    loads[1].start()
+    fetch(range(1), 1)
+    loads[2].start()
+    fetch(range(1, 3), 0)
+    fetch(range(1, 3), 1)
+    place.barrier([place.up, place.down] + partners, [place.core, place.chip])
+
     def tick(step, i):
+        if i != 1:
+            for way in range(2):
+                block_of(step, way, i // 2).wait()
         for lane in lanes[i]:
             half = slice(lane.way * size // 2, (lane.way + 1) * size // 2)
             if i == 2:
@@ -1415,16 +1443,17 @@
             tick(*next(plan))
 
     loads[0].wait()
+    advance()
     loads[1].wait()
-    for load in loads[2:5]:
+    loads[3].start()
+    advance()
+    for load in loads[4:]:
         load.start()
-    advance(2)
-    for load in loads[5:]:
-        load.start()
+    fetch(range(3, n), 0)
+    fetch(range(3, n), 1)
     loads[2].wait()
+    advance()
     loads[3].wait()
-    advance()
-    loads[4].wait()
 
     def lines(block):
         return dlin[pl.ds(pl.multiple_of(block * rows, rows), rows), :]
@@ -1462,7 +1491,7 @@
         copy.start()
     advance()
     outs[0].wait_recv()
-    loads[5].wait()
+    loads[4].wait()
     for j in range(0, rows, 64):
         tile = slice(j, j + 64)
         ffn_send[tile, :] = (ffn_own[0, tile, :].astype(f32) + ffn_recv[0, tile, :].astype(f32)).astype(bf16)
@@ -1471,8 +1500,8 @@
     count = small.shape[2]
     gain = lane_vector(small, 0, size // count)
     acc[...] = jnp.zeros_like(acc)
+    loads[7].wait()
     loads[8].wait()
-    loads[9].wait()
     advance(4)
     far.wait_recv()
 
@@ -1522,8 +1551,8 @@
     advance(2)
     outs[1].wait_recv()
     outs_far.wait_recv()
+    loads[5].wait()
     loads[6].wait()
-    loads[7].wait()
     for j in range(0, rows, 64):
         tile = slice(j, j + 64)
         layer[tile, :] = (
@@ -1603,6 +1632,7 @@
             DMA((5,)),
             DMA((5,)),
             DMA((16,)),
+            DMA((2, 2, n)),
         ],
         compiler_params=pltpu.CompilerParams(collective_id=4, has_side_effects=True, vmem_limit_bytes=62 << 20),
         cost_estimate=pl.CostEstimate(flops=14 * seq * model * width, bytes_accessed=40 << 20, transcendentals=0),

time: 555 us -> 552 us (level)
  no operation moved by 1% of the time
where the time goes in v8:
time: 552 us; the launch traced here: 544 us
  Pallas kernels  541 us (98%)
    pallas_call x1, Pallas kernels, middle(): pl.pallas_call(lambda *refs: middle_kernel(n, *refs), in_specs=[HBM] + [V...  178 us
    pallas_call x1, Pallas kernels, back(): pl.pallas_call(lambda *refs: back_kernel(n, *refs), in_specs=[HBM] * 8 +...  172 us
    pallas_call x1, Pallas kernels, enter(): pl.pallas_call(kernel, in_specs=[HBM] * 5 + [VMEM] * 7, out_specs=[HBM, H...  93 us
    pallas_call x1, Pallas kernels, leave(): pl.pallas_call(lambda *refs: leave_kernel(n, *refs), in_specs=[HBM] * 9 +...  89.7 us

profile of v8, /device:TPU:0, one launch (start us, length us, event | category | flops | bytes accessed | tf_op | source)
XLA Modules:
  0.0 543.8 jit_solution(14294169414409856209)
XLA Ops:
  0.7 0.7 convert_element_type.11
  1.3 0.8 multiply_sine_fusion
  2.2 93.0 %enter.1 = (bf16[1024,2048]{1,0:T(8,128)(2,1)}, bf16[4,256,2048]{2,1,0:T(8,128)(2,1)}, bf16[8,256,1536]{2,1,0:T(8,128)(2,1)}, bf16[8,256,512]{2,1,0:T(8,128)(2,1...) custom-call(bf16[256,2048]{1,0:T(8,128)(2,1)} %refs_6_.3, bf16[256,2048]{1,0:T(8,128)(2,1)} %refs_1_.2, ...), custom_call_target="tpu_custom_call" | custom-call | flops 6442450944 | bytes 41943040 | tf_op jit(solution)/shard_map/enter/pallas_call | solution.py:535
  95.2 177.7 %middle.1 = (bf16[512,1024]{1,0:T(8,128)(2,1)}, bf16[512,1024]{1,0:T(8,128)(2,1)}, bf16[512,1024]{1,0:T(8,128)(2,1)}, f32[8,1024]{1,0:T(8,128)}, bf16[1024,512]{...) custom-call(f32[1536,1024]{1,0:T(8,128)} %get-tuple-element.66.refs_, ...), custom_call_target="tpu_custom_call" | custom-call | flops 29527900160 | bytes 62914560 | tf_op jit(solution)/shard_map/middle/pallas_call | solution.py:938
  272.9 171.9 %back.1 = (f32[256,1408]{1,0:T(8,128)}, f32[256,1408]{1,0:T(8,128)}, f32[256,1408]{1,0:T(8,128)}, f32[256,2048]{1,0:T(8,128)}, bf16[4,256,2048]{2,1,0:T(8,128)(2...) custom-call(bf16[1024,1408]{1,0:T(8,128)(2,1)} %bitcast.22, bf16[1024,1408]{1,0:T(8,128)(2,1)} %bitcast.23, ...), custom_call_target="tpu_custom_call" | custom-call | flops 41339060224 | bytes 62914560 | tf_op jit(solution)/shard_map/back/pallas_call | solution.py:1308
  444.9 89.7 %leave.1 = (bf16[256,2048]{1,0:T(8,128)(2,1)}, f32[256,2048]{1,0:T(8,128)}, f32[256,512]{1,0:T(8,128)}, f32[256,512]{1,0:T(8,128)}, f32[256,512]{1,0:T(8,128)}, /*index=5*/f32[512,256]{1,0:T(8,128)}, f32[8,2048]{1,0:T(8,128)}) custom-call(bf16[1024,2048]{1,0:T(8,128)(2,1)} %get-tuple-element.65.refs_0_, bf16[1024,1536]{1,0:T(8,128)(2,1)} %get-tuple-element.81.refs_1_, ...), custom_call_target="tpu_custom_call" | custom-call | flops 15032385536 | bytes 41943040 | tf_op jit(solution)/shard_map/leave/pallas_call | solution.py:1593
  534.6 9.0 %finish.1 = (bf16[256,2048]{1,0:T(8,128)(2,1)}, f32[256,2048]{1,0:T(8,128)}, f32[1,64]{1,0:T(1,128)}, f32[1,64]{1,0:T(1,128)}, f32[256,512]{1,0:T(8,128)}, /*ind...) custom-call(bf16[256,2048]{1,0:T(8,128)(2,1)} %get-tuple-element.88., ...), custom_call_target="tpu_custom_call" | custom-call | tf_op jit(solution)/shard_map/finish/pallas_call | solution.py:1717
  (1 shorter events, 0.0 us)

commit v9 on v8

--- a/solution.py
+++ b/solution.py
@@ -893,25 +893,32 @@
             for copy in write(step):
                 copy.wait()
         advance(2)
-        collect(before, 0, half)
-        collect(after, half, half)
-        final = []
-        for block in range(4):
-
-            @pl.loop(0, rows // 16)
-            def _(i):
-                here = pl.ds(pl.multiple_of(i * 16, 16), 16)
-                incoming = grad[block, here, :]
-                gate[block, here, :] = (incoming * up_lin[block, here, :]).astype(bf16)
-                gate[4 + block, here, :] = (incoming * gate_lin[block, here, :]).astype(bf16)
-
-            for first, out in ((0, dgate_out), (4, dup_out)):
-                final.append(pltpu.make_async_copy(gate.at[first + block], out.at[block], local.at[last + 5 + len(final)]))
-                final[-1].start()
+        low_at = pl.ds(pl.multiple_of(before * size, half), half)
+        high_at = pl.ds(pl.multiple_of(after * size + half, half), half)
+
+        def leaving(block):
+            return [
+                pltpu.make_async_copy(gate.at[first + block], out.at[block], local.at[last + 5 + i * 4 + block])
+                for i, (first, out) in enumerate(((0, dgate_out), (4, dup_out)))
+            ]
+
+        @pl.loop(0, 4)
+        def _(block):
+            for low in range(0, cols, 512):
+                tile = slice(low, min(low + 512, cols))
+                total = dot(g[block, :, low_at], down[before, 0:half, tile], ((1,), (0,)))
+                total = total + dot(g[block, :, high_at], down[after, half:, tile], ((1,), (0,)))
+                total = total + grad[block, :, tile]
+                gate[block, :, tile] = (total * up_lin[block, :, tile]).astype(bf16)
+                gate[4 + block, :, tile] = (total * gate_lin[block, :, tile]).astype(bf16)
+            for copy in leaving(block):
+                copy.start()
+
         output(before, 0, half)
         output(after, half, half)
         for lane in downs[0] + downs[1]:
             lane.finish()
+        final = [copy for block in range(4) for copy in leaving(block)]
         for copy in final + stages[-2:] + [hidden_store, second_store, att_store]:
             copy.wait()
 

time: 552 us -> 551 us (level)
  no operation moved by 1% of the time
where the time goes in v9:
time: 551 us; the launch traced here: 542 us
  Pallas kernels  540 us (98%)
    pallas_call x1, Pallas kernels, middle(): pl.pallas_call(lambda *refs: middle_kernel(n, *refs), in_specs=[HBM] + [V...  176 us
    pallas_call x1, Pallas kernels, back(): pl.pallas_call(lambda *refs: back_kernel(n, *refs), in_specs=[HBM] * 8 +...  172 us
    pallas_call x1, Pallas kernels, enter(): pl.pallas_call(kernel, in_specs=[HBM] * 5 + [VMEM] * 7, out_specs=[HBM, H...  93 us
    pallas_call x1, Pallas kernels, leave(): pl.pallas_call(lambda *refs: leave_kernel(n, *refs), in_specs=[HBM] * 9 +...  89.8 us

profile of v9, /device:TPU:0, one launch (start us, length us, event | category | flops | bytes accessed | tf_op | source)
XLA Modules:
  0.0 542.1 jit_solution(6564714392951684838)
XLA Ops:
  0.7 0.7 convert_element_type.11
  1.3 0.8 multiply_sine_fusion
  2.2 93.0 %enter.1 = (bf16[1024,2048]{1,0:T(8,128)(2,1)}, bf16[4,256,2048]{2,1,0:T(8,128)(2,1)}, bf16[8,256,1536]{2,1,0:T(8,128)(2,1)}, bf16[8,256,512]{2,1,0:T(8,128)(2,1...) custom-call(bf16[256,2048]{1,0:T(8,128)(2,1)} %refs_6_.3, bf16[256,2048]{1,0:T(8,128)(2,1)} %refs_1_.2, ...), custom_call_target="tpu_custom_call" | custom-call | flops 6442450944 | bytes 41943040 | tf_op jit(solution)/shard_map/enter/pallas_call | solution.py:535
  95.2 176.0 %middle.1 = (bf16[512,1024]{1,0:T(8,128)(2,1)}, bf16[512,1024]{1,0:T(8,128)(2,1)}, bf16[512,1024]{1,0:T(8,128)(2,1)}, f32[8,1024]{1,0:T(8,128)}, bf16[1024,512]{...) custom-call(f32[1536,1024]{1,0:T(8,128)} %get-tuple-element.66.refs_, ...), custom_call_target="tpu_custom_call" | custom-call | flops 29527900160 | bytes 62914560 | tf_op jit(solution)/shard_map/middle/pallas_call | solution.py:945
  271.2 171.9 %back.1 = (f32[256,1408]{1,0:T(8,128)}, f32[256,1408]{1,0:T(8,128)}, f32[256,1408]{1,0:T(8,128)}, f32[256,2048]{1,0:T(8,128)}, bf16[4,256,2048]{2,1,0:T(8,128)(2...) custom-call(bf16[1024,1408]{1,0:T(8,128)(2,1)} %bitcast.22, bf16[1024,1408]{1,0:T(8,128)(2,1)} %bitcast.23, ...), custom_call_target="tpu_custom_call" | custom-call | flops 41339060224 | bytes 62914560 | tf_op jit(solution)/shard_map/back/pallas_call | solution.py:1315
  443.1 89.8 %leave.1 = (bf16[256,2048]{1,0:T(8,128)(2,1)}, f32[256,2048]{1,0:T(8,128)}, f32[256,512]{1,0:T(8,128)}, f32[256,512]{1,0:T(8,128)}, f32[256,512]{1,0:T(8,128)}, /*index=5*/f32[512,256]{1,0:T(8,128)}, f32[8,2048]{1,0:T(8,128)}) custom-call(bf16[1024,2048]{1,0:T(8,128)(2,1)} %get-tuple-element.65.refs_0_, bf16[1024,1536]{1,0:T(8,128)(2,1)} %get-tuple-element.81.refs_1_, ...), custom_call_target="tpu_custom_call" | custom-call | flops 15032385536 | bytes 41943040 | tf_op jit(solution)/shard_map/leave/pallas_call | solution.py:1600
  532.9 9.0 %finish.1 = (bf16[256,2048]{1,0:T(8,128)(2,1)}, f32[256,2048]{1,0:T(8,128)}, f32[1,64]{1,0:T(1,128)}, f32[1,64]{1,0:T(1,128)}, f32[256,512]{1,0:T(8,128)}, /*ind...) custom-call(bf16[256,2048]{1,0:T(8,128)(2,1)} %get-tuple-element.88., ...), custom_call_target="tpu_custom_call" | custom-call | tf_op jit(solution)/shard_map/finish/pallas_call | solution.py:1724
  (1 shorter events, 0.0 us)
